TPU v7x, 32 devices: a whole 2x2x4 slice. The times are simulated.
32 devices in a mesh: mem: 4 (over y, x), reg: 8 (over z, core).
Axes of the slice: x: 2, y: 2, z: 4, core: 2. Of those that a mesh axis runs over, the one named last changes fastest.
Arguments:
- alpha: float32 [32, 16, 32, 128], P('mem', None, 'reg'), may hold values from -6 to 6
- perturbation: bfloat16 [32, 2, 16, 128, 512], P('mem', None, None, 'reg'), may hold values from -6 to 6
- obs_cell: int32 [8192], P('reg'), may hold values from 0 to 131071
- obs_kind: int32 [8192], P('reg'), may hold values from 0 to 3
- obs_value: float32 [8192], P('reg'), may hold values from -6 to 6
- obs_weight: float32 [8192], P('reg'), may hold values from 1 to 4
Outputs:
- obs_gradient: float32 [32, 16, 32, 128], P('mem', None, 'reg')
Inputs may be any that keep to these rules, and one draw needn't show every extreme that they name: `obs_cell`: each entry is level * 16 * 512 + row * 512 + column of a fine cell, the row counted from the first row of the observation's own region. `obs_kind`: 0 zonal wind, 1 meridional wind, 2 relative vorticity, 3 zonal wind advection.
All inputs are finite; a program needn't handle non-finite values.
Results may differ from a plain program's by a relative error of at most 0.0003.
Values sent between devices are 32-bit elements; how exact they have to be, the bound alone decides.
No kernel may reach another device: no remote copies, remote signals or barrier semaphores. Data moves between devices by JAX's collectives and lax.ppermute only.
A program may use at most 64 MiB of HBM per device.

v0:
```python
import math

import jax
import jax.numpy as jnp
from jax import lax
from jax.sharding import PartitionSpec as P

PASSES = 2


diffuse = 0.2
highest = lax.Precision.HIGHEST


def padded_2(value, sides, width):
    for axis, dim in sides:
        devices, length = (lax.axis_size(axis), value.shape[dim])
        up = [(i, (i + 1) % devices) for i in range(devices - 1)]
        down = [(j, i) for i, j in up]
        last = lax.slice_in_dim(value, length - width, length, axis=dim)
        first = lax.slice_in_dim(value, 0, width, axis=dim)
        before = lax.ppermute(last, axis, up)
        after = lax.ppermute(first, axis, down)
        value = jnp.concatenate([before, value, after], axis=dim)
    return value


def from_behind(value, axis, by):
    devices = lax.axis_size(axis)
    pairs = [(i, i + by) for i in range(devices) if 0 <= i + by < devices]
    return lax.ppermute(value, axis, pairs)


def weights(fine_rows, fine_start, coarse_count, coarse_start):
    finer = (jnp.arange(fine_rows) + fine_start).astype(jnp.float32)
    coarser = (jnp.arange(coarse_count) + coarse_start).astype(jnp.float32)
    where_at = (finer[:, None] + 0.5) / 4.0 - 0.5
    return jnp.maximum(0.0, 1.0 - jnp.abs(where_at - coarser[None, :]))


def one_pass(block):
    padded = jnp.pad(block, ((0, 0), (0, 0), (1, 1), (1, 1)))
    beside_all = (
        padded[:, :, 2:, 1:-1]
        + padded[:, :, :-2, 1:-1]
        + padded[:, :, 1:-1, 2:]
        + padded[:, :, 1:-1, :-2]
    )
    return block + diffuse * (beside_all - 4.0 * block)


def slopes(padded):
    along_x = (padded[..., 2:, 1:-1] - padded[..., :-2, 1:-1]) * 0.5
    along_y = (padded[..., 1:-1, 2:] - padded[..., 1:-1, :-2]) * 0.5
    return (along_x, along_y)


def mask_rows(block, first_row, total_rows):
    rows_here = first_row + jnp.arange(block.shape[2])
    keeping = (rows_here >= 0) & (rows_here < total_rows)
    return jnp.where(keeping[None, None, :, None], block, 0.0)


def smooth_rows(block, passes, keep):
    region = lax.axis_index("reg")
    total_rows = block.shape[2] * lax.axis_size("reg")
    extended = padded_2(block, (("reg", 2),), passes + keep)
    first_row = region * block.shape[2] - passes - keep
    for step in range(passes):
        extended = one_pass(extended)[:, :, 1:-1, :]
        first_row = first_row + 1
        extended = mask_rows(extended, first_row, total_rows)
    return extended


def observe(extended, level_first, obs_cell, obs_kind, obs_value, obs_weight, back_rim):
    levels = extended.shape[1]
    rows = extended.shape[2] - 2
    fine_cols = extended.shape[3] - 2
    zonal_x, zonal_y = slopes(extended[0])
    merid_x, _ = slopes(extended[1])
    zonal = extended[0, :, 1:-1, 1:-1]
    merid = extended[1, :, 1:-1, 1:-1]
    fields = jnp.stack([zonal, merid, merid_x - zonal_y, zonal * zonal_x + merid * zonal_y])
    plane = rows * fine_cols
    level = obs_cell // plane
    rest = obs_cell % plane
    row_in = rest // fine_cols
    column = rest % fine_cols
    inside = (level >= level_first) & (level < level_first + levels)
    local_level = jnp.clip(level - level_first, 0, levels - 1)
    line_count = 4 * levels * rows
    line = obs_kind * (levels * rows) + local_level * rows + row_in
    line_hot = (line[:, None] == jnp.arange(line_count, dtype=jnp.int32)[None, :]).astype(
        jnp.float32
    )
    column_hot = (column[:, None] == jnp.arange(fine_cols, dtype=jnp.int32)[None, :]).astype(
        jnp.float32
    )
    table = fields.reshape(line_count, fine_cols)
    picked = jnp.dot(line_hot, table, precision=highest, preferred_element_type=jnp.float32)
    seen = jnp.sum(picked * column_hot, axis=1)
    misfit = jnp.where(inside, obs_weight * (seen - obs_value), 0.0)
    weighted = misfit[:, None] * column_hot
    adjoint = lax.dot_general(
        line_hot,
        weighted,
        (((0,), (0,)), ((), ())),
        precision=highest,
        preferred_element_type=jnp.float32,
    )
    adjoint = adjoint.reshape(4, levels, rows, fine_cols)
    back = back_rim(jnp.stack([adjoint[2], adjoint[3] * zonal, adjoint[3] * merid]))
    vort_x, vort_y = slopes(back[0])
    flux_x, _ = slopes(back[1])
    _, flux_y = slopes(back[2])
    grad_u = adjoint[0] + adjoint[3] * zonal_x + vort_y - flux_x - flux_y
    grad_v = adjoint[1] + adjoint[3] * zonal_y - vort_x
    return jnp.stack([grad_u, grad_v])


def local(alpha, perturbation, obs_cell, obs_kind, obs_value, obs_weight):
    members, levels, coarse_rows, coarse_cols = alpha.shape
    fine_rows = perturbation.shape[3]
    region = lax.axis_index("reg")
    scale = 1.0 / math.sqrt(members * lax.axis_size("mem"))
    rows_x = weights(fine_rows, region * fine_rows, coarse_rows + 2, region * coarse_rows - 1)
    rows_y = weights(perturbation.shape[4], 0, coarse_cols, 0)
    smoothed = smooth_rows(alpha, PASSES, 1)
    part = jnp.einsum("ia,mlab->mlib", rows_x, smoothed, precision=highest)
    fine = jnp.einsum("mlib,jb->mlij", part, rows_y, precision=highest)
    partial_value = jnp.sum(fine[:, None] * perturbation.astype(jnp.float32), axis=0) * scale
    whole = lax.psum(partial_value, "mem")
    level_first = 0
    extended = jnp.pad(padded_2(whole, (("reg", 2),), 1), ((0, 0), (0, 0), (0, 0), (1, 1)))

    def back_rim(carried):
        rimmed_rows = padded_2(carried, (("reg", 2),), 1)
        return jnp.pad(rimmed_rows, ((0, 0), (0, 0), (0, 0), (1, 1)))

    grad_fine = observe(extended, level_first, obs_cell, obs_kind, obs_value, obs_weight, back_rim)
    product = jnp.sum(perturbation.astype(jnp.float32) * grad_fine[None], axis=1)
    projected_part = jnp.einsum("mlij,jb->mlib", product, rows_y, precision=highest)
    coarse = jnp.einsum("ia,mlib->mlab", rows_x, projected_part, precision=highest) * scale
    from_above = from_behind(coarse[:, :, 0], "reg", -1)
    from_below = from_behind(coarse[:, :, -1], "reg", 1)
    inner = coarse[:, :, 1:-1]
    inner = inner.at[:, :, -1].add(from_above)
    inner = inner.at[:, :, 0].add(from_below)
    return smooth_rows(inner, PASSES, 0)


def solution(mesh):
    return jax.shard_map(
        local,
        mesh=mesh,
        in_specs=(
            P("mem", None, "reg", None),
            P("mem", None, None, "reg", None),
            P("reg"),
            P("reg"),
            P("reg"),
            P("reg"),
        ),
        out_specs=P("mem", None, "reg", None),
        check_vma=False,
    )
```

profile of v0, /device:TPU:1, one launch (start us, length us, event | category | flops | bytes accessed | tf_op | source)
XLA Modules:
  0.0 147.5 jit_solution(11208299931560446973)
XLA Ops:
  6.5 1.2 fusion.90
  7.7 4.6 %collective-permute-start = (f32[8,16,3,128]{3,1,0,2:T(8,128)S(1)}, f32[8,16,3,128]{3,1,0,2:T(8,128)S(1)}, u32[]{:S(2)}, u32[]{:S(2)}) collective-permute-start(f32[8,16,3,128]{3,1,0,2:T(8,128)S(1)} %copy.30), channel_id=1, source_target_pairs={{0,1},{1,2},{2,3},{3,4},{4,5},{5,6},{6,7},{8,9},{9,10},{10,11},{11... | collective-permute-start | bytes 589832 | tf_op jit(solution)/shard_map/ppermute | solution.py:22
  12.4 1.9 %collective-permute-start.1 = (f32[8,16,3,128]{3,1,0,2:T(8,128)S(1)}, f32[8,16,3,128]{3,1,0,2:T(8,128)S(1)}, u32[]{:S(2)}, u32[]{:S(2)}) collective-permute-start(f32[8,16,3,128]{3,1,0,2:T(8,128)S(1)} %copy.31), channel_id=1, source_target_pairs={{1,0},{2,1},{3,2},{4,3},{5,4},{6,5},{7,6},{9,8},{10,9},{11,10},{12... | collective-permute-start | bytes 589832 | tf_op jit(solution)/shard_map/ppermute | solution.py:23
  14.4 0.6 collective-permute-done
  15.0 4.4 %collective-permute-done.1 = f32[8,16,3,128]{3,1,0,2:T(8,128)S(1)} collective-permute-done((f32[8,16,3,128]{3,1,0,2:T(8,128)S(1)}, f32[8,16,3,128]{3,1,0,2:T(8,128)S(1)}, u32[]{:S(2)}, u32[]{:S(2)}) %collective-permute-start.1) | collective-permute-done | bytes 196640 | tf_op jit(solution)/shard_map/ppermute | solution.py:23
  19.4 0.4 pad_slice_fusion.3
  19.8 0.2 fusion.31
  20.0 0.4 pad_slice_fusion.11
  20.4 0.2 fusion.42
  20.6 1.2 convolution_bitcast_fusion
  21.8 3.5 %fusion.49 = f32[8,16,16,512]{3,2,1,0:T(8,128)S(1)} fusion(f32[8,16,16,128]{3,2,1,0:T(8,128)S(1)} %convolution_bitcast_fusion, f32[128]{0:T(128)S(1)} %iota_convert_fusion, f32[512]{0:T(512)S(1)} %multiply_add_fusion), kind=kOutput, calls=%fused_computation.114 | convolution fusion | flops 1610874880 | bytes 5245440 | tf_op jit(solution)/shard_map/mlib,jb->mlij/dot_general | solution.py:131
  25.3 1.1 fusion
  26.5 1.1 broadcast_multiply_fusion
  27.6 52.2 %all-reduce.8.cloned.1.call-done = f32[2,16,16,512]{3,2,1,0:T(8,128)} async-done(((f32[2,16,16,512]{3,2,1,0:T(8,128)}), f32[2,16,16,512]{3,2,1,0:T(8,128)}) %all-reduce.8.cloned.1.call-update) | async-done | bytes 1048592 | tf_op jit(solution)/shard_map/psum | solution.py:133
  79.8 1.3 fusion.87
  81.1 3.8 %collective-permute-start.2 = (f32[2,16,1,512]{3,2,1,0:T(1,128)S(1)}, f32[2,16,1,512]{3,2,1,0:T(1,128)S(1)}, u32[]{:S(2)}, u32[]{:S(2)}) collective-permute-start(f32[2,16,1,512]{3,2,1,0:T(1,128)S(1)} %get-tuple-element.44), channel_id=1, source_target_pairs={{0,1},{1,2},{2,3},{3,4},{4,5},{5,6},{6,7},{8,9},{9,10},{10,11},{11... | collective-permute-start | bytes 196616 | tf_op jit(solution)/shard_map/ppermute | solution.py:22
  85.0 2.1 %collective-permute-start.3 = (f32[2,16,1,512]{3,2,1,0:T(1,128)S(1)}, f32[2,16,1,512]{3,2,1,0:T(1,128)S(1)}, u32[]{:S(2)}, u32[]{:S(2)}) collective-permute-start(f32[2,16,1,512]{3,2,1,0:T(1,128)S(1)} %get-tuple-element.45), channel_id=1, source_target_pairs={{1,0},{2,1},{3,2},{4,3},{5,4},{6,5},{7,6},{9,8},{10,9},{11,10},{12... | collective-permute-start | bytes 196616 | tf_op jit(solution)/shard_map/ppermute | solution.py:23
  87.2 3.4 %collective-permute-done.3 = f32[2,16,1,512]{3,2,1,0:T(1,128)S(1)} collective-permute-done((f32[2,16,1,512]{3,2,1,0:T(1,128)S(1)}, f32[2,16,1,512]{3,2,1,0:T(1,128)S(1)}, u32[]{:S(2)}, u32[]{:S(2)}) %collective-permute-start.3) | collective-permute-done | bytes 65568 | tf_op jit(solution)/shard_map/ppermute | solution.py:23
  90.6 2.3 %select_maximum_fusion.4 = f32[2,16,18,514]{3,2,1,0:T(8,128)S(1)} fusion(f32[2,16,1,512]{3,2,1,0:T(1,128)S(1)} %collective-permute-done.3, f32[2,16,16,512]{3,2,1,0:T(8,128)} %all-reduce.8.cloned.1.call-done, f32[2,16,1,512]{3,2,1,0:T(1,128)S(1)} %collective-permute-done.2), kind=kLoop, calls=%fused_computation.34 | loop fusion | flops 2368512 | bytes 2363904 | tf_op jit(solution)/shard_map/concatenate | solution.py:24
  93.0 1.1 copy-done
  94.1 0.8 fusion.27
  94.9 0.2 pad_maximum_fusion
  95.2 3.7 %select_reduce_fusion = f32[1024]{0:T(1024)S(1)} fusion(f32[1024,512]{1,0:T(8,128)S(1)} %bitcast.71, s32[1024]{0:T(1024)S(1)} %get-tuple-element.72, s32[1024]{0:T(1024)S(1)} %get-tuple-element.71), kind=kOutput, calls=%fused_computation.30 | convolution fusion | flops 6445071360 | bytes 2109440 | tf_op jit(solution)/shard_map/dot_general | solution.py:101
  98.8 4.2 %fusion.2 = f32[1024,512]{1,0:T(8,128)S(1)} fusion(s32[1024]{0:T(1024)S(1)} %get-tuple-element.72, f32[1024]{0:T(1024)S(1)} %multiply_select_fusion, s32[1024]{0:T(1024)S(1)} %get-tuple-element.71), kind=kOutput, calls=%fused_computation.7 | convolution fusion | flops 6444548096 | bytes 2109440 | tf_op jit(solution)/shard_map/dot_general | solution.py:105
  103.0 0.2 fusion.86
  103.3 0.2 slice_multiply_fusion.1
  103.5 0.2 pad_maximum_fusion.5
  103.7 1.9 %collective-permute-start.4 = (f32[3,16,1,512]{3,2,1,0:T(1,128)S(1)}, f32[3,16,1,512]{3,2,1,0:T(1,128)S(1)}, u32[]{:S(2)}, u32[]{:S(2)}) collective-permute-start(f32[3,16,1,512]{3,2,1,0:T(1,128)S(1)} %get-tuple-element.40), channel_id=1, source_target_pairs={{0,1},{1,2},{2,3},{3,4},{4,5},{5,6},{6,7},{8,9},{9,10},{10,11},{11... | collective-permute-start | bytes 294920 | tf_op jit(solution)/shard_map/ppermute | solution.py:22
  105.6 2.6 %collective-permute-start.5 = (f32[3,16,1,512]{3,2,1,0:T(1,128)S(1)}, f32[3,16,1,512]{3,2,1,0:T(1,128)S(1)}, u32[]{:S(2)}, u32[]{:S(2)}) collective-permute-start(f32[3,16,1,512]{3,2,1,0:T(1,128)S(1)} %get-tuple-element.41), channel_id=1, source_target_pairs={{1,0},{2,1},{3,2},{4,3},{5,4},{6,5},{7,6},{9,8},{10,9},{11,10},{12... | collective-permute-start | bytes 294920 | tf_op jit(solution)/shard_map/ppermute | solution.py:23
  108.2 3.3 %collective-permute-done.5 = f32[3,16,1,512]{3,2,1,0:T(1,128)S(1)} collective-permute-done((f32[3,16,1,512]{3,2,1,0:T(1,128)S(1)}, f32[3,16,1,512]{3,2,1,0:T(1,128)S(1)}, u32[]{:S(2)}, u32[]{:S(2)}) %collective-permute-start.5) | collective-permute-done | bytes 98336 | tf_op jit(solution)/shard_map/ppermute | solution.py:23
  111.5 1.6 %select_maximum_fusion = f32[3,16,18,514]{3,2,1,0:T(8,128)S(1)} fusion(f32[3,16,1,512]{3,2,1,0:T(1,128)S(1)} %collective-permute-done.5, f32[3,16,1,512]{3,2,1,0:T(1,128)S(1)} %collective-permute-done.4, f32[1,16,16,512]{3,2,1,0:T(8,128)S(1)} %get-tuple-element.43, f32[1,16,16,512]{3,2,1,0:T(8,128)S(1)} %get-tuple-element.42, f32[1,16,16,512]{3,2,1,0:T(8,128)S(1)} %bitcast.70), kind=kLoop, calls=%fused_computation.9 | loop fusion | flops 5329152 | bytes 3545856 | tf_op jit(solution)/shard_map/concatenate | solution.py:24
  113.1 0.2 slice_bitcast_fusion.1
  113.3 1.5 %fusion.18 = (f32[1,16,16,512]{3,2,1,0:T(8,128)S(1)}, f32[1,16,16,512]{3,2,1,0:T(8,128)S(1)}) fusion(f32[16,18,514]{2,1,0:T(8,128)S(1)} %get-tuple-element.31, f32[16,18,514]{2,1,0:T(8,128)S(1)} %get-tuple-element.29, f32[16,18,514]{2,1,0:T(8,128)S(1)} %get-tuple-element.30, f32[16,16,512]{2,1,0:T(8,128)S(1)} %bitcast.72, f32[16,16,512]{2,1,0:T(8,128)S(1)} %bitcast.68, ...), kind=kLoop, calls=%fused_computation.60 | loop fusion | flops 2621440 | bytes 8912896 | tf_op jit(solution)/shard_map/stack | solution.py:119
  114.9 0.6 copy-done.2
  115.5 1.2 fusion.1
  116.7 3.6 %fusion.47 = f32[8,16,16,128]{3,2,1,0:T(8,128)S(1)} fusion(f32[8,16,16,512]{3,2,1,0:T(8,128)S(1)} %fusion.1, f32[128]{0:T(128)S(1)} %iota_convert_fusion, f32[512]{0:T(512)S(1)} %multiply_add_fusion), kind=kOutput, calls=%fused_computation.112 | convolution fusion | flops 1610874880 | bytes 5245440 | tf_op jit(solution)/shard_map/mlij,jb->mlib/dot_general | solution.py:143
  120.3 0.7 fusion.9
  121.0 0.1 fusion.88
  121.2 1.9 %collective-permute-start.6 = (f32[8,16,128]{2,1,0:T(8,128)S(1)}, f32[8,16,128]{2,1,0:T(8,128)S(1)}, u32[]{:S(2)}, u32[]{:S(2)}) collective-permute-start(f32[8,16,128]{2,1,0:T(8,128)S(1)} %bitcast.76), channel_id=1, source_target_pairs={{1,0},{2,1},{3,2},{4,3},{5,4},{6,5},{7,6},{9,8},{10,9},{11,10},{12... | collective-permute-start | bytes 196616 | tf_op jit(solution)/shard_map/ppermute | solution.py:31
  123.2 3.6 %collective-permute-start.7 = (f32[8,16,128]{2,1,0:T(8,128)S(1)}, f32[8,16,128]{2,1,0:T(8,128)S(1)}, u32[]{:S(2)}, u32[]{:S(2)}) collective-permute-start(f32[8,16,128]{2,1,0:T(8,128)S(1)} %bitcast.75), channel_id=1, source_target_pairs={{0,1},{1,2},{2,3},{3,4},{4,5},{5,6},{6,7},{8,9},{9,10},{10,11},{11... | collective-permute-start | bytes 196616 | tf_op jit(solution)/shard_map/ppermute | solution.py:31
  126.9 1.3 collective-permute-done.7
  128.2 4.3 %collective-permute-start.8 = (f32[8,16,2,128]{3,1,0,2:T(8,128)S(1)}, f32[8,16,2,128]{3,1,0,2:T(8,128)S(1)}, u32[]{:S(2)}, u32[]{:S(2)}) collective-permute-start(f32[8,16,2,128]{3,1,0,2:T(8,128)S(1)} %get-tuple-element.67), channel_id=1, source_target_pairs={{0,1},{1,2},{2,3},{3,4},{4,5},{5,6},{6,7},{8,9},{9,10},{10,11},{11... | collective-permute-start | bytes 393224 | tf_op jit(solution)/shard_map/ppermute | solution.py:22
  132.5 1.9 %collective-permute-start.9 = (f32[8,16,2,128]{3,1,0,2:T(8,128)S(1)}, f32[8,16,2,128]{3,1,0,2:T(8,128)S(1)}, u32[]{:S(2)}, u32[]{:S(2)}) collective-permute-start(f32[8,16,2,128]{3,1,0,2:T(8,128)S(1)} %get-tuple-element.68), channel_id=1, source_target_pairs={{1,0},{2,1},{3,2},{4,3},{5,4},{6,5},{7,6},{9,8},{10,9},{11,10},{12... | collective-permute-start | bytes 393224 | tf_op jit(solution)/shard_map/ppermute | solution.py:23
  134.5 4.3 %collective-permute-done.9 = f32[8,16,2,128]{3,1,0,2:T(8,128)S(1)} collective-permute-done((f32[8,16,2,128]{3,1,0,2:T(8,128)S(1)}, f32[8,16,2,128]{3,1,0,2:T(8,128)S(1)}, u32[]{:S(2)}, u32[]{:S(2)}) %collective-permute-start.9) | collective-permute-done | bytes 131104 | tf_op jit(solution)/shard_map/ppermute | solution.py:23
  138.8 0.4 pad_slice_fusion.7
  139.2 0.2 fusion.38
  139.4 0.3 pad_slice_fusion.15
  139.8 0.9 copy.20
  (43 shorter events, 0.7 us)
Async XLA Ops:
  6.5 8.4 %copy-start.3 = (f32[8,16,4,128]{3,2,1,0:T(4,128)S(1)}, f32[8,16,4,128]{3,2,1,0:T(4,128)}, u32[]{:S(2)}) copy-start(f32[8,16,4,128]{3,2,1,0:T(4,128)} %param.10) | copy-start | bytes 786436
  6.5 73.3 %all-reduce.8.cloned.1.call-start = ((), (), s32[]{:S(2)}) async-start(), calls=%async_computation | async-start | bytes 2097152 | tf_op jit(solution)/shard_map/psum | solution.py:133
  7.7 7.2 %collective-permute-start = (f32[8,16,3,128]{3,1,0,2:T(8,128)S(1)}, f32[8,16,3,128]{3,1,0,2:T(8,128)S(1)}, u32[]{:S(2)}, u32[]{:S(2)}) collective-permute-start(f32[8,16,3,128]{3,1,0,2:T(8,128)S(1)} %copy.30), channel_id=1, source_target_pairs={{0,1},{1,2},{2,3},{3,4},{4,5},{5,6},{6,7},{8,9},{9,10},{10,11},{11... | collective-permute-start | bytes 589832 | tf_op jit(solution)/shard_map/ppermute | solution.py:22
  12.4 7.0 %collective-permute-start.1 = (f32[8,16,3,128]{3,1,0,2:T(8,128)S(1)}, f32[8,16,3,128]{3,1,0,2:T(8,128)S(1)}, u32[]{:S(2)}, u32[]{:S(2)}) collective-permute-start(f32[8,16,3,128]{3,1,0,2:T(8,128)S(1)} %copy.31), channel_id=1, source_target_pairs={{1,0},{2,1},{3,2},{4,3},{5,4},{6,5},{7,6},{9,8},{10,9},{11,10},{12... | collective-permute-start | bytes 589832 | tf_op jit(solution)/shard_map/ppermute | solution.py:23
  21.8 3.5 %copy-start.1 = (bf16[8,2,16,16,512]{4,3,2,1,0:T(8,128)(2,1)S(1)}, bf16[8,2,16,16,512]{4,3,2,1,0:T(8,128)(2,1)}, u32[]{:S(2)}) copy-start(bf16[8,2,16,16,512]{4,3,2,1,0:T(8,128)(2,1)} %param.11) | copy-start | bytes 12582916
  26.5 60.6 %copy-start.4 = (s32[1024]{0:T(1024)S(1)}, s32[1024]{0:T(1024)}, u32[]{:S(2)}) copy-start(s32[1024]{0:T(1024)} %param.12) | copy-start | bytes 12292
  26.5 60.6 %copy-start.7 = (s32[1024]{0:T(1024)S(1)}, s32[1024]{0:T(1024)}, u32[]{:S(2)}) copy-start(s32[1024]{0:T(1024)} %param.13) | copy-start | bytes 12292
  81.1 6.0 %collective-permute-start.2 = (f32[2,16,1,512]{3,2,1,0:T(1,128)S(1)}, f32[2,16,1,512]{3,2,1,0:T(1,128)S(1)}, u32[]{:S(2)}, u32[]{:S(2)}) collective-permute-start(f32[2,16,1,512]{3,2,1,0:T(1,128)S(1)} %get-tuple-element.44), channel_id=1, source_target_pairs={{0,1},{1,2},{2,3},{3,4},{4,5},{5,6},{6,7},{8,9},{9,10},{10,11},{11... | collective-permute-start | bytes 196616 | tf_op jit(solution)/shard_map/ppermute | solution.py:22
  85.0 5.6 %collective-permute-start.3 = (f32[2,16,1,512]{3,2,1,0:T(1,128)S(1)}, f32[2,16,1,512]{3,2,1,0:T(1,128)S(1)}, u32[]{:S(2)}, u32[]{:S(2)}) collective-permute-start(f32[2,16,1,512]{3,2,1,0:T(1,128)S(1)} %get-tuple-element.45), channel_id=1, source_target_pairs={{1,0},{2,1},{3,2},{4,3},{5,4},{6,5},{7,6},{9,8},{10,9},{11,10},{12... | collective-permute-start | bytes 196616 | tf_op jit(solution)/shard_map/ppermute | solution.py:23
  92.9 1.2 copy-start
  95.1 3.7 %copy-start.5 = (f32[1024]{0:T(1024)S(1)}, f32[1024]{0:T(1024)}, u32[]{:S(2)}) copy-start(f32[1024]{0:T(1024)} %param.15) | copy-start | bytes 12292
  95.1 3.7 %copy-start.6 = (f32[1024]{0:T(1024)S(1)}, f32[1024]{0:T(1024)}, u32[]{:S(2)}) copy-start(f32[1024]{0:T(1024)} %param.14) | copy-start | bytes 12292
  103.7 4.6 %collective-permute-start.4 = (f32[3,16,1,512]{3,2,1,0:T(1,128)S(1)}, f32[3,16,1,512]{3,2,1,0:T(1,128)S(1)}, u32[]{:S(2)}, u32[]{:S(2)}) collective-permute-start(f32[3,16,1,512]{3,2,1,0:T(1,128)S(1)} %get-tuple-element.40), channel_id=1, source_target_pairs={{0,1},{1,2},{2,3},{3,4},{4,5},{5,6},{6,7},{8,9},{9,10},{10,11},{11... | collective-permute-start | bytes 294920 | tf_op jit(solution)/shard_map/ppermute | solution.py:22
  105.6 5.9 %collective-permute-start.5 = (f32[3,16,1,512]{3,2,1,0:T(1,128)S(1)}, f32[3,16,1,512]{3,2,1,0:T(1,128)S(1)}, u32[]{:S(2)}, u32[]{:S(2)}) collective-permute-start(f32[3,16,1,512]{3,2,1,0:T(1,128)S(1)} %get-tuple-element.41), channel_id=1, source_target_pairs={{1,0},{2,1},{3,2},{4,3},{5,4},{6,5},{7,6},{9,8},{10,9},{11,10},{12... | collective-permute-start | bytes 294920 | tf_op jit(solution)/shard_map/ppermute | solution.py:23
  113.3 2.2 %copy-start.2 = (bf16[8,2,16,16,512]{4,3,2,1,0:T(8,128)(2,1)S(1)}, bf16[8,2,16,16,512]{4,3,2,1,0:T(8,128)(2,1)}, u32[]{:S(2)}) copy-start(bf16[8,2,16,16,512]{4,3,2,1,0:T(8,128)(2,1)} %param.11) | copy-start | bytes 12582916
  121.2 5.7 %collective-permute-start.6 = (f32[8,16,128]{2,1,0:T(8,128)S(1)}, f32[8,16,128]{2,1,0:T(8,128)S(1)}, u32[]{:S(2)}, u32[]{:S(2)}) collective-permute-start(f32[8,16,128]{2,1,0:T(8,128)S(1)} %bitcast.76), channel_id=1, source_target_pairs={{1,0},{2,1},{3,2},{4,3},{5,4},{6,5},{7,6},{9,8},{10,9},{11,10},{12... | collective-permute-start | bytes 196616 | tf_op jit(solution)/shard_map/ppermute | solution.py:31
  123.2 5.0 %collective-permute-start.7 = (f32[8,16,128]{2,1,0:T(8,128)S(1)}, f32[8,16,128]{2,1,0:T(8,128)S(1)}, u32[]{:S(2)}, u32[]{:S(2)}) collective-permute-start(f32[8,16,128]{2,1,0:T(8,128)S(1)} %bitcast.75), channel_id=1, source_target_pairs={{0,1},{1,2},{2,3},{3,4},{4,5},{5,6},{6,7},{8,9},{9,10},{10,11},{11... | collective-permute-start | bytes 196616 | tf_op jit(solution)/shard_map/ppermute | solution.py:31
  128.2 6.2 %collective-permute-start.8 = (f32[8,16,2,128]{3,1,0,2:T(8,128)S(1)}, f32[8,16,2,128]{3,1,0,2:T(8,128)S(1)}, u32[]{:S(2)}, u32[]{:S(2)}) collective-permute-start(f32[8,16,2,128]{3,1,0,2:T(8,128)S(1)} %get-tuple-element.67), channel_id=1, source_target_pairs={{0,1},{1,2},{2,3},{3,4},{4,5},{5,6},{6,7},{8,9},{9,10},{10,11},{11... | collective-permute-start | bytes 393224 | tf_op jit(solution)/shard_map/ppermute | solution.py:22
  132.5 6.3 %collective-permute-start.9 = (f32[8,16,2,128]{3,1,0,2:T(8,128)S(1)}, f32[8,16,2,128]{3,1,0,2:T(8,128)S(1)}, u32[]{:S(2)}, u32[]{:S(2)}) collective-permute-start(f32[8,16,2,128]{3,1,0,2:T(8,128)S(1)} %get-tuple-element.68), channel_id=1, source_target_pairs={{1,0},{2,1},{3,2},{4,3},{5,4},{6,5},{7,6},{9,8},{10,9},{11,10},{12... | collective-permute-start | bytes 393224 | tf_op jit(solution)/shard_map/ppermute | solution.py:23
Sparse Core Ops, SparseCore 0:
  27.8 52.0 all-reduce.7
where the time goes:
time: 148 us; the launch traced here: 147 us
  waiting for transfers between devices  69.5 us (47%)
  starting transfers between devices  28.7 us (19%)
  matrix products  16.9 us (11%)
  between operations  13.9 us (9%)
  other arithmetic  11.1 us (8%)
  local copies, waits for them, and re-layouts  7.37 us (5%)
    psum x1, waiting for transfers between devices, local(): whole = lax.psum(partial_value, 'mem')  52.2 us
    ppermute x4, waiting for transfers between devices, padded_2(): after = lax.ppermute(first, axis, down)  15.4 us
    ppermute x4, starting transfers between devices, padded_2(): before = lax.ppermute(last, axis, up)  14.6 us
    ppermute x4, starting transfers between devices, padded_2(): after = lax.ppermute(first, axis, down)  8.57 us
    ppermute x2, starting transfers between devices, from_behind(): return lax.ppermute(value, axis, pairs)  5.56 us
    dot_general x1, matrix products, observe(): lax.dot_general(line_hot, weighted, (((0,), (0,)), ((), ())), precision=h...  4.19 us
    concatenate x3, other arithmetic, padded_2(): value = jnp.concatenate([before, value, after], axis=dim)  3.91 us
    dot_general x1, matrix products, observe(): jnp.dot(line_hot, table, precision=highest, preferred_element_type=jnp.fl...  3.66 us
  transfers between devices with their start and end apart: 11, of which 7 were waited for; matrix products, arithmetic and copies ran while one was open for 0% of the time, Pallas kernels for 0%

commit v1 on v0

v1 whole, which is shorter than its diff:
```python
import functools
import math

import jax
import jax.numpy as jnp
from jax import lax
from jax.experimental import pallas as pl
from jax.experimental.pallas import tpu as pltpu
from jax.sharding import PartitionSpec as P

PASSES = 2
HALO = PASSES + 1
DIFFUSE = 0.2
F32 = jnp.float32
BF16 = jnp.bfloat16


def params(mib):
    return pltpu.CompilerParams(vmem_limit_bytes=mib << 20)


def swap_pairs(n, odd):
    pairs = []
    for i in range(1 if odd else 0, n - 1, 2):
        pairs += [(i, i + 1), (i + 1, i)]
    return pairs


def swap_even(value):
    return lax.ppermute(value, "reg", swap_pairs(lax.axis_size("reg"), False))


def swap_odd(value):
    return lax.ppermute(value, "reg", swap_pairs(lax.axis_size("reg"), True))


def others(value, axis):
    n = lax.axis_size(axis)
    stride = 1
    rounds = []
    while stride < n:
        left = n // stride
        radix = 4 if left % 4 == 0 else 2 if left % 2 == 0 else left
        sends = []
        for k in range(1, radix):
            pairs = []
            for i in range(n):
                digit = (i // stride) % radix
                other = digit ^ k if radix in (2, 4) else (digit + k) % radix
                pairs.append((i, i + (other - digit) * stride))
            sends.append(pairs)
        rounds.append(sends)
        stride *= radix
    for number, sends in enumerate(rounds):
        got = [lax.ppermute(value, axis, pairs) for pairs in sends]
        if number == len(rounds) - 1:
            return [value] + got
        for part in got:
            value = value + part
    return [value]


def split(x):
    high = x.astype(BF16)
    return high, (x - high.astype(F32)).astype(BF16)


def dot_nn(a, b):
    return lax.dot_general(a, b, (((1,), (0,)), ((), ())), preferred_element_type=F32)


def dot_nt(a, b):
    return lax.dot_general(a, b, (((1,), (1,)), ((), ())), preferred_element_type=F32)


def iota(shape, dim):
    return lax.broadcasted_iota(jnp.int32, shape, dim)


def table_y(coarse, fine, coarse_dim):
    shape = (coarse, fine) if coarse_dim == 0 else (fine, coarse)
    ratio = fine // coarse
    at = (iota(shape, 1 - coarse_dim).astype(F32) + 0.5) / ratio - 0.5
    return jnp.maximum(0.0, 1.0 - jnp.abs(at - iota(shape, coarse_dim).astype(F32))).astype(BF16)


def weights_x(i, ratio):
    at = (i + 0.5) / ratio - 0.5
    low = math.floor(at)
    return low, 1.0 - (at - low), at - low


def one_pass(rows, index, columns):
    mid = rows.get(index)
    around = None
    if mid is not None:
        lane = iota(mid.shape, 1)
        left = jnp.where(lane == 0, 0.0, pltpu.roll(mid, 1, 1))
        right = jnp.where(lane == columns - 1, 0.0, pltpu.roll(mid, columns - 1, 1))
        around = left + right
    for near in (index + 1, index - 1):
        if near in rows:
            around = rows[near] if around is None else around + rows[near]
    if mid is None:
        return DIFFUSE * around
    return mid + DIFFUSE * (around - 4.0 * mid)


def mask_row(value, index, coarse_rows, region, regions):
    if index < 0:
        return jnp.where(region * coarse_rows + index >= 0, value, 0.0)
    if index >= coarse_rows:
        return jnp.where(region * coarse_rows + index < regions * coarse_rows, value, 0.0)
    return value


def pack_kernel(pert_ref, a_ref, b_ref):
    even = lax.rem(lax.axis_index("reg"), 2) == 0
    block = pert_ref[0].astype(F32)
    first = block[:, :, 0, :]
    last = block[:, :, block.shape[2] - 1, :]
    a_ref[0] = jnp.where(even, last, first)
    b_ref[0] = jnp.where(even, first, last)


def pack(pert):
    members, parts, levels, rows, columns = pert.shape
    out = jax.ShapeDtypeStruct((members, parts, levels, columns), F32)
    spec = pl.BlockSpec((1, parts, levels, columns), lambda m: (m, 0, 0, 0))
    return pl.pallas_call(
        pack_kernel,
        grid=(members,),
        in_specs=[pl.BlockSpec((1, parts, levels, rows, columns), lambda m: (m, 0, 0, 0, 0))],
        out_specs=[spec, spec],
        out_shape=[out, out],
        compiler_params=params(16),
        name="pack_rows",
    )(pert)


def decode(cell, rows, columns):
    plane = rows * columns
    level = cell // plane
    rest = cell - level * plane
    row = rest // columns
    return level, row, rest - row * columns


def tables_kernel(levels, rows, columns, cell_ref, kind_ref, r0_ref, ru_ref, rv_ref, c0_ref, cy_ref):
    cell, kind = cell_ref[...], kind_ref[...]
    level, row, column = decode(cell, rows, columns)
    line = level * rows + row
    count = cell.shape[1]
    inner = levels * rows
    above = jnp.where(row > 0, line - 1, -1)
    below = jnp.where(row < rows - 1, line + 1, -1)
    up_edge = jnp.where(row == 0, inner + level, -1)
    down_edge = jnp.where(row == rows - 1, inner + levels + level, -1)
    minus = jnp.where(row > 0, above, up_edge)
    plus = jnp.where(row < rows - 1, below, down_edge)
    none = jnp.full_like(line, -1)
    here_u = line
    minus_u = jnp.where(kind == 3, minus, none)
    plus_u = jnp.where(kind == 3, plus, none)
    here_v = jnp.where((kind == 1) | (kind == 3), line, none)
    minus_v = jnp.where(kind == 2, minus, none)
    plus_v = jnp.where(kind == 2, plus, none)
    step = 32

    def lines(k, _):
        start = pl.multiple_of(k * step, step)
        at = iota((step, count), 0) + start
        ru = jnp.where(at == plus_u, 0.5, jnp.where(at == minus_u, -0.5, 0.0))
        rv = jnp.where(at == plus_v, 0.5, jnp.where(at == minus_v, -0.5, jnp.where(at == here_v, 1.0, 0.0)))
        r0 = jnp.where(at == here_u, 1.0, 0.0)
        ru_ref[pl.ds(start, step), :] = ru.astype(BF16)
        rv_ref[pl.ds(start, step), :] = rv.astype(BF16)
        r0_ref[pl.ds(start, step), :] = r0.astype(BF16)
        return 0

    lax.fori_loop(0, (inner + 2 * levels) // step, lines, 0)

    def cells(k, _):
        start = pl.multiple_of(k * step, step)
        at = iota((step, count), 0) + start
        c0_ref[pl.ds(start, step), :] = jnp.where(at == column, 1.0, 0.0).astype(BF16)
        cy = jnp.where(at == column + 1, 0.5, jnp.where(at == column - 1, -0.5, 0.0))
        cy_ref[pl.ds(start, step), :] = cy.astype(BF16)
        return 0

    lax.fori_loop(0, columns // step, cells, 0)


def tables(cell, kind, levels, rows, columns):
    count = cell.shape[1]
    lines = levels * rows + 2 * levels
    shapes = [jax.ShapeDtypeStruct((n, count), BF16) for n in (lines, lines, lines, columns, columns)]
    return pl.pallas_call(
        functools.partial(tables_kernel, levels, rows, columns),
        out_shape=shapes,
        compiler_params=params(16),
        name="one_hots",
    )(cell, kind)


def forward_kernel(
    scale, members, levels, chunk, coarse_rows, rows,
    own_ref, even_ref, odd_ref, pert_ref, r0_ref, ru_ref, rv_ref, c0_ref, cy_ref,
    q_ref, edge_ref,
    fine_in, fine_scr, u_scr, v_scr, ty_scr, t_scr,
):
    step = pl.program_id(0)
    steps = pl.num_programs(0)
    region = lax.axis_index("reg")
    regions = lax.axis_size("reg")
    pairs = members * levels
    coarse_columns = own_ref.shape[1]
    columns = u_scr.shape[1]
    ratio = rows // coarse_rows
    block = chunk * rows

    @pl.when(step == 0)
    def _():
        even = lax.rem(region, 2) == 0
        table = table_y(coarse_columns, columns, 0)
        ty_scr[pl.ds(0, coarse_columns), :] = table
        ty_scr[pl.ds(coarse_columns, coarse_columns), :] = table
        rows_in = {}
        for r in range(coarse_rows):
            rows_in[r] = own_ref[pl.ds(r, pairs, stride=coarse_rows), :]
        for k in range(HALO):
            low = coarse_rows - HALO + k
            e = even_ref[pl.ds(low, pairs, stride=coarse_rows), :]
            o = odd_ref[pl.ds(low, pairs, stride=coarse_rows), :]
            rows_in[k - HALO] = jnp.where(even, o, e)
            e = even_ref[pl.ds(k, pairs, stride=coarse_rows), :]
            o = odd_ref[pl.ds(k, pairs, stride=coarse_rows), :]
            rows_in[coarse_rows + k] = jnp.where(even, e, o)
        for done in range(PASSES):
            reach = HALO - 1 - done
            rows_in = {
                r: mask_row(one_pass(rows_in, r, coarse_columns), r, coarse_rows, region, regions)
                for r in range(-reach, coarse_rows + reach)
            }
        for i in range(-1, rows + 1):
            low, w0, w1 = weights_x(i, ratio)
            value = (w0 * rows_in[low] + w1 * rows_in[low + 1]) * scale
            if 0 <= i < rows:
                fine_in[pl.ds(i, pairs, stride=rows), :] = value
            else:
                high, lower = split(value)
                got = dot_nn(jnp.concatenate([high, lower], axis=1), ty_scr[...])
                edge_ref[0 if i < 0 else 1] = got

    parts = []
    for m in range(members):
        start = pl.multiple_of(m * levels * rows + step * block, block)
        parts.append(fine_in[pl.ds(start, block), :])
    high, lower = split(jnp.concatenate(parts, axis=0))
    fine_scr[...] = dot_nn(jnp.concatenate([high, lower], axis=1), ty_scr[...])
    base = step * block

    def level(k, _):
        at = pl.multiple_of(k * rows, rows)
        u = v = None
        for m in range(members):
            fine = fine_scr[pl.ds(m * block + at, rows), :]
            pu = fine * pert_ref[m, 0, k].astype(F32)
            pv = fine * pert_ref[m, 1, k].astype(F32)
            u = pu if u is None else u + pu
            v = pv if v is None else v + pv
        to = pl.multiple_of(base + at, rows)
        u_scr[pl.ds(to, rows), :] = u
        v_scr[pl.ds(to, rows), :] = v
        return 0

    lax.fori_loop(0, chunk, level, 0)

    @pl.when(step == steps - 1)
    def _():
        inner = levels * rows
        for n, source in enumerate((u_scr, v_scr)):
            high, lower = split(source[...].T)
            t_scr[2 * n] = high
            t_scr[2 * n + 1] = lower
        count = r0_ref.shape[1]
        width = min(256, count)

        def observe(k, _):
            at = pl.ds(pl.multiple_of(k * width, width), width)
            c0 = c0_ref[:, at].astype(F32)
            cy = cy_ref[:, at].astype(F32)
            r0 = r0_ref[pl.ds(0, inner), at]
            u_row = dot_nn(t_scr[0], r0) + dot_nn(t_scr[1], r0)
            q_ref[pl.ds(0, 1), at] = jnp.sum(u_row * c0, axis=0, keepdims=True)
            q_ref[pl.ds(3, 1), at] = jnp.sum(u_row * cy, axis=0, keepdims=True)
            rv = rv_ref[pl.ds(0, inner), at]
            v_row = dot_nn(t_scr[2], rv) + dot_nn(t_scr[3], rv)
            q_ref[pl.ds(1, 1), at] = jnp.sum(v_row * c0, axis=0, keepdims=True)
            ru = ru_ref[pl.ds(0, inner), at]
            d_row = dot_nn(t_scr[0], ru) + dot_nn(t_scr[1], ru)
            q_ref[pl.ds(2, 1), at] = jnp.sum(d_row * c0, axis=0, keepdims=True)
            return 0

        lax.fori_loop(0, count // width, observe, 0)


def forward(own, got_even, got_odd, pert, hot, scale):
    members, parts, levels, rows, columns = pert.shape
    pairs = members * levels
    coarse_rows = own.shape[0] // pairs
    coarse_columns = own.shape[1]
    chunk = 4 if levels % 4 == 0 else 1
    count = hot[0].shape[1]
    whole = lambda x: pl.BlockSpec(x.shape, lambda s: (0,) * x.ndim)
    return pl.pallas_call(
        functools.partial(forward_kernel, scale, members, levels, chunk, coarse_rows, rows),
        grid=(levels // chunk,),
        in_specs=[whole(own), whole(own), whole(own),
                  pl.BlockSpec((members, parts, chunk, rows, columns), lambda s: (0, 0, s, 0, 0)),
                  *[whole(h) for h in hot]],
        out_specs=[pl.BlockSpec((4, count), lambda s: (0, 0)),
                   pl.BlockSpec((2, pairs, columns), lambda s: (0, 0, 0))],
        out_shape=[jax.ShapeDtypeStruct((4, count), F32),
                   jax.ShapeDtypeStruct((2, pairs, columns), F32)],
        scratch_shapes=[
            pltpu.VMEM((pairs * rows, coarse_columns), F32),
            pltpu.VMEM((members * chunk * rows, columns), F32),
            pltpu.VMEM((levels * rows, columns), F32),
            pltpu.VMEM((levels * rows, columns), F32),
            pltpu.VMEM((2 * coarse_columns, columns), BF16),
            pltpu.VMEM((4, columns, levels * rows), BF16),
        ],
        compiler_params=params(40),
        name="increment_at_obs",
    )(own, got_even, got_odd, pert, *hot)


def edge_kernel(members, levels, q_ref, fine_ref, even_ref, odd_ref, ru_ref, rv_ref, c0_ref, out_ref):
    even = lax.rem(lax.axis_index("reg"), 2) == 0
    columns = fine_ref.shape[2]
    table = []
    for part in range(2):
        for side in range(2):
            total = None
            for m in range(members):
                e, o = even_ref[m, part], odd_ref[m, part]
                halo = jnp.where(even, o, e) if side == 0 else jnp.where(even, e, o)
                term = fine_ref[side, pl.ds(m * levels, levels), :] * halo
                total = term if total is None else total + term
            table.append(total)
    u = jnp.concatenate(table[:2], axis=0).T
    v = jnp.concatenate(table[2:], axis=0).T
    u_high, u_low = split(u)
    v_high, v_low = split(v)
    left = jnp.concatenate([u_high, u_low, v_high, v_low], axis=1)
    ru, rv = ru_ref[...], rv_ref[...]
    count = ru.shape[1]
    width = min(256, count)
    for k in range(count // width):
        at = pl.ds(k * width, width)
        rc = ru_ref[:, at]
        vc = rv_ref[:, at]
        row = dot_nn(left, jnp.concatenate([rc, rc, vc, vc], axis=0))
        seen = jnp.sum(row * c0_ref[:, at].astype(F32), axis=0, keepdims=True)
        in_u = jnp.sum(jnp.abs(rc.astype(F32)), axis=0, keepdims=True) > 0.0
        in_v = jnp.sum(jnp.abs(vc.astype(F32)), axis=0, keepdims=True) > 0.0
        out_ref[pl.ds(0, 1), at] = q_ref[pl.ds(0, 1), at]
        out_ref[pl.ds(1, 1), at] = q_ref[pl.ds(1, 1), at] + jnp.where(in_v, seen, 0.0)
        out_ref[pl.ds(2, 1), at] = q_ref[pl.ds(2, 1), at] + jnp.where(in_u, seen, 0.0)
        out_ref[pl.ds(3, 1), at] = q_ref[pl.ds(3, 1), at]


def edge(q, fine, halo_even, halo_odd, hot, members, levels):
    _, ru, rv, c0, _ = hot
    lines, count = ru.shape
    tail = 2 * levels
    whole = lambda x: pl.BlockSpec(x.shape, lambda s: (0,) * x.ndim)
    last = pl.BlockSpec((tail, count), lambda s: (lines // tail - 1, 0))
    return pl.pallas_call(
        functools.partial(edge_kernel, members, levels),
        grid=(1,),
        in_specs=[whole(q), whole(fine), whole(halo_even), whole(halo_odd), last, last, whole(c0)],
        out_specs=whole(q),
        out_shape=jax.ShapeDtypeStruct(q.shape, F32),
        compiler_params=params(24),
        name="edge_at_obs",
    )(q, fine, halo_even, halo_odd, ru, rv, c0)


def backward_kernel(
    scale, members, levels, chunk, coarse_rows, rows, terms,
    *refs,
):
    q_refs = refs[:terms]
    (kind_ref, value_ref, weight_ref, pert_ref, even_ref, odd_ref,
     r0_ref, ru_ref, rv_ref, c0_ref, cy_ref,
     own_out, a_out, b_out,
     u_scr, v_scr, ty_scr, f_scr) = refs[terms:]
    step = pl.program_id(0)
    steps = pl.num_programs(0)
    region = lax.axis_index("reg")
    regions = lax.axis_size("reg")
    pairs = members * levels
    columns, coarse_columns = ty_scr.shape
    ratio = rows // coarse_rows
    block = chunk * rows
    inner = levels * rows
    even = lax.rem(region, 2) == 0

    @pl.when(step == 0)
    def _():
        ty_scr[...] = table_y(coarse_columns, columns, 1)
        q = q_refs[0][...]
        for ref in q_refs[1:]:
            q = q + ref[...]
        q0, q1, q2, q3 = (q[n : n + 1] for n in range(4))
        kind = kind_ref[...]
        seen = jnp.where(kind == 0, q0, jnp.where(kind == 1, q1, jnp.where(kind == 2, q1 - q3, q0 * q2 + q1 * q3)))
        misfit = weight_ref[...] * (seen - value_ref[...])
        zero = jnp.zeros_like(misfit)
        a = jnp.where(kind == 0, misfit, jnp.where(kind == 3, misfit * q2, zero))
        b = jnp.where(kind == 2, -misfit, jnp.where(kind == 3, misfit * q1, zero))
        c = jnp.where(kind == 3, misfit * q0, zero)
        g = jnp.where(kind == 3, misfit * q3, jnp.where(kind == 0, zero, misfit))
        c0, cy = c0_ref[...], cy_ref[...]
        r0, ru, rv = r0_ref[pl.ds(0, inner), :], ru_ref[...], rv_ref[...]
        total_u = total_c = total_v = None
        for a_part, b_part, c_part, g_part in zip(split(a), split(b), split(c), split(g)):
            t = dot_nt(r0, c0 * a_part + cy * b_part)
            total_u = t if total_u is None else total_u + t
            t = dot_nt(ru, c0 * c_part)
            total_c = t if total_c is None else total_c + t
            t = dot_nt(rv, c0 * g_part)
            total_v = t if total_v is None else total_v + t
        u_scr[pl.ds(0, inner), :] = total_u + total_c[:inner]
        u_scr[pl.ds(inner, 2 * levels), :] = total_c[inner:]
        v_scr[...] = total_v

    def level(k, _):
        at = pl.multiple_of(k * rows, rows)
        here = pl.multiple_of(step * block + at, rows)
        u = u_scr[pl.ds(here, rows), :]
        v = v_scr[pl.ds(here, rows), :]
        product = [u * pert_ref[m, 0, k].astype(F32) + v * pert_ref[m, 1, k].astype(F32) for m in range(members)]
        high, lower = split(jnp.concatenate(product, axis=0))
        got = dot_nn(high, ty_scr[...]) + dot_nn(lower, ty_scr[...])
        for m in range(members):
            to = pl.multiple_of(m * inner + here, rows)
            f_scr[pl.ds(to, rows), :] = got[m * rows : (m + 1) * rows]
        return 0

    lax.fori_loop(0, chunk, level, 0)

    @pl.when(step == steps - 1)
    def _():
        out = {}

        def add(i, value):
            low, w0, w1 = weights_x(i, ratio)
            for at, w in ((low, w0), (low + 1, w1)):
                out[at] = w * value if at not in out else out[at] + w * value

        for side in range(2):
            u = u_scr[pl.ds(inner + side * levels, levels), :]
            v = v_scr[pl.ds(inner + side * levels, levels), :]
            product = []
            for m in range(members):
                halo = []
                for part in range(2):
                    e, o = even_ref[m, part], odd_ref[m, part]
                    halo.append(jnp.where(even, o, e) if side == 0 else jnp.where(even, e, o))
                product.append(u * halo[0] + v * halo[1])
            high, lower = split(jnp.concatenate(product, axis=0))
            got = dot_nn(high, ty_scr[...]) + dot_nn(lower, ty_scr[...])
            add(-1 if side == 0 else rows, got)
        for i in range(rows):
            add(i, f_scr[pl.ds(i, pairs, stride=rows), :])
        held = {r: mask_row(value * scale, r, coarse_rows, region, regions) for r, value in out.items()}
        for done in range(PASSES):
            reach = 2 + done
            held = {
                r: mask_row(one_pass(held, r, coarse_columns), r, coarse_rows, region, regions)
                for r in range(-reach, coarse_rows + reach)
            }
        for r in range(coarse_rows):
            own_out[r] = held[r]
        for k in range(HALO):
            before, after = held[k - HALO], held[coarse_rows + k]
            a_out[k] = jnp.where(even, after, before)
            b_out[k] = jnp.where(even, before, after)


def backward(q_terms, kind, value, weight, pert, halo_even, halo_odd, hot, scale, coarse_rows, coarse_columns):
    members, parts, levels, rows, columns = pert.shape
    pairs = members * levels
    chunk = 4 if levels % 4 == 0 else 1
    whole = lambda x: pl.BlockSpec(x.shape, lambda s: (0,) * len(x.shape))
    outs = [jax.ShapeDtypeStruct((n, pairs, coarse_columns), F32) for n in (coarse_rows, HALO, HALO)]
    return pl.pallas_call(
        functools.partial(backward_kernel, scale, members, levels, chunk, coarse_rows, rows, len(q_terms)),
        grid=(levels // chunk,),
        in_specs=[*[whole(q) for q in q_terms], whole(kind), whole(value), whole(weight),
                  pl.BlockSpec((members, parts, chunk, rows, columns), lambda s: (0, 0, s, 0, 0)),
                  whole(halo_even), whole(halo_odd), *[whole(h) for h in hot]],
        out_specs=[whole(o) for o in outs],
        out_shape=outs,
        scratch_shapes=[
            pltpu.VMEM((levels * rows + 2 * levels, columns), F32),
            pltpu.VMEM((levels * rows + 2 * levels, columns), F32),
            pltpu.VMEM((columns, coarse_columns), BF16),
            pltpu.VMEM((pairs * rows, coarse_columns), F32),
        ],
        compiler_params=params(40),
        name="adjoint_to_coarse",
    )(*q_terms, kind, value, weight, pert, halo_even, halo_odd, *hot)


def join_kernel(coarse_rows, own_ref, even_ref, odd_ref, out_ref):
    even = lax.rem(lax.axis_index("reg"), 2) == 0
    pairs = own_ref.shape[1]
    for r in range(coarse_rows):
        total = own_ref[r]
        if r < HALO:
            total = total + jnp.where(even, odd_ref[r], even_ref[r])
        k = r - (coarse_rows - HALO)
        if k >= 0:
            total = total + jnp.where(even, even_ref[k], odd_ref[k])
        out_ref[pl.ds(r, pairs, stride=coarse_rows), :] = total


def join(own, got_even, got_odd):
    coarse_rows, pairs, columns = own.shape
    return pl.pallas_call(
        functools.partial(join_kernel, coarse_rows),
        out_shape=jax.ShapeDtypeStruct((pairs * coarse_rows, columns), F32),
        compiler_params=params(16),
        name="join_rows",
    )(own, got_even, got_odd)


def local(alpha, perturbation, obs_cell, obs_kind, obs_value, obs_weight):
    members, levels, coarse_rows, coarse_columns = alpha.shape
    _, _, _, rows, columns = perturbation.shape
    scale = 1.0 / math.sqrt(members * lax.axis_size("mem"))
    flat = alpha.reshape(-1, coarse_columns)
    flat_even, flat_odd = swap_even(flat), swap_odd(flat)
    pack_a, pack_b = pack(perturbation)
    halo_even, halo_odd = swap_even(pack_a), swap_odd(pack_b)
    cell, kind, value, weight = (x.reshape(1, -1) for x in (obs_cell, obs_kind, obs_value, obs_weight))
    hot = tables(cell, kind, levels, rows, columns)
    q, edge_fine = forward(flat, flat_even, flat_odd, perturbation, hot, scale)
    q = edge(q, edge_fine, halo_even, halo_odd, hot, members, levels)
    own, send_a, send_b = backward(
        others(q, "mem"), kind, value, weight, perturbation, halo_even, halo_odd, hot, scale,
        coarse_rows, coarse_columns,
    )
    return join(own, swap_even(send_a), swap_odd(send_b)).reshape(alpha.shape)


def solution(mesh):
    return jax.shard_map(
        local,
        mesh=mesh,
        in_specs=(
            P("mem", None, "reg", None),
            P("mem", None, None, "reg", None),
            P("reg"),
            P("reg"),
            P("reg"),
            P("reg"),
        ),
        out_specs=P("mem", None, "reg", None),
        check_vma=False,
    )
```

time: 148 us -> 48.7 us (0.33)
  waiting for transfers between devices: 69.5 us -> 12.2 us
  Pallas kernels: 0 us -> 18.3 us
  matrix products: 16.9 us -> 0 us
  starting transfers between devices: 28.7 us -> 14.7 us
  between operations: 13.9 us -> 0.13 us
  other arithmetic: 11.1 us -> 0 us
  local copies, waits for them, and re-layouts: 7.37 us -> 3.15 us
    psum x1 -> x0, waiting for transfers between devices: 52.2 us -> none  [local(): whole = lax.psum(partial_value, 'mem')]
    pallas_call x0 -> x6, Pallas kernels: none -> 18.3 us  [the longest x1 7.71 us: backward(): pl.pallas_call(functools.partial(backward_kernel, scale, members, levels,...]
    dot_general x6 -> x0, matrix products: 16.9 us -> none  [the longest x1 4.19 us: observe(): lax.dot_general(line_hot, weighted, (((0,), (0,)), ((), ())), precision=h...]
    ppermute x10 -> x9, starting transfers between devices: 28.7 us -> 14.7 us  [the longest x3 11.3 us: swap_odd(): return lax.ppermute(value, 'reg', swap_pairs(lax.axis_size('reg'), True))]
    ppermute x10 -> x9, waiting for transfers between devices: 17.3 us -> 12.2 us  [the longest x3 9.75 us: swap_odd(): return lax.ppermute(value, 'reg', swap_pairs(lax.axis_size('reg'), True))]
    slice x10 -> x0, local copies, waits for them, and re-layouts: 4.36 us -> none  [the longest x4 1.43 us: one_pass(): padded[:, :, 2:, 1:-1] + padded[:, :, :-2, 1:-1] + padded[:, :, 1:-1, 2:]]
    concatenate x3 -> x0, other arithmetic: 3.91 us -> none  [padded_2(): value = jnp.concatenate([before, value, after], axis=dim)]
    another operation x4 -> x0, other arithmetic: 2.6 us -> none  [the longest x2 1.57 us: observe(): return jnp.stack([grad_u, grad_v])]
  transfers between devices with their start and end apart: 11 -> 9, of which waited for: 7 -> 5; matrix products, arithmetic and copies ran while one was open for 0% -> 0% of each run, Pallas kernels for 0% -> 15%
where the time goes in v1:
time: 48.7 us; the launch traced here: 48.5 us
  Pallas kernels  18.3 us (38%)
  starting transfers between devices  14.7 us (30%)
  waiting for transfers between devices  12.2 us (25%)
  local copies, waits for them, and re-layouts  3.15 us (6%)
    ppermute x3, starting transfers between devices, swap_odd(): return lax.ppermute(value, 'reg', swap_pairs(lax.axis_size('reg'), True))  11.3 us
    ppermute x3, waiting for transfers between devices, swap_odd(): return lax.ppermute(value, 'reg', swap_pairs(lax.axis_size('reg'), True))  9.75 us
    pallas_call x1, Pallas kernels, backward(): pl.pallas_call(functools.partial(backward_kernel, scale, members, levels,...  7.71 us
    pallas_call x1, Pallas kernels, forward(): pl.pallas_call(functools.partial(forward_kernel, scale, members, levels,...  6.16 us
    unnamed x14, local copies, waits for them, and re-layouts  3.15 us
    ppermute x3, starting transfers between devices, others(): got = [lax.ppermute(value, axis, pairs) for pairs in sends]  3.12 us
    ppermute x3, waiting for transfers between devices, others(): got = [lax.ppermute(value, axis, pairs) for pairs in sends]  2.46 us
    pallas_call x1, Pallas kernels, pack(): pl.pallas_call(pack_kernel, grid=(members,), in_specs=[pl.BlockSpec((1, p...  1.7 us
  transfers between devices with their start and end apart: 9, of which 5 were waited for; matrix products, arithmetic and copies ran while one was open for 0% of the time, Pallas kernels for 15%

profile of v1, /device:TPU:1, one launch (start us, length us, event | category | flops | bytes accessed | tf_op | source)
XLA Modules:
  0.0 48.5 jit_solution(17685318212106362897)
XLA Ops:
  0.0 0.0 copy-start
  0.0 2.2 %copy-done = bf16[8,2,16,16,512]{4,3,2,1,0:T(8,128)(2,1)S(1)} copy-done((bf16[8,2,16,16,512]{4,3,2,1,0:T(8,128)(2,1)S(1)}, bf16[8,2,16,16,512]{4,3,2,1,0:T(8,128)(2,1)}, u32[]{:S(2)}) %copy-start) | copy-done | bytes 4194328
  2.2 0.0 copy-start.3
  2.2 0.0 copy-start.6
  2.2 0.0 copy-start.1
  2.2 1.7 %pack_rows.1 = (f32[8,2,16,512]{3,2,1,0:T(8,128)S(1)}, f32[8,2,16,512]{3,2,1,0:T(8,128)S(1)}) custom-call(bf16[8,2,16,16,512]{4,3,2,1,0:T(8,128)(2,1)S(1)} %copy-done), custom_call_target="tpu_custom_call" | custom-call | tf_op jit(solution)/shard_map/pack_rows/pallas_call | solution.py:130
  3.9 0.1 collective-permute-start.2
  4.0 4.6 %collective-permute-start.3 = (f32[8,2,16,512]{3,2,1,0:T(8,128)S(1)}, f32[8,2,16,512]{3,2,1,0:T(8,128)S(1)}, u32[]{:S(2)}, u32[]{:S(2)}) collective-permute-start(f32[8,2,16,512]{3,2,1,0:T(8,128)S(1)} %get-tuple-element.25), channel_id=1, source_target_pairs={{1,2},{2,1},{3,4},{4,3},{5,6},{6,5},{9,10},{10,9},{11,12},{12,11},... | collective-permute-start | bytes 1572872 | tf_op jit(solution)/shard_map/ppermute | solution.py:34
  8.6 1.9 %collective-permute-start.1 = (f32[512,128]{1,0:T(8,128)}, f32[512,128]{1,0:T(8,128)S(1)}, u32[]{:S(2)}, u32[]{:S(2)}) collective-permute-start(f32[512,128]{1,0:T(8,128)} %bitcast.6), channel_id=1, source_target_pairs={{1,2},{2,1},{3,4},{4,3},{5,6},{6,5},{9,10},{10,9},{11,12},{12,11},... | collective-permute-start | bytes 786440 | tf_op jit(solution)/shard_map/ppermute | solution.py:34
  10.5 0.1 collective-permute-start
  10.6 0.0 copy-done.3
  10.6 0.0 copy-done.6
  10.6 1.2 %one_hots.1 = (bf16[288,1024]{1,0:T(8,128)(2,1)S(1)}, bf16[288,1024]{1,0:T(8,128)(2,1)S(1)}, bf16[288,1024]{1,0:T(8,128)(2,1)S(1)}, bf16[512,1024]{1,0:T(8,128)(2,1)S(1)}, bf16[512,1024]{1,0:T(8,128)(2,1)S(1)}) custom-call(s32[1,1024]{1,0:T(1,128)S(1)} %bitcast.13, s32[1,1024]{1,0:T(1,128)S(1)} %bitcast.9), custom_call_target="tpu_custom_call" | custom-call | tf_op jit(solution)/shard_map/one_hots/pallas_call | solution.py:198
  11.8 6.4 %collective-permute-done.1.odd_ref = f32[512,128]{1,0:T(8,128)S(1)} collective-permute-done((f32[512,128]{1,0:T(8,128)}, f32[512,128]{1,0:T(8,128)S(1)}, u32[]{:S(2)}, u32[]{:S(2)}) %collective-permute-start.1) | collective-permute-done | bytes 262176 | tf_op jit(solution)/shard_map/ppermute | solution.py:34
  18.2 0.0 collective-permute-done.even_ref
  18.2 0.0 copy-done.1
  18.2 0.0 copy-start.2
  18.2 0.9 %copy-done.2 = f32[8,16,4,128]{3,2,1,0:T(4,128)S(1)} copy-done((f32[8,16,4,128]{3,2,1,0:T(4,128)S(1)}, f32[8,16,4,128]{3,2,1,0:T(4,128)}, u32[]{:S(2)}) %copy-start.2) | copy-done | bytes 262168
  19.2 0.0 copy-start.4
  19.2 0.0 copy-start.5
  19.2 6.2 %increment_at_obs.1 = (f32[4,1024]{1,0:T(4,128)S(1)}, f32[2,128,512]{2,1,0:T(8,128)S(1)}) custom-call(f32[512,128]{1,0:T(8,128)S(1)} %bitcast.8, f32[512,128]{1,0:T(8,128)S(1)} %collective-permute-done.even_ref, f32[512,128]{1,0:T(8,128)S(1)} %collective-permute-done.1.odd_ref, bf16[8,2,16,16,512]{4,3,2,1,0:T(8,128)(2,1)S(1)} %copy-done.1, ...), custom_call_target="tpu_custom_call" | custom-call | tf_op jit(solution)/shard_map/increment_at_obs/pallas_call | solution.py:316
  25.4 0.0 collective-permute-done.2.even_ref.refs_8_
  25.4 0.0 collective-permute-done.3.odd_ref.refs_9_
  25.4 0.8 %edge_at_obs.1.refs_0_ = f32[4,1024]{1,0:T(4,128)S(1)} custom-call(f32[4,1024]{1,0:T(4,128)S(1)} %get-tuple-element.22.q_ref, f32[2,128,512]{2,1,0:T(8,128)S(1)} %get-tuple-element.23.fine_ref, f32[8,2,16,512]{3,2,1,0:T(8,128)S(1)} %collective-permute-done.2.even_ref.refs_8_, f32[8,2,16,512]{3,2,1,0:T(8,128)S(1)} %collective-permute-done.3.odd_ref.refs_9_, ...), custom_call_target="tpu_custom_call" | custom-call | tf_op jit(solution)/shard_map/edge_at_obs/pallas_call | solution.py:380
  26.2 2.8 %collective-permute-start.6 = (f32[4,1024]{1,0:T(4,128)S(1)}, f32[4,1024]{1,0:T(4,128)S(1)}, u32[]{:S(2)}, u32[]{:S(2)}) collective-permute-start(f32[4,1024]{1,0:T(4,128)S(1)} %edge_at_obs.1.refs_0_), channel_id=1, source_target_pairs={{0,24},{8,16},{16,8},{24,0},{1,25},{9,17},{17,9},{25,1},{2,26},{10... | collective-permute-start | bytes 49160 | tf_op jit(solution)/shard_map/ppermute | solution.py:55
  28.9 0.2 collective-permute-start.5
  29.2 0.1 collective-permute-start.4
  29.3 0.8 %collective-permute-done.6.refs_3_ = f32[4,1024]{1,0:T(4,128)S(1)} collective-permute-done((f32[4,1024]{1,0:T(4,128)S(1)}, f32[4,1024]{1,0:T(4,128)S(1)}, u32[]{:S(2)}, u32[]{:S(2)}) %collective-permute-start.6) | collective-permute-done | bytes 16416 | tf_op jit(solution)/shard_map/ppermute | solution.py:55
  30.1 1.5 %collective-permute-done.5.refs_2_ = f32[4,1024]{1,0:T(4,128)S(1)} collective-permute-done((f32[4,1024]{1,0:T(4,128)S(1)}, f32[4,1024]{1,0:T(4,128)S(1)}, u32[]{:S(2)}, u32[]{:S(2)}) %collective-permute-start.5) | collective-permute-done | bytes 16416 | tf_op jit(solution)/shard_map/ppermute | solution.py:55
  31.5 0.2 collective-permute-done.4.refs_1_
  31.8 0.0 copy-done.4
  31.8 0.0 copy-done.5
  31.8 7.7 %adjoint_to_coarse.1 = (f32[4,128,128]{2,1,0:T(8,128)S(1)}, f32[3,128,128]{2,1,0:T(8,128)S(1)}, f32[3,128,128]{2,1,0:T(8,128)S(1)}) custom-call(f32[4,1024]{1,0:T(4,128)S(1)} %edge_at_obs.1.refs_0_, f32[4,1024]{1,0:T(4,128)S(1)} %collective-permute-done.4.refs_1_, f32[4,1024]{1,0:T(4,128)S(1)} %collective-permute-done.5.refs_2_, ...), custom_call_target="tpu_custom_call" | custom-call | tf_op jit(solution)/shard_map/adjoint_to_coarse/pallas_call | solution.py:500
  39.5 0.1 collective-permute-start.7
  39.6 4.8 %collective-permute-start.8 = (f32[3,128,128]{2,1,0:T(8,128)S(1)}, f32[3,128,128]{2,1,0:T(8,128)S(1)}, u32[]{:S(2)}, u32[]{:S(2)}) collective-permute-start(f32[3,128,128]{2,1,0:T(8,128)S(1)} %get-tuple-element.28), channel_id=1, source_target_pairs={{1,2},{2,1},{3,4},{4,3},{5,6},{6,5},{9,10},{10,9},{11,12},{12,11},... | collective-permute-start | bytes 589832 | tf_op jit(solution)/shard_map/ppermute | solution.py:34
  44.4 0.0 collective-permute-done.7.even_ref
  44.4 3.3 %collective-permute-done.8.odd_ref = f32[3,128,128]{2,1,0:T(8,128)S(1)} collective-permute-done((f32[3,128,128]{2,1,0:T(8,128)S(1)}, f32[3,128,128]{2,1,0:T(8,128)S(1)}, u32[]{:S(2)}, u32[]{:S(2)}) %collective-permute-start.8) | collective-permute-done | bytes 196640 | tf_op jit(solution)/shard_map/ppermute | solution.py:34
  47.7 0.8 %join_rows.1 = f32[512,128]{1,0:T(8,128)} custom-call(f32[4,128,128]{2,1,0:T(8,128)S(1)} %get-tuple-element.26.own_ref, f32[3,128,128]{2,1,0:T(8,128)S(1)} %collective-permute-done.7.even_ref, f32[3,128,128]{2,1,0:T(8,128)S(1)} %collective-permute-done.8.odd_ref), custom_call_target="tpu_custom_call" | custom-call | tf_op jit(solution)/shard_map/join_rows/pallas_call | solution.py:534
Async XLA Ops:
  0.0 2.2 %copy-start = (bf16[8,2,16,16,512]{4,3,2,1,0:T(8,128)(2,1)S(1)}, bf16[8,2,16,16,512]{4,3,2,1,0:T(8,128)(2,1)}, u32[]{:S(2)}) copy-start(bf16[8,2,16,16,512]{4,3,2,1,0:T(8,128)(2,1)} %refs_7_.1) | copy-start | bytes 12582916
  2.2 8.4 %copy-start.3 = (s32[1024]{0:T(1024)S(1)}, s32[1024]{0:T(1024)}, u32[]{:S(2)}) copy-start(s32[1024]{0:T(1024)} %param.9) | copy-start | bytes 12292
  2.2 8.4 %copy-start.6 = (s32[1024]{0:T(1024)S(1)}, s32[1024]{0:T(1024)}, u32[]{:S(2)}) copy-start(s32[1024]{0:T(1024)} %param.8) | copy-start | bytes 12292
  2.2 16.0 %copy-start.1 = (bf16[8,2,16,16,512]{4,3,2,1,0:T(8,128)(2,1)S(1)}, bf16[8,2,16,16,512]{4,3,2,1,0:T(8,128)(2,1)}, u32[]{:S(2)}) copy-start(bf16[8,2,16,16,512]{4,3,2,1,0:T(8,128)(2,1)} %refs_7_.1) | copy-start | bytes 12582916
  3.9 21.5 %collective-permute-start.2 = (f32[8,2,16,512]{3,2,1,0:T(8,128)S(1)}, f32[8,2,16,512]{3,2,1,0:T(8,128)S(1)}, u32[]{:S(2)}, u32[]{:S(2)}) collective-permute-start(f32[8,2,16,512]{3,2,1,0:T(8,128)S(1)} %get-tuple-element.24), channel_id=1, source_target_pairs={{0,1},{1,0},{2,3},{3,2},{4,5},{5,4},{6,7},{7,6},{8,9},{9,8},{10,11... | collective-permute-start | bytes 1572872 | tf_op jit(solution)/shard_map/ppermute | solution.py:30
  4.0 21.4 %collective-permute-start.3 = (f32[8,2,16,512]{3,2,1,0:T(8,128)S(1)}, f32[8,2,16,512]{3,2,1,0:T(8,128)S(1)}, u32[]{:S(2)}, u32[]{:S(2)}) collective-permute-start(f32[8,2,16,512]{3,2,1,0:T(8,128)S(1)} %get-tuple-element.25), channel_id=1, source_target_pairs={{1,2},{2,1},{3,4},{4,3},{5,6},{6,5},{9,10},{10,9},{11,12},{12,11},... | collective-permute-start | bytes 1572872 | tf_op jit(solution)/shard_map/ppermute | solution.py:34
  8.6 9.7 %collective-permute-start.1 = (f32[512,128]{1,0:T(8,128)}, f32[512,128]{1,0:T(8,128)S(1)}, u32[]{:S(2)}, u32[]{:S(2)}) collective-permute-start(f32[512,128]{1,0:T(8,128)} %bitcast.6), channel_id=1, source_target_pairs={{1,2},{2,1},{3,4},{4,3},{5,6},{6,5},{9,10},{10,9},{11,12},{12,11},... | collective-permute-start | bytes 786440 | tf_op jit(solution)/shard_map/ppermute | solution.py:34
  10.5 7.7 %collective-permute-start = (f32[512,128]{1,0:T(8,128)}, f32[512,128]{1,0:T(8,128)S(1)}, u32[]{:S(2)}, u32[]{:S(2)}) collective-permute-start(f32[512,128]{1,0:T(8,128)} %bitcast.7), channel_id=1, source_target_pairs={{0,1},{1,0},{2,3},{3,2},{4,5},{5,4},{6,7},{7,6},{8,9},{9,8},{10,11... | collective-permute-start | bytes 786440 | tf_op jit(solution)/shard_map/ppermute | solution.py:30
  18.2 1.0 %copy-start.2 = (f32[8,16,4,128]{3,2,1,0:T(4,128)S(1)}, f32[8,16,4,128]{3,2,1,0:T(4,128)}, u32[]{:S(2)}) copy-start(f32[8,16,4,128]{3,2,1,0:T(4,128)} %param.6) | copy-start | bytes 786436
  19.2 12.6 %copy-start.4 = (f32[1024]{0:T(1024)S(1)}, f32[1024]{0:T(1024)}, u32[]{:S(2)}) copy-start(f32[1024]{0:T(1024)} %param.10) | copy-start | bytes 12292
  19.2 12.6 %copy-start.5 = (f32[1024]{0:T(1024)S(1)}, f32[1024]{0:T(1024)}, u32[]{:S(2)}) copy-start(f32[1024]{0:T(1024)} %param.11) | copy-start | bytes 12292
  26.2 3.9 %collective-permute-start.6 = (f32[4,1024]{1,0:T(4,128)S(1)}, f32[4,1024]{1,0:T(4,128)S(1)}, u32[]{:S(2)}, u32[]{:S(2)}) collective-permute-start(f32[4,1024]{1,0:T(4,128)S(1)} %edge_at_obs.1.refs_0_), channel_id=1, source_target_pairs={{0,24},{8,16},{16,8},{24,0},{1,25},{9,17},{17,9},{25,1},{2,26},{10... | collective-permute-start | bytes 49160 | tf_op jit(solution)/shard_map/ppermute | solution.py:55
  28.9 2.6 %collective-permute-start.5 = (f32[4,1024]{1,0:T(4,128)S(1)}, f32[4,1024]{1,0:T(4,128)S(1)}, u32[]{:S(2)}, u32[]{:S(2)}) collective-permute-start(f32[4,1024]{1,0:T(4,128)S(1)} %edge_at_obs.1.refs_0_), channel_id=1, source_target_pairs={{0,16},{8,24},{16,0},{24,8},{1,17},{9,25},{17,1},{25,9},{2,18},{10... | collective-permute-start | bytes 49160 | tf_op jit(solution)/shard_map/ppermute | solution.py:55
  29.2 2.6 %collective-permute-start.4 = (f32[4,1024]{1,0:T(4,128)S(1)}, f32[4,1024]{1,0:T(4,128)S(1)}, u32[]{:S(2)}, u32[]{:S(2)}) collective-permute-start(f32[4,1024]{1,0:T(4,128)S(1)} %edge_at_obs.1.refs_0_), channel_id=1, source_target_pairs={{0,8},{8,0},{16,24},{24,16},{1,9},{9,1},{17,25},{25,17},{2,10},{10... | collective-permute-start | bytes 49160 | tf_op jit(solution)/shard_map/ppermute | solution.py:55
  39.5 4.9 %collective-permute-start.7 = (f32[3,128,128]{2,1,0:T(8,128)S(1)}, f32[3,128,128]{2,1,0:T(8,128)S(1)}, u32[]{:S(2)}, u32[]{:S(2)}) collective-permute-start(f32[3,128,128]{2,1,0:T(8,128)S(1)} %get-tuple-element.27), channel_id=1, source_target_pairs={{0,1},{1,0},{2,3},{3,2},{4,5},{5,4},{6,7},{7,6},{8,9},{9,8},{10,11... | collective-permute-start | bytes 589832 | tf_op jit(solution)/shard_map/ppermute | solution.py:30
  39.6 8.2 %collective-permute-start.8 = (f32[3,128,128]{2,1,0:T(8,128)S(1)}, f32[3,128,128]{2,1,0:T(8,128)S(1)}, u32[]{:S(2)}, u32[]{:S(2)}) collective-permute-start(f32[3,128,128]{2,1,0:T(8,128)S(1)} %get-tuple-element.28), channel_id=1, source_target_pairs={{1,2},{2,1},{3,4},{4,3},{5,6},{6,5},{9,10},{10,9},{11,12},{12,11},... | collective-permute-start | bytes 589832 | tf_op jit(solution)/shard_map/ppermute | solution.py:34

commit v2 on v1

v2 whole, which is shorter than its diff:
```python
import functools
import math

import jax
import jax.numpy as jnp
from jax import lax
from jax.experimental import pallas as pl
from jax.experimental.pallas import tpu as pltpu
from jax.sharding import PartitionSpec as P


PASSES = 2
HALO = PASSES + 1
DIFFUSE = 0.2
F32 = jnp.float32
BF16 = jnp.bfloat16


def params(mib):
    return pltpu.CompilerParams(vmem_limit_bytes=mib << 20)


def swap_pairs(n, odd):
    pairs = []
    for i in range(1 if odd else 0, n - 1, 2):
        pairs += [(i, i + 1), (i + 1, i)]
    return pairs


def swap_even(value):
    return lax.ppermute(value, "reg", swap_pairs(lax.axis_size("reg"), False))


def swap_odd(value):
    return lax.ppermute(value, "reg", swap_pairs(lax.axis_size("reg"), True))


def others(value, axis):
    n = lax.axis_size(axis)
    stride = 1
    rounds = []
    while stride < n:
        left = n // stride
        radix = 4 if left % 4 == 0 else 2 if left % 2 == 0 else left
        sends = []
        for k in range(1, radix):
            pairs = []
            for i in range(n):
                digit = (i // stride) % radix
                other = digit ^ k if radix in (2, 4) else (digit + k) % radix
                pairs.append((i, i + (other - digit) * stride))
            sends.append(pairs)
        rounds.append(sends)
        stride *= radix
    for number, sends in enumerate(rounds):
        got = [lax.ppermute(value, axis, pairs) for pairs in sends]
        if number == len(rounds) - 1:
            return [value] + got
        for part in got:
            value = value + part
    return [value]


def split(x):
    high = x.astype(BF16)
    return high, (x - high.astype(F32)).astype(BF16)


def dot_nn(a, b):
    return lax.dot_general(a, b, (((1,), (0,)), ((), ())), preferred_element_type=F32)


def dot_nt(a, b):
    return lax.dot_general(a, b, (((1,), (1,)), ((), ())), preferred_element_type=F32)


def iota(shape, dim):
    return lax.broadcasted_iota(jnp.int32, shape, dim)


def table_y(coarse, fine, coarse_dim):
    shape = (coarse, fine) if coarse_dim == 0 else (fine, coarse)
    ratio = fine // coarse
    at = (iota(shape, 1 - coarse_dim).astype(F32) + 0.5) / ratio - 0.5
    return jnp.maximum(0.0, 1.0 - jnp.abs(at - iota(shape, coarse_dim).astype(F32))).astype(BF16)


def weights_x(i, ratio):
    at = (i + 0.5) / ratio - 0.5
    low = math.floor(at)
    return low, 1.0 - (at - low), at - low


def one_pass(rows, index, columns):
    mid = rows.get(index)
    around = None
    if mid is not None:
        lane = iota(mid.shape, 1)
        left = jnp.where(lane == 0, 0.0, pltpu.roll(mid, 1, 1))
        right = jnp.where(lane == columns - 1, 0.0, pltpu.roll(mid, columns - 1, 1))
        around = left + right
    for near in (index + 1, index - 1):
        if near in rows:
            around = rows[near] if around is None else around + rows[near]
    if mid is None:
        return DIFFUSE * around
    return mid + DIFFUSE * (around - 4.0 * mid)


def mask_row(value, index, coarse_rows, region, regions):
    if index < 0:
        return jnp.where(region * coarse_rows + index >= 0, value, 0.0)
    if index >= coarse_rows:
        return jnp.where(region * coarse_rows + index < regions * coarse_rows, value, 0.0)
    return value


def decode(cell, rows, columns):
    plane = rows * columns
    level = cell // plane
    rest = cell - level * plane
    row = rest // columns
    return level, row, rest - row * columns


def prepare_kernel(
    pert_hbm, cell_hbm, kind_hbm, flat_hbm,
    pert_ref, a_ref, b_ref, r0_ref, ru_ref, rv_ref, c0_ref, cy_ref, own_ref,
    cell_ref, kind_ref, flat_ref, sem, small_sem,
):
    members, parts, levels, rows, columns = pert_ref.shape
    small = []
    for n, (source, to) in enumerate(((cell_hbm, cell_ref), (kind_hbm, kind_ref), (flat_hbm, flat_ref))):
        copy = pltpu.make_async_copy(source, to, small_sem.at[n])
        copy.start()
        small.append(copy)
    copies = []
    for m in range(members):
        copy = pltpu.make_async_copy(pert_hbm.at[m], pert_ref.at[m], sem.at[m])
        copy.start()
        copies.append(copy)

    small[0].wait()
    small[1].wait()
    cell, kind = cell_ref[...], kind_ref[...]
    level, row, column = decode(cell, rows, columns)
    line = level * rows + row
    count = cell.shape[1]
    inner = levels * rows
    minus = jnp.where(row > 0, line - 1, inner + level)
    plus = jnp.where(row < rows - 1, line + 1, inner + levels + level)
    none = jnp.full_like(line, -1)
    minus_u = jnp.where(kind == 3, minus, none)
    plus_u = jnp.where(kind == 3, plus, none)
    here_v = jnp.where((kind == 1) | (kind == 3), line, none)
    minus_v = jnp.where(kind == 2, minus, none)
    plus_v = jnp.where(kind == 2, plus, none)
    step = 32

    def lines(k, _):
        start = pl.multiple_of(k * step, step)
        at = iota((step, count), 0) + start
        ru = jnp.where(at == plus_u, 0.5, jnp.where(at == minus_u, -0.5, 0.0))
        rv = jnp.where(at == plus_v, 0.5, jnp.where(at == minus_v, -0.5, jnp.where(at == here_v, 1.0, 0.0)))
        r0 = jnp.where(at == line, 1.0, 0.0)
        ru_ref[pl.ds(start, step), :] = ru.astype(BF16)
        rv_ref[pl.ds(start, step), :] = rv.astype(BF16)
        r0_ref[pl.ds(start, step), :] = r0.astype(BF16)
        return 0

    lax.fori_loop(0, (inner + 2 * levels) // step, lines, 0)

    def cells(k, _):
        start = pl.multiple_of(k * step, step)
        at = iota((step, count), 0) + start
        c0_ref[pl.ds(start, step), :] = jnp.where(at == column, 1.0, 0.0).astype(BF16)
        cy = jnp.where(at == column + 1, 0.5, jnp.where(at == column - 1, -0.5, 0.0))
        cy_ref[pl.ds(start, step), :] = cy.astype(BF16)
        return 0

    lax.fori_loop(0, columns // step, cells, 0)

    coarse_rows, pairs, _ = own_ref.shape
    small[2].wait()
    for r in range(coarse_rows):
        own_ref[r] = flat_ref[pl.ds(r, pairs, stride=coarse_rows), :]

    even = lax.rem(lax.axis_index("reg"), 2) == 0
    shape = (2 * levels, inner)
    pick = iota(shape, 0)
    to_a = pick < levels
    edge = jnp.where(to_a == even, rows - 1, 0)
    wanted = jnp.where(to_a, pick, pick - levels) * rows + edge
    chooser = jnp.where(iota(shape, 1) == wanted, 1.0, 0.0).astype(BF16)
    for m in range(members):
        copies[m].wait()
        for part in range(parts):
            got = dot_nn(chooser, pert_ref[m, part].reshape(inner, columns))
            a_ref[m, part] = got[:levels]
            b_ref[m, part] = got[levels:]


def prepare(pert, cell, kind, flat, coarse_rows):
    members, parts, levels, rows, columns = pert.shape
    count = cell.shape[1]
    lines = levels * rows + 2 * levels
    shapes = [jax.ShapeDtypeStruct(pert.shape, pert.dtype)]
    shapes += [jax.ShapeDtypeStruct((members, parts, levels, columns), F32)] * 2
    shapes += [jax.ShapeDtypeStruct((n, count), BF16) for n in (lines, lines, lines, columns, columns)]
    shapes.append(jax.ShapeDtypeStruct((coarse_rows, flat.shape[0] // coarse_rows, flat.shape[1]), F32))
    vmem = pl.BlockSpec(memory_space=pltpu.VMEM)
    hbm = pl.BlockSpec(memory_space=pltpu.HBM)
    pert, cell, kind, flat = (pltpu.with_memory_space_constraint(x, pltpu.HBM) for x in (pert, cell, kind, flat))
    held, pack_a, pack_b, *hot, own = pl.pallas_call(
        prepare_kernel,
        in_specs=[hbm] * 4,
        out_specs=[vmem] * len(shapes),
        out_shape=shapes,
        scratch_shapes=[
            pltpu.VMEM(cell.shape, cell.dtype),
            pltpu.VMEM(kind.shape, kind.dtype),
            pltpu.VMEM(flat.shape, flat.dtype),
            pltpu.SemaphoreType.DMA((members,)),
            pltpu.SemaphoreType.DMA((3,)),
        ],
        compiler_params=params(16),
        name="prepare",
    )(pert, cell, kind, flat)
    return held, pack_a, pack_b, hot, own


def forward_kernel(
    scale, chunk,
    own_ref, even_ref, odd_ref, pert_ref, r0_ref, ru_ref, rv_ref, c0_ref, cy_ref,
    q_ref, edge_ref,
    fine_in, fine_scr, u_scr, v_scr, t_scr,
):
    region = lax.axis_index("reg")
    regions = lax.axis_size("reg")
    members, _, levels, rows, columns = pert_ref.shape
    coarse_rows, pairs, coarse_columns = own_ref.shape
    ratio = rows // coarse_rows
    block = chunk * rows
    inner = levels * rows
    even = lax.rem(region, 2) == 0
    table = table_y(coarse_columns, columns, 0)
    table = jnp.concatenate([table, table], axis=0)

    rows_in = {r: own_ref[r] for r in range(coarse_rows)}
    for k in range(HALO):
        low = coarse_rows - HALO + k
        e = even_ref[pl.ds(low, pairs, stride=coarse_rows), :]
        o = odd_ref[pl.ds(low, pairs, stride=coarse_rows), :]
        rows_in[k - HALO] = jnp.where(even, o, e)
        e = even_ref[pl.ds(k, pairs, stride=coarse_rows), :]
        o = odd_ref[pl.ds(k, pairs, stride=coarse_rows), :]
        rows_in[coarse_rows + k] = jnp.where(even, e, o)
    for done in range(PASSES):
        reach = HALO - 1 - done
        rows_in = {
            r: mask_row(one_pass(rows_in, r, coarse_columns), r, coarse_rows, region, regions)
            for r in range(-reach, coarse_rows + reach)
        }
    for i in range(-1, rows + 1):
        low, w0, w1 = weights_x(i, ratio)
        value = (w0 * rows_in[low] + w1 * rows_in[low + 1]) * scale
        if 0 <= i < rows:
            fine_in[pl.ds(i, pairs, stride=rows), :] = value
        else:
            high, lower = split(value)
            got = dot_nn(jnp.concatenate([high, lower], axis=1), table)
            edge_ref[0 if i < 0 else 1] = got

    for step in range(levels // chunk):
        parts = []
        for m in range(members):
            parts.append(fine_in[pl.ds(m * inner + step * block, block), :])
        high, lower = split(jnp.concatenate(parts, axis=0))
        fine_scr[...] = dot_nn(jnp.concatenate([high, lower], axis=1), table)

        def level(k, _, step=step):
            at = pl.multiple_of(k * rows, rows)
            u = v = None
            for m in range(members):
                fine = fine_scr[pl.ds(m * block + at, rows), :]
                pu = fine * pert_ref[m, 0, step * chunk + k].astype(F32)
                pv = fine * pert_ref[m, 1, step * chunk + k].astype(F32)
                u = pu if u is None else u + pu
                v = pv if v is None else v + pv
            to = pl.multiple_of(step * block + at, rows)
            u_scr[pl.ds(to, rows), :] = u
            v_scr[pl.ds(to, rows), :] = v
            return 0

        lax.fori_loop(0, chunk, level, 0)

    for n, source in enumerate((u_scr, v_scr)):
        high, lower = split(source[...].T)
        t_scr[2 * n] = high
        t_scr[2 * n + 1] = lower
    count = r0_ref.shape[1]
    width = min(256, count)

    def observe(k, _):
        at = pl.ds(pl.multiple_of(k * width, width), width)
        c0 = c0_ref[:, at].astype(F32)
        cy = cy_ref[:, at].astype(F32)
        r0 = r0_ref[pl.ds(0, inner), at]
        u_row = dot_nn(t_scr[0], r0) + dot_nn(t_scr[1], r0)
        q_ref[pl.ds(0, 1), at] = jnp.sum(u_row * c0, axis=0, keepdims=True)
        q_ref[pl.ds(3, 1), at] = jnp.sum(u_row * cy, axis=0, keepdims=True)
        rv = rv_ref[pl.ds(0, inner), at]
        v_row = dot_nn(t_scr[2], rv) + dot_nn(t_scr[3], rv)
        q_ref[pl.ds(1, 1), at] = jnp.sum(v_row * c0, axis=0, keepdims=True)
        ru = ru_ref[pl.ds(0, inner), at]
        d_row = dot_nn(t_scr[0], ru) + dot_nn(t_scr[1], ru)
        q_ref[pl.ds(2, 1), at] = jnp.sum(d_row * c0, axis=0, keepdims=True)
        return 0

    lax.fori_loop(0, count // width, observe, 0)


def forward(own, got_even, got_odd, pert, hot, scale):
    members, _, levels, rows, columns = pert.shape
    _, pairs, coarse_columns = own.shape
    chunk = 4 if levels % 4 == 0 else 1
    count = hot[0].shape[1]
    return pl.pallas_call(
        functools.partial(forward_kernel, scale, chunk),
        out_shape=[jax.ShapeDtypeStruct((4, count), F32),
                   jax.ShapeDtypeStruct((2, pairs, columns), F32)],
        scratch_shapes=[
            pltpu.VMEM((pairs * rows, coarse_columns), F32),
            pltpu.VMEM((members * chunk * rows, columns), F32),
            pltpu.VMEM((levels * rows, columns), F32),
            pltpu.VMEM((levels * rows, columns), F32),
            pltpu.VMEM((4, columns, levels * rows), BF16),
        ],
        compiler_params=params(28),
        name="increment_at_obs",
    )(own, got_even, got_odd, pert, *hot)


def edge_kernel(members, levels, q_ref, fine_ref, even_ref, odd_ref, ru_ref, rv_ref, c0_ref, out_ref):
    even = lax.rem(lax.axis_index("reg"), 2) == 0
    table = []
    for part in range(2):
        for side in range(2):
            total = None
            for m in range(members):
                e, o = even_ref[m, part], odd_ref[m, part]
                halo = jnp.where(even, o, e) if side == 0 else jnp.where(even, e, o)
                term = fine_ref[side, pl.ds(m * levels, levels), :] * halo
                total = term if total is None else total + term
            table.append(total)
    u = jnp.concatenate(table[:2], axis=0).T
    v = jnp.concatenate(table[2:], axis=0).T
    u_high, u_low = split(u)
    v_high, v_low = split(v)
    left = jnp.concatenate([u_high, u_low, v_high, v_low], axis=1)
    lines, count = ru_ref.shape
    tail = pl.ds(lines - 2 * levels, 2 * levels)
    width = min(256, count)
    for k in range(count // width):
        at = pl.ds(k * width, width)
        rc = ru_ref[tail, at]
        vc = rv_ref[tail, at]
        row = dot_nn(left, jnp.concatenate([rc, rc, vc, vc], axis=0))
        seen = jnp.sum(row * c0_ref[:, at].astype(F32), axis=0, keepdims=True)
        in_u = jnp.sum(jnp.abs(rc.astype(F32)), axis=0, keepdims=True) > 0.0
        in_v = jnp.sum(jnp.abs(vc.astype(F32)), axis=0, keepdims=True) > 0.0
        out_ref[pl.ds(0, 1), at] = q_ref[pl.ds(0, 1), at]
        out_ref[pl.ds(1, 1), at] = q_ref[pl.ds(1, 1), at] + jnp.where(in_v, seen, 0.0)
        out_ref[pl.ds(2, 1), at] = q_ref[pl.ds(2, 1), at] + jnp.where(in_u, seen, 0.0)
        out_ref[pl.ds(3, 1), at] = q_ref[pl.ds(3, 1), at]


def edge(q, fine, halo_even, halo_odd, hot, members, levels):
    _, ru, rv, c0, _ = hot
    return pl.pallas_call(
        functools.partial(edge_kernel, members, levels),
        out_shape=jax.ShapeDtypeStruct(q.shape, F32),
        compiler_params=params(16),
        name="edge_at_obs",
    )(q, fine, halo_even, halo_odd, ru, rv, c0)


def backward_kernel(scale, chunk, terms, *refs):
    q_refs = refs[:terms]
    (kind_ref, value_ref, weight_ref, pert_ref, even_ref, odd_ref,
     r0_ref, ru_ref, rv_ref, c0_ref, cy_ref,
     own_out, a_out, b_out,
     u_scr, v_scr, f_scr) = refs[terms:]
    region = lax.axis_index("reg")
    regions = lax.axis_size("reg")
    members, _, levels, rows, columns = pert_ref.shape
    coarse_rows, pairs, coarse_columns = own_out.shape
    ratio = rows // coarse_rows
    inner = levels * rows
    even = lax.rem(region, 2) == 0
    table = table_y(coarse_columns, columns, 1)

    q = q_refs[0][...]
    for ref in q_refs[1:]:
        q = q + ref[...]
    q0, q1, q2, q3 = (q[n : n + 1] for n in range(4))
    kind = kind_ref[...]
    seen = jnp.where(kind == 0, q0, jnp.where(kind == 1, q1, jnp.where(kind == 2, q1 - q3, q0 * q2 + q1 * q3)))
    misfit = weight_ref[...] * (seen - value_ref[...])
    zero = jnp.zeros_like(misfit)
    a = jnp.where(kind == 0, misfit, jnp.where(kind == 3, misfit * q2, zero))
    b = jnp.where(kind == 2, -misfit, jnp.where(kind == 3, misfit * q1, zero))
    c = jnp.where(kind == 3, misfit * q0, zero)
    g = jnp.where(kind == 3, misfit * q3, jnp.where(kind == 0, zero, misfit))
    c0, cy = c0_ref[...], cy_ref[...]
    r0, ru, rv = r0_ref[pl.ds(0, inner), :], ru_ref[...], rv_ref[...]
    total_u = total_c = total_v = None
    for a_part, b_part, c_part, g_part in zip(split(a), split(b), split(c), split(g)):
        t = dot_nt(r0, c0 * a_part + cy * b_part)
        total_u = t if total_u is None else total_u + t
        t = dot_nt(ru, c0 * c_part)
        total_c = t if total_c is None else total_c + t
        t = dot_nt(rv, c0 * g_part)
        total_v = t if total_v is None else total_v + t
    u_scr[pl.ds(0, inner), :] = total_u + total_c[:inner]
    u_scr[pl.ds(inner, 2 * levels), :] = total_c[inner:]
    v_scr[...] = total_v

    def some(s, _):
        products = [[] for _ in range(members)]
        for n in range(chunk):
            k = s * chunk + n
            here = pl.multiple_of(k * rows, rows)
            u = u_scr[pl.ds(here, rows), :]
            v = v_scr[pl.ds(here, rows), :]
            for m in range(members):
                products[m].append(u * pert_ref[m, 0, k].astype(F32) + v * pert_ref[m, 1, k].astype(F32))
        high, lower = split(jnp.concatenate([p for one in products for p in one], axis=0))
        got = dot_nn(high, table) + dot_nn(lower, table)
        block = chunk * rows
        for m in range(members):
            to = pl.multiple_of(m * inner + s * block, block)
            f_scr[pl.ds(to, block), :] = got[m * block : (m + 1) * block]
        return 0

    lax.fori_loop(0, levels // chunk, some, 0)

    out = {}

    def add(i, value):
        low, w0, w1 = weights_x(i, ratio)
        for at, w in ((low, w0), (low + 1, w1)):
            out[at] = w * value if at not in out else out[at] + w * value

    for side in range(2):
        u = u_scr[pl.ds(inner + side * levels, levels), :]
        v = v_scr[pl.ds(inner + side * levels, levels), :]
        product = []
        for m in range(members):
            halo = []
            for part in range(2):
                e, o = even_ref[m, part], odd_ref[m, part]
                halo.append(jnp.where(even, o, e) if side == 0 else jnp.where(even, e, o))
            product.append(u * halo[0] + v * halo[1])
        high, lower = split(jnp.concatenate(product, axis=0))
        got = dot_nn(high, table) + dot_nn(lower, table)
        add(-1 if side == 0 else rows, got)
    for i in range(rows):
        add(i, f_scr[pl.ds(i, pairs, stride=rows), :])
    held = {r: mask_row(value * scale, r, coarse_rows, region, regions) for r, value in out.items()}
    for done in range(PASSES):
        reach = 2 + done
        held = {
            r: mask_row(one_pass(held, r, coarse_columns), r, coarse_rows, region, regions)
            for r in range(-reach, coarse_rows + reach)
        }
    for r in range(coarse_rows):
        own_out[r] = held[r]
    for k in range(HALO):
        before, after = held[k - HALO], held[coarse_rows + k]
        a_out[k] = jnp.where(even, after, before)
        b_out[k] = jnp.where(even, before, after)


def backward(q_terms, kind, value, weight, pert, halo_even, halo_odd, hot, scale, coarse_rows, coarse_columns):
    members, _, levels, rows, columns = pert.shape
    pairs = members * levels
    chunk = 2 if levels % 2 == 0 else 1
    outs = [jax.ShapeDtypeStruct((n, pairs, coarse_columns), F32) for n in (coarse_rows, HALO, HALO)]
    return pl.pallas_call(
        functools.partial(backward_kernel, scale, chunk, len(q_terms)),
        out_shape=outs,
        scratch_shapes=[
            pltpu.VMEM((levels * rows + 2 * levels, columns), F32),
            pltpu.VMEM((levels * rows + 2 * levels, columns), F32),
            pltpu.VMEM((pairs * rows, coarse_columns), F32),
        ],
        compiler_params=params(28),
        name="adjoint_to_coarse",
    )(*q_terms, kind, value, weight, pert, halo_even, halo_odd, *hot)


def join_kernel(coarse_rows, own_ref, even_ref, odd_ref, out_ref):
    even = lax.rem(lax.axis_index("reg"), 2) == 0
    pairs = own_ref.shape[1]
    for r in range(coarse_rows):
        total = own_ref[r]
        if r < HALO:
            total = total + jnp.where(even, odd_ref[r], even_ref[r])
        k = r - (coarse_rows - HALO)
        if k >= 0:
            total = total + jnp.where(even, even_ref[k], odd_ref[k])
        out_ref[pl.ds(r, pairs, stride=coarse_rows), :] = total


def join(own, got_even, got_odd):
    coarse_rows, pairs, columns = own.shape
    return pl.pallas_call(
        functools.partial(join_kernel, coarse_rows),
        out_shape=jax.ShapeDtypeStruct((pairs * coarse_rows, columns), F32),
        compiler_params=params(16),
        name="join_rows",
    )(own, got_even, got_odd)


def local(alpha, perturbation, obs_cell, obs_kind, obs_value, obs_weight):
    members, levels, coarse_rows, coarse_columns = alpha.shape
    scale = 1.0 / math.sqrt(members * lax.axis_size("mem"))
    flat = alpha.reshape(-1, coarse_columns)
    cell, kind, value, weight = (x.reshape(1, -1) for x in (obs_cell, obs_kind, obs_value, obs_weight))
    perturbation, pack_a, pack_b, hot, own = prepare(perturbation, cell, kind, flat, coarse_rows)
    flat_odd = swap_odd(flat)
    flat_even = swap_even(flat)
    halo_odd = swap_odd(pack_b)
    halo_even = swap_even(pack_a)
    q, edge_fine = forward(own, flat_even, flat_odd, perturbation, hot, scale)
    q = edge(q, edge_fine, halo_even, halo_odd, hot, members, levels)
    terms = others(q, "mem")
    own, send_a, send_b = backward(
        terms, kind, value, weight, perturbation, halo_even, halo_odd, hot, scale,
        coarse_rows, coarse_columns,
    )
    got_odd = swap_odd(send_b)
    got_even = swap_even(send_a)
    return join(own, got_even, got_odd).reshape(alpha.shape)


def solution(mesh):
    return jax.shard_map(
        local,
        mesh=mesh,
        in_specs=(
            P("mem", None, "reg", None),
            P("mem", None, None, "reg", None),
            P("reg"),
            P("reg"),
            P("reg"),
            P("reg"),
        ),
        out_specs=P("mem", None, "reg", None),
        check_vma=False,
    )
```

time: 48.7 us -> 46.4 us (0.953)
  local copies, waits for them, and re-layouts: 3.15 us -> 0.01 us
  waiting for transfers between devices: 12.2 us -> 13.4 us
    unnamed x14 -> x8, local copies, waits for them, and re-layouts: 3.15 us -> 0.01 us
    ppermute x3, waiting for transfers between devices: 9.75 us -> 11 us  [swap_odd(): return lax.ppermute(value, 'reg', swap_pairs(lax.axis_size('reg'), True))]
    pallas_call x5 -> x4, Pallas kernels: 17.6 us -> 17.2 us  [the longest x1 6.07 us: backward(): pl.pallas_call(functools.partial(backward_kernel, scale, chunk, len(q_ter...]
  transfers between devices with their start and end apart: 9 -> 9, of which waited for: 5 -> 5; matrix products, arithmetic and copies ran while one was open for 0% -> 0% of each run, Pallas kernels for 15% -> 12%
where the time goes in v2:
time: 46.4 us; the launch traced here: 46.2 us
  Pallas kernels  18 us (39%)
  starting transfers between devices  14.7 us (32%)
  waiting for transfers between devices  13.4 us (29%)
    ppermute x3, starting transfers between devices, swap_odd(): return lax.ppermute(value, 'reg', swap_pairs(lax.axis_size('reg'), True))  11.3 us
    ppermute x3, waiting for transfers between devices, swap_odd(): return lax.ppermute(value, 'reg', swap_pairs(lax.axis_size('reg'), True))  11 us
    pallas_call x1, Pallas kernels, backward(): pl.pallas_call(functools.partial(backward_kernel, scale, chunk, len(q_ter...  6.07 us
    pallas_call x1, Pallas kernels, forward(): pl.pallas_call(functools.partial(forward_kernel, scale, chunk), out_shape...  5.77 us
    pallas_call x1, Pallas kernels, prepare(): pl.pallas_call(prepare_kernel, in_specs=[hbm] * 4, out_specs=[vmem] * len...  4.6 us
    ppermute x3, starting transfers between devices, others(): got = [lax.ppermute(value, axis, pairs) for pairs in sends]  3.1 us
    ppermute x3, waiting for transfers between devices, others(): got = [lax.ppermute(value, axis, pairs) for pairs in sends]  2.45 us
  transfers between devices with their start and end apart: 9, of which 5 were waited for; matrix products, arithmetic and copies ran while one was open for 0% of the time, Pallas kernels for 12%

profile of v2, /device:TPU:1, one launch (start us, length us, event | category | flops | bytes accessed | tf_op | source)
XLA Modules:
  0.0 46.2 jit_solution(15085644525990654093)
XLA Ops:
  0.0 0.0 copy-start.3
  0.0 4.6 %prepare.1 = (bf16[8,2,16,16,512]{4,3,2,1,0:T(8,128)(2,1)S(1)}, f32[8,2,16,512]{3,2,1,0:T(8,128)S(1)}, f32[8,2,16,512]{3,2,1,0:T(8,128)S(1)}, bf16[288,1024]{1,0...) custom-call(bf16[8,2,16,16,512]{4,3,2,1,0:T(8,128)(2,1)} %pert_hbm.1, ...), custom_call_target="tpu_custom_call" | custom-call | tf_op jit(solution)/shard_map/prepare/pallas_call | solution.py:214
  4.6 0.1 collective-permute-start.2
  4.7 4.6 %collective-permute-start.3 = (f32[8,2,16,512]{3,2,1,0:T(8,128)S(1)}, f32[8,2,16,512]{3,2,1,0:T(8,128)S(1)}, u32[]{:S(2)}, u32[]{:S(2)}) collective-permute-start(f32[8,2,16,512]{3,2,1,0:T(8,128)S(1)} %get-tuple-element.29), channel_id=1, source_target_pairs={{1,2},{2,1},{3,4},{4,3},{5,6},{6,5},{9,10},{10,9},{11,12},{12,11},... | collective-permute-start | bytes 1572872 | tf_op jit(solution)/shard_map/ppermute | solution.py:35
  9.3 0.0 copy-done.3
  9.3 1.9 %collective-permute-start.1 = (f32[512,128]{1,0:T(8,128)S(1)}, f32[512,128]{1,0:T(8,128)S(1)}, u32[]{:S(2)}, u32[]{:S(2)}) collective-permute-start(f32[512,128]{1,0:T(8,128)S(1)} %bitcast.11), channel_id=1, source_target_pairs={{1,2},{2,1},{3,4},{4,3},{5,6},{6,5},{9,10},{10,9},{11,12},{12,11},... | collective-permute-start | bytes 786440 | tf_op jit(solution)/shard_map/ppermute | solution.py:35
  11.2 0.1 collective-permute-start
  11.3 7.6 %collective-permute-done.1.odd_ref = f32[512,128]{1,0:T(8,128)S(1)} collective-permute-done((f32[512,128]{1,0:T(8,128)S(1)}, f32[512,128]{1,0:T(8,128)S(1)}, u32[]{:S(2)}, u32[]{:S(2)}) %collective-permute-start.1) | collective-permute-done | bytes 262176 | tf_op jit(solution)/shard_map/ppermute | solution.py:35
  18.9 0.0 collective-permute-done.even_ref
  18.9 0.0 copy-start
  18.9 0.0 copy-start.1
  18.9 0.0 copy-start.2
  19.0 5.8 %increment_at_obs.1 = (f32[4,1024]{1,0:T(4,128)S(1)}, f32[2,128,512]{2,1,0:T(8,128)S(1)}) custom-call(f32[4,128,128]{2,1,0:T(8,128)S(1)} %get-tuple-element.19.own_ref, f32[512,128]{1,0:T(8,128)S(1)} %collective-permute-done.even_ref, f32[512,128]{1,0:T(8,128)S(1)} %collective-permute-done.1.odd_ref, ...), custom_call_target="tpu_custom_call" | custom-call | tf_op jit(solution)/shard_map/increment_at_obs/pallas_call | solution.py:328
  24.7 0.0 collective-permute-done.2.even_ref.refs_8_
  24.7 0.0 collective-permute-done.3.odd_ref.refs_9_
  24.8 0.8 %edge_at_obs.1.refs_0_ = f32[4,1024]{1,0:T(4,128)S(1)} custom-call(f32[4,1024]{1,0:T(4,128)S(1)} %get-tuple-element.26.q_ref, f32[2,128,512]{2,1,0:T(8,128)S(1)} %get-tuple-element.27.fine_ref, f32[8,2,16,512]{3,2,1,0:T(8,128)S(1)} %collective-permute-done.2.even_ref.refs_8_, f32[8,2,16,512]{3,2,1,0:T(8,128)S(1)} %collective-permute-done.3.odd_ref.refs_9_, ...), custom_call_target="tpu_custom_call" | custom-call | tf_op jit(solution)/shard_map/edge_at_obs/pallas_call | solution.py:380
  25.6 2.7 %collective-permute-start.6 = (f32[4,1024]{1,0:T(4,128)S(1)}, f32[4,1024]{1,0:T(4,128)S(1)}, u32[]{:S(2)}, u32[]{:S(2)}) collective-permute-start(f32[4,1024]{1,0:T(4,128)S(1)} %edge_at_obs.1.refs_0_), channel_id=1, source_target_pairs={{0,24},{8,16},{16,8},{24,0},{1,25},{9,17},{17,9},{25,1},{2,26},{10... | collective-permute-start | bytes 49160 | tf_op jit(solution)/shard_map/ppermute | solution.py:56
  28.3 0.2 collective-permute-start.5
  28.5 0.1 collective-permute-start.4
  28.7 0.8 %collective-permute-done.6.refs_3_ = f32[4,1024]{1,0:T(4,128)S(1)} collective-permute-done((f32[4,1024]{1,0:T(4,128)S(1)}, f32[4,1024]{1,0:T(4,128)S(1)}, u32[]{:S(2)}, u32[]{:S(2)}) %collective-permute-start.6) | collective-permute-done | bytes 16416 | tf_op jit(solution)/shard_map/ppermute | solution.py:56
  29.4 1.5 %collective-permute-done.5.refs_2_ = f32[4,1024]{1,0:T(4,128)S(1)} collective-permute-done((f32[4,1024]{1,0:T(4,128)S(1)}, f32[4,1024]{1,0:T(4,128)S(1)}, u32[]{:S(2)}, u32[]{:S(2)}) %collective-permute-start.5) | collective-permute-done | bytes 16416 | tf_op jit(solution)/shard_map/ppermute | solution.py:56
  30.9 0.2 collective-permute-done.4.refs_1_
  31.1 0.0 copy-done
  31.1 0.0 copy-done.1
  31.1 0.0 copy-done.2
  31.1 6.1 %adjoint_to_coarse.1 = (f32[4,128,128]{2,1,0:T(8,128)S(1)}, f32[3,128,128]{2,1,0:T(8,128)S(1)}, f32[3,128,128]{2,1,0:T(8,128)S(1)}) custom-call(f32[4,1024]{1,0:T(4,128)S(1)} %edge_at_obs.1.refs_0_, f32[4,1024]{1,0:T(4,128)S(1)} %collective-permute-done.4.refs_1_, f32[4,1024]{1,0:T(4,128)S(1)} %collective-permute-done.5.refs_2_, ...), custom_call_target="tpu_custom_call" | custom-call | tf_op jit(solution)/shard_map/adjoint_to_coarse/pallas_call | solution.py:490
  37.2 0.1 collective-permute-start.7
  37.3 4.8 %collective-permute-start.8 = (f32[3,128,128]{2,1,0:T(8,128)S(1)}, f32[3,128,128]{2,1,0:T(8,128)S(1)}, u32[]{:S(2)}, u32[]{:S(2)}) collective-permute-start(f32[3,128,128]{2,1,0:T(8,128)S(1)} %get-tuple-element.32), channel_id=1, source_target_pairs={{1,2},{2,1},{3,4},{4,3},{5,6},{6,5},{9,10},{10,9},{11,12},{12,11},... | collective-permute-start | bytes 589832 | tf_op jit(solution)/shard_map/ppermute | solution.py:35
  42.1 0.0 collective-permute-done.7.even_ref
  42.1 3.3 %collective-permute-done.8.odd_ref = f32[3,128,128]{2,1,0:T(8,128)S(1)} collective-permute-done((f32[3,128,128]{2,1,0:T(8,128)S(1)}, f32[3,128,128]{2,1,0:T(8,128)S(1)}, u32[]{:S(2)}, u32[]{:S(2)}) %collective-permute-start.8) | collective-permute-done | bytes 196640 | tf_op jit(solution)/shard_map/ppermute | solution.py:35
  45.5 0.8 %join_rows.1 = f32[512,128]{1,0:T(8,128)} custom-call(f32[4,128,128]{2,1,0:T(8,128)S(1)} %get-tuple-element.30.own_ref, f32[3,128,128]{2,1,0:T(8,128)S(1)} %collective-permute-done.7.even_ref, f32[3,128,128]{2,1,0:T(8,128)S(1)} %collective-permute-done.8.odd_ref), custom_call_target="tpu_custom_call" | custom-call | tf_op jit(solution)/shard_map/join_rows/pallas_call | solution.py:518
Async XLA Ops:
  0.0 9.3 %copy-start.3 = (f32[8,16,4,128]{3,2,1,0:T(4,128)S(1)}, f32[8,16,4,128]{3,2,1,0:T(4,128)}, u32[]{:S(2)}) copy-start(f32[8,16,4,128]{3,2,1,0:T(4,128)} %param.6) | copy-start | bytes 786436
  4.6 20.1 %collective-permute-start.2 = (f32[8,2,16,512]{3,2,1,0:T(8,128)S(1)}, f32[8,2,16,512]{3,2,1,0:T(8,128)S(1)}, u32[]{:S(2)}, u32[]{:S(2)}) collective-permute-start(f32[8,2,16,512]{3,2,1,0:T(8,128)S(1)} %get-tuple-element.28), channel_id=1, source_target_pairs={{0,1},{1,0},{2,3},{3,2},{4,5},{5,4},{6,7},{7,6},{8,9},{9,8},{10,11... | collective-permute-start | bytes 1572872 | tf_op jit(solution)/shard_map/ppermute | solution.py:31
  4.7 20.1 %collective-permute-start.3 = (f32[8,2,16,512]{3,2,1,0:T(8,128)S(1)}, f32[8,2,16,512]{3,2,1,0:T(8,128)S(1)}, u32[]{:S(2)}, u32[]{:S(2)}) collective-permute-start(f32[8,2,16,512]{3,2,1,0:T(8,128)S(1)} %get-tuple-element.29), channel_id=1, source_target_pairs={{1,2},{2,1},{3,4},{4,3},{5,6},{6,5},{9,10},{10,9},{11,12},{12,11},... | collective-permute-start | bytes 1572872 | tf_op jit(solution)/shard_map/ppermute | solution.py:35
  9.3 9.6 %collective-permute-start.1 = (f32[512,128]{1,0:T(8,128)S(1)}, f32[512,128]{1,0:T(8,128)S(1)}, u32[]{:S(2)}, u32[]{:S(2)}) collective-permute-start(f32[512,128]{1,0:T(8,128)S(1)} %bitcast.11), channel_id=1, source_target_pairs={{1,2},{2,1},{3,4},{4,3},{5,6},{6,5},{9,10},{10,9},{11,12},{12,11},... | collective-permute-start | bytes 786440 | tf_op jit(solution)/shard_map/ppermute | solution.py:35
  11.2 7.7 %collective-permute-start = (f32[512,128]{1,0:T(8,128)S(1)}, f32[512,128]{1,0:T(8,128)S(1)}, u32[]{:S(2)}, u32[]{:S(2)}) collective-permute-start(f32[512,128]{1,0:T(8,128)S(1)} %bitcast.12), channel_id=1, source_target_pairs={{0,1},{1,0},{2,3},{3,2},{4,5},{5,4},{6,7},{7,6},{8,9},{9,8},{10,11... | collective-permute-start | bytes 786440 | tf_op jit(solution)/shard_map/ppermute | solution.py:31
  18.9 12.2 %copy-start = (s32[1024]{0:T(1024)S(1)}, s32[1024]{0:T(1024)}, u32[]{:S(2)}) copy-start(s32[1024]{0:T(1024)} %param.9) | copy-start | bytes 12292
  18.9 12.2 %copy-start.1 = (f32[1024]{0:T(1024)S(1)}, f32[1024]{0:T(1024)}, u32[]{:S(2)}) copy-start(f32[1024]{0:T(1024)} %param.10) | copy-start | bytes 12292
  18.9 12.2 %copy-start.2 = (f32[1024]{0:T(1024)S(1)}, f32[1024]{0:T(1024)}, u32[]{:S(2)}) copy-start(f32[1024]{0:T(1024)} %param.11) | copy-start | bytes 12292
  25.6 3.9 %collective-permute-start.6 = (f32[4,1024]{1,0:T(4,128)S(1)}, f32[4,1024]{1,0:T(4,128)S(1)}, u32[]{:S(2)}, u32[]{:S(2)}) collective-permute-start(f32[4,1024]{1,0:T(4,128)S(1)} %edge_at_obs.1.refs_0_), channel_id=1, source_target_pairs={{0,24},{8,16},{16,8},{24,0},{1,25},{9,17},{17,9},{25,1},{2,26},{10... | collective-permute-start | bytes 49160 | tf_op jit(solution)/shard_map/ppermute | solution.py:56
  28.3 2.6 %collective-permute-start.5 = (f32[4,1024]{1,0:T(4,128)S(1)}, f32[4,1024]{1,0:T(4,128)S(1)}, u32[]{:S(2)}, u32[]{:S(2)}) collective-permute-start(f32[4,1024]{1,0:T(4,128)S(1)} %edge_at_obs.1.refs_0_), channel_id=1, source_target_pairs={{0,16},{8,24},{16,0},{24,8},{1,17},{9,25},{17,1},{25,9},{2,18},{10... | collective-permute-start | bytes 49160 | tf_op jit(solution)/shard_map/ppermute | solution.py:56
  28.5 2.6 %collective-permute-start.4 = (f32[4,1024]{1,0:T(4,128)S(1)}, f32[4,1024]{1,0:T(4,128)S(1)}, u32[]{:S(2)}, u32[]{:S(2)}) collective-permute-start(f32[4,1024]{1,0:T(4,128)S(1)} %edge_at_obs.1.refs_0_), channel_id=1, source_target_pairs={{0,8},{8,0},{16,24},{24,16},{1,9},{9,1},{17,25},{25,17},{2,10},{10... | collective-permute-start | bytes 49160 | tf_op jit(solution)/shard_map/ppermute | solution.py:56
  37.2 4.9 %collective-permute-start.7 = (f32[3,128,128]{2,1,0:T(8,128)S(1)}, f32[3,128,128]{2,1,0:T(8,128)S(1)}, u32[]{:S(2)}, u32[]{:S(2)}) collective-permute-start(f32[3,128,128]{2,1,0:T(8,128)S(1)} %get-tuple-element.31), channel_id=1, source_target_pairs={{0,1},{1,0},{2,3},{3,2},{4,5},{5,4},{6,7},{7,6},{8,9},{9,8},{10,11... | collective-permute-start | bytes 589832 | tf_op jit(solution)/shard_map/ppermute | solution.py:31
  37.3 8.2 %collective-permute-start.8 = (f32[3,128,128]{2,1,0:T(8,128)S(1)}, f32[3,128,128]{2,1,0:T(8,128)S(1)}, u32[]{:S(2)}, u32[]{:S(2)}) collective-permute-start(f32[3,128,128]{2,1,0:T(8,128)S(1)} %get-tuple-element.32), channel_id=1, source_target_pairs={{1,2},{2,1},{3,4},{4,3},{5,6},{6,5},{9,10},{10,9},{11,12},{12,11},... | collective-permute-start | bytes 589832 | tf_op jit(solution)/shard_map/ppermute | solution.py:35

commit v3 on v2

v3 whole, which is shorter than its diff:
```python
import functools
import math

import jax
import jax.numpy as jnp
from jax import lax
from jax.experimental import pallas as pl
from jax.experimental.pallas import tpu as pltpu
from jax.sharding import PartitionSpec as P


PASSES = 2
HALO = PASSES + 1
DIFFUSE = 0.2
CENTRE = round((1.0 - 4.0 * DIFFUSE) / DIFFUSE)
F32 = jnp.float32
BF16 = jnp.bfloat16


def params(mib):
    return pltpu.CompilerParams(vmem_limit_bytes=mib << 20)


def swap_pairs(n, odd):
    pairs = []
    for i in range(1 if odd else 0, n - 1, 2):
        pairs += [(i, i + 1), (i + 1, i)]
    return pairs


def swap_even(value):
    return lax.ppermute(value, "reg", swap_pairs(lax.axis_size("reg"), False))


def swap_odd(value):
    return lax.ppermute(value, "reg", swap_pairs(lax.axis_size("reg"), True))


def others(value, axis):
    n = lax.axis_size(axis)
    stride = 1
    rounds = []
    while stride < n:
        left = n // stride
        radix = 4 if left % 4 == 0 else 2 if left % 2 == 0 else left
        sends = []
        for k in range(1, radix):
            pairs = []
            for i in range(n):
                digit = (i // stride) % radix
                other = digit ^ k if radix in (2, 4) else (digit + k) % radix
                pairs.append((i, i + (other - digit) * stride))
            sends.append(pairs)
        rounds.append(sends)
        stride *= radix
    for number, sends in enumerate(rounds):
        got = [lax.ppermute(value, axis, pairs) for pairs in sends]
        if number == len(rounds) - 1:
            return [value] + got
        for part in got:
            value = value + part
    return [value]


def split(x):
    high = x.astype(BF16)
    return high, (x - high.astype(F32)).astype(BF16)


def dot_nn(a, b):
    return lax.dot_general(a, b, (((1,), (0,)), ((), ())), preferred_element_type=F32)


def dot_nt(a, b):
    return lax.dot_general(a, b, (((1,), (1,)), ((), ())), preferred_element_type=F32)


def iota(shape, dim):
    return lax.broadcasted_iota(jnp.int32, shape, dim)


def table_y(coarse, fine, coarse_dim):
    shape = (coarse, fine) if coarse_dim == 0 else (fine, coarse)
    ratio = fine // coarse
    at = (iota(shape, 1 - coarse_dim).astype(F32) + 0.5) / ratio - 0.5
    return jnp.maximum(0.0, 1.0 - jnp.abs(at - iota(shape, coarse_dim).astype(F32))).astype(BF16)


def weights_x(i, ratio):
    at = (i + 0.5) / ratio - 0.5
    low = math.floor(at)
    return low, 1.0 - (at - low), at - low


def filters(columns):
    row, column = iota((columns, columns), 0), iota((columns, columns), 1)
    near = jnp.abs(row - column)
    once = jnp.where(near == 0, CENTRE, jnp.where(near == 1, 1.0, 0.0)).astype(BF16)
    twice = dot_nn(once, once).astype(BF16)
    once = once + once
    return jnp.concatenate([twice, twice], axis=0), jnp.concatenate([once, once], axis=0)


def smooth(rows, wanted, coarse_rows, region, regions, twice, once):
    pairs = next(iter(rows.values())).shape[0]

    def both(values):
        high, lower = split(jnp.concatenate(values, axis=0))
        return jnp.concatenate([high, lower], axis=1)

    def total(*names):
        found = [rows[n] for n in names if n in rows]
        return functools.reduce(jnp.add, found) if found else None

    mids = [r for r in wanted if r in rows]
    at_mid = dot_nn(both([rows[r] for r in mids]), twice)
    sides = [r for r in wanted if total(r - 1, r + 1) is not None]
    at_side = dot_nn(both([total(r - 1, r + 1) for r in sides]), once)
    out = {}
    for r in wanted:
        terms = []
        if r in mids:
            k = mids.index(r)
            terms.append(at_mid[k * pairs : (k + 1) * pairs])
            around = 2.0
            if r == 0:
                around = jnp.where(region > 0, 2.0, 1.0)
            elif r == coarse_rows - 1:
                around = jnp.where(region < regions - 1, 2.0, 1.0)
            terms.append(around * rows[r])
        if r in sides:
            k = sides.index(r)
            terms.append(at_side[k * pairs : (k + 1) * pairs])
        far = total(r - 2, r + 2)
        if far is not None:
            terms.append(far)
        out[r] = (DIFFUSE * DIFFUSE) * functools.reduce(jnp.add, terms)
    return out


def mask_row(value, index, coarse_rows, region, regions):
    if index < 0:
        return jnp.where(region * coarse_rows + index >= 0, value, 0.0)
    if index >= coarse_rows:
        return jnp.where(region * coarse_rows + index < regions * coarse_rows, value, 0.0)
    return value


def decode(cell, rows, columns):
    plane = rows * columns
    level = cell // plane
    rest = cell - level * plane
    row = rest // columns
    return level, row, rest - row * columns


def weights_kernel(up_ref, down_ref, twice_ref, once_ref):
    coarse = twice_ref.shape[1]
    fine = up_ref.shape[1]
    up = table_y(coarse, fine, 0)
    up_ref[...] = jnp.concatenate([up, up], axis=0)
    down_ref[...] = table_y(coarse, fine, 1)
    twice_ref[...], once_ref[...] = filters(coarse)


def weights(coarse, fine):
    shapes = ((2 * coarse, fine), (fine, coarse), (2 * coarse, coarse), (2 * coarse, coarse))
    return pl.pallas_call(
        weights_kernel,
        out_shape=[jax.ShapeDtypeStruct(shape, BF16) for shape in shapes],
        compiler_params=params(16),
        cost_estimate=pl.CostEstimate(flops=1 << 33, bytes_accessed=1 << 24, transcendentals=0),
        name="weights",
    )()


def pack_kernel(
    pert_ref, cell_hbm, kind_hbm, flat_hbm,
    a_ref, b_ref, cell_ref, kind_ref, own_ref,
    flat_ref, sem,
):
    members, parts, levels, rows, columns = pert_ref.shape
    copies = []
    for n, (source, to) in enumerate(((cell_hbm, cell_ref), (kind_hbm, kind_ref), (flat_hbm, flat_ref))):
        copy = pltpu.make_async_copy(source, to, sem.at[n])
        copy.start()
        copies.append(copy)
    inner = levels * rows
    even = lax.rem(lax.axis_index("reg"), 2) == 0
    shape = (2 * levels, inner)
    pick = iota(shape, 0)
    to_a = pick < levels
    edge = jnp.where(to_a == even, rows - 1, 0)
    wanted = jnp.where(to_a, pick, pick - levels) * rows + edge
    chooser = jnp.where(iota(shape, 1) == wanted, 1.0, 0.0).astype(BF16)
    for m in range(members):
        for part in range(parts):
            got = dot_nn(chooser, pert_ref[m, part].reshape(inner, columns))
            a_ref[m, part] = got[:levels]
            b_ref[m, part] = got[levels:]
    for copy in copies:
        copy.wait()
    coarse_rows, pairs, _ = own_ref.shape
    for r in range(coarse_rows):
        own_ref[r] = flat_ref[pl.ds(r, pairs, stride=coarse_rows), :]


def pack(pert, cell, kind, flat, coarse_rows):
    members, parts, levels, _, columns = pert.shape
    shapes = [jax.ShapeDtypeStruct((members, parts, levels, columns), F32)] * 2
    shapes += [jax.ShapeDtypeStruct(cell.shape, cell.dtype)] * 2
    shapes.append(jax.ShapeDtypeStruct((coarse_rows, flat.shape[0] // coarse_rows, flat.shape[1]), F32))
    vmem = pl.BlockSpec(memory_space=pltpu.VMEM)
    hbm = pl.BlockSpec(memory_space=pltpu.HBM)
    cell, kind, flat = (pltpu.with_memory_space_constraint(x, pltpu.HBM) for x in (cell, kind, flat))
    return pl.pallas_call(
        pack_kernel,
        in_specs=[vmem, hbm, hbm, hbm],
        out_specs=[vmem] * len(shapes),
        out_shape=shapes,
        scratch_shapes=[pltpu.VMEM(flat.shape, flat.dtype), pltpu.SemaphoreType.DMA((3,))],
        compiler_params=params(16),
        name="pack_rows",
    )(pert, cell, kind, flat)


def tables_kernel(levels, rows, columns, cell_ref, kind_ref, r0_ref, ru_ref, rv_ref, c0_ref, cy_ref):
    cell, kind = cell_ref[...], kind_ref[...]
    level, row, column = decode(cell, rows, columns)
    line = level * rows + row
    count = cell.shape[1]
    inner = levels * rows
    minus = jnp.where(row > 0, line - 1, inner + level)
    plus = jnp.where(row < rows - 1, line + 1, inner + levels + level)
    none = jnp.full_like(line, -1)
    minus_u = jnp.where(kind == 3, minus, none)
    plus_u = jnp.where(kind == 3, plus, none)
    here_v = jnp.where((kind == 1) | (kind == 3), line, none)
    minus_v = jnp.where(kind == 2, minus, none)
    plus_v = jnp.where(kind == 2, plus, none)
    step = 32

    def lines(k, _):
        start = pl.multiple_of(k * step, step)
        at = iota((step, count), 0) + start
        ru = jnp.where(at == plus_u, 0.5, jnp.where(at == minus_u, -0.5, 0.0))
        rv = jnp.where(at == plus_v, 0.5, jnp.where(at == minus_v, -0.5, jnp.where(at == here_v, 1.0, 0.0)))
        r0 = jnp.where(at == line, 1.0, 0.0)
        ru_ref[pl.ds(start, step), :] = ru.astype(BF16)
        rv_ref[pl.ds(start, step), :] = rv.astype(BF16)
        r0_ref[pl.ds(start, step), :] = r0.astype(BF16)
        return 0

    lax.fori_loop(0, (inner + 2 * levels) // step, lines, 0)

    def cells(k, _):
        start = pl.multiple_of(k * step, step)
        at = iota((step, count), 0) + start
        c0_ref[pl.ds(start, step), :] = jnp.where(at == column, 1.0, 0.0).astype(BF16)
        cy = jnp.where(at == column + 1, 0.5, jnp.where(at == column - 1, -0.5, 0.0))
        cy_ref[pl.ds(start, step), :] = cy.astype(BF16)
        return 0

    lax.fori_loop(0, columns // step, cells, 0)


def tables(cell, kind, levels, rows, columns):
    count = cell.shape[1]
    lines = levels * rows + 2 * levels
    return pl.pallas_call(
        functools.partial(tables_kernel, levels, rows, columns),
        out_shape=[jax.ShapeDtypeStruct((n, count), BF16) for n in (lines, lines, lines, columns, columns)],
        compiler_params=params(16),
        name="one_hots",
    )(cell, kind)


def forward_kernel(
    scale, chunk,
    own_ref, even_ref, odd_ref, up_ref, twice_ref, once_ref, pert_ref, r0_ref, ru_ref, rv_ref, c0_ref, cy_ref,
    q_ref, edge_ref,
    fine_in, fine_scr, t_scr,
):
    region = lax.axis_index("reg")
    regions = lax.axis_size("reg")
    members, _, levels, rows, _ = pert_ref.shape
    coarse_rows, pairs, _ = own_ref.shape
    ratio = rows // coarse_rows
    block = chunk * rows
    inner = levels * rows
    even = lax.rem(region, 2) == 0
    table = up_ref[...]
    rows_in = {r: own_ref[r] for r in range(coarse_rows)}
    for k in range(HALO):
        low = coarse_rows - HALO + k
        e = even_ref[pl.ds(low, pairs, stride=coarse_rows), :]
        o = odd_ref[pl.ds(low, pairs, stride=coarse_rows), :]
        rows_in[k - HALO] = jnp.where(even, o, e)
        e = even_ref[pl.ds(k, pairs, stride=coarse_rows), :]
        o = odd_ref[pl.ds(k, pairs, stride=coarse_rows), :]
        rows_in[coarse_rows + k] = jnp.where(even, e, o)
    rows_in = smooth(
        rows_in, range(-1, coarse_rows + 1), coarse_rows, region, regions, twice_ref[...], once_ref[...]
    )
    rows_in = {r: mask_row(value, r, coarse_rows, region, regions) for r, value in rows_in.items()}
    for i in range(-1, rows + 1):
        low, w0, w1 = weights_x(i, ratio)
        value = (w0 * rows_in[low] + w1 * rows_in[low + 1]) * scale
        if 0 <= i < rows:
            fine_in[pl.ds(i, pairs, stride=rows), :] = value
        else:
            high, lower = split(value)
            got = dot_nn(jnp.concatenate([high, lower], axis=1), table)
            edge_ref[0 if i < 0 else 1] = got

    for step in range(levels // chunk):
        parts = []
        for m in range(members):
            parts.append(fine_in[pl.ds(m * inner + step * block, block), :])
        high, lower = split(jnp.concatenate(parts, axis=0))
        fine_scr[step % 2] = dot_nn(jnp.concatenate([high, lower], axis=1), table)
        for k in range(chunk):
            u = v = None
            for m in range(members):
                fine = fine_scr[step % 2, pl.ds(m * block + k * rows, rows), :]
                pu = fine * pert_ref[m, 0, step * chunk + k].astype(F32)
                pv = fine * pert_ref[m, 1, step * chunk + k].astype(F32)
                u = pu if u is None else u + pu
                v = pv if v is None else v + pv
            for n, value in enumerate((*split(u), *split(v))):
                t_scr[pl.ds(n * inner + step * block + k * rows, rows), :] = value

    count = r0_ref.shape[1]
    width = min(256, count)
    for k in range(count // width):
        at = pl.ds(k * width, width)
        z = dot_nn(t_scr[...], c0_ref[:, at])
        zy = dot_nn(t_scr[pl.ds(0, 2 * inner), :], cy_ref[:, at])
        zu = z[:inner] + z[inner : 2 * inner]
        zv = z[2 * inner : 3 * inner] + z[3 * inner :]
        zy = zy[:inner] + zy[inner:]
        inside = pl.ds(0, inner)
        r0 = r0_ref[inside, at].astype(F32)
        q_ref[pl.ds(0, 1), at] = jnp.sum(r0 * zu, axis=0, keepdims=True)
        q_ref[pl.ds(1, 1), at] = jnp.sum(rv_ref[inside, at].astype(F32) * zv, axis=0, keepdims=True)
        q_ref[pl.ds(2, 1), at] = jnp.sum(ru_ref[inside, at].astype(F32) * zu, axis=0, keepdims=True)
        q_ref[pl.ds(3, 1), at] = jnp.sum(r0 * zy, axis=0, keepdims=True)


def forward(own, got_even, got_odd, weight, pert, hot, scale):
    up, _, twice, once = weight
    members, _, levels, rows, columns = pert.shape
    _, pairs, coarse_columns = own.shape
    chunk = 4 if levels % 4 == 0 else 1
    count = hot[0].shape[1]
    return pl.pallas_call(
        functools.partial(forward_kernel, scale, chunk),
        out_shape=[jax.ShapeDtypeStruct((4, count), F32),
                   jax.ShapeDtypeStruct((2, pairs, columns), F32)],
        scratch_shapes=[
            pltpu.VMEM((pairs * rows, coarse_columns), F32),
            pltpu.VMEM((2, members * chunk * rows, columns), F32),
            pltpu.VMEM((4 * levels * rows, columns), BF16),
        ],
        compiler_params=params(28),
        name="increment_at_obs",
    )(own, got_even, got_odd, up, twice, once, pert, *hot)


def edge_kernel(members, levels, q_ref, fine_ref, even_ref, odd_ref, ru_ref, rv_ref, c0_ref, out_ref):
    even = lax.rem(lax.axis_index("reg"), 2) == 0
    table = []
    for part in range(2):
        for side in range(2):
            total = None
            for m in range(members):
                e, o = even_ref[m, part], odd_ref[m, part]
                halo = jnp.where(even, o, e) if side == 0 else jnp.where(even, e, o)
                term = fine_ref[side, pl.ds(m * levels, levels), :] * halo
                total = term if total is None else total + term
            table.append(total)
    high, lower = split(jnp.concatenate(table, axis=0))
    z = dot_nn(jnp.concatenate([high, lower], axis=0), c0_ref[...])
    tail = 2 * levels
    z = z[: 2 * tail] + z[2 * tail :]
    rim = pl.ds(ru_ref.shape[0] - tail, tail)
    in_u = jnp.sum(ru_ref[rim, :].astype(F32) * z[:tail], axis=0, keepdims=True)
    in_v = jnp.sum(rv_ref[rim, :].astype(F32) * z[tail:], axis=0, keepdims=True)
    out_ref[pl.ds(0, 1), :] = q_ref[pl.ds(0, 1), :]
    out_ref[pl.ds(1, 1), :] = q_ref[pl.ds(1, 1), :] + in_v
    out_ref[pl.ds(2, 1), :] = q_ref[pl.ds(2, 1), :] + in_u
    out_ref[pl.ds(3, 1), :] = q_ref[pl.ds(3, 1), :]


def edge(q, fine, halo_even, halo_odd, hot, members, levels):
    _, ru, rv, c0, _ = hot
    return pl.pallas_call(
        functools.partial(edge_kernel, members, levels),
        out_shape=jax.ShapeDtypeStruct(q.shape, F32),
        compiler_params=params(16),
        name="edge_at_obs",
    )(q, fine, halo_even, halo_odd, ru, rv, c0)


def backward_kernel(scale, chunk, terms, *refs):
    q_refs = refs[:terms]
    (kind_ref, value_ref, weight_ref, down_ref, twice_ref, once_ref, pert_ref, even_ref, odd_ref,
     r0_ref, ru_ref, rv_ref, c0_ref, cy_ref,
     own_out, a_out, b_out,
     u_scr, v_scr, f_scr) = refs[terms:]
    region = lax.axis_index("reg")
    regions = lax.axis_size("reg")
    members, _, levels, rows, _ = pert_ref.shape
    coarse_rows, pairs, _ = own_out.shape
    ratio = rows // coarse_rows
    inner = levels * rows
    even = lax.rem(region, 2) == 0
    table = down_ref[...]

    q = q_refs[0][...]
    for ref in q_refs[1:]:
        q = q + ref[...]
    q0, q1, q2, q3 = (q[n : n + 1] for n in range(4))
    kind = kind_ref[...]
    seen = jnp.where(kind == 0, q0, jnp.where(kind == 1, q1, jnp.where(kind == 2, q1 - q3, q0 * q2 + q1 * q3)))
    misfit = weight_ref[...] * (seen - value_ref[...])
    zero = jnp.zeros_like(misfit)
    a = jnp.where(kind == 0, misfit, jnp.where(kind == 3, misfit * q2, zero))
    b = jnp.where(kind == 2, -misfit, jnp.where(kind == 3, misfit * q1, zero))
    c = jnp.where(kind == 3, misfit * q0, zero)
    g = jnp.where(kind == 3, misfit * q3, jnp.where(kind == 0, zero, misfit))
    r0, ru, rv = r0_ref[...], ru_ref[...], rv_ref[...]
    lines = r0.shape[0]
    left = [r0 * x + ru * y for x, y in zip(split(a), split(c))] + [rv * x for x in split(g)]
    both = dot_nt(jnp.concatenate(left, axis=0), c0_ref[...])
    left = [r0[:inner] * x for x in split(b)]
    along = dot_nt(jnp.concatenate(left, axis=0), cy_ref[...])
    total = both[:lines] + both[lines : 2 * lines]
    u_scr[pl.ds(0, inner), :] = total[:inner] + (along[:inner] + along[inner:])
    u_scr[pl.ds(inner, lines - inner), :] = total[inner:]
    v_scr[...] = both[2 * lines : 3 * lines] + both[3 * lines :]

    block = chunk * rows
    for s in range(levels // chunk):
        product = []
        for m in range(members):
            for n in range(chunk):
                k = s * chunk + n
                u = u_scr[pl.ds(k * rows, rows), :]
                v = v_scr[pl.ds(k * rows, rows), :]
                product.append(u * pert_ref[m, 0, k].astype(F32) + v * pert_ref[m, 1, k].astype(F32))
        high, lower = split(jnp.concatenate(product, axis=0))
        got = dot_nn(high, table) + dot_nn(lower, table)
        for m in range(members):
            f_scr[pl.ds(m * inner + s * block, block), :] = got[m * block : (m + 1) * block]

    out = {}

    def add(i, value):
        low, w0, w1 = weights_x(i, ratio)
        for at, w in ((low, w0), (low + 1, w1)):
            out[at] = w * value if at not in out else out[at] + w * value

    for side in range(2):
        u = u_scr[pl.ds(inner + side * levels, levels), :]
        v = v_scr[pl.ds(inner + side * levels, levels), :]
        product = []
        for m in range(members):
            halo = []
            for part in range(2):
                e, o = even_ref[m, part], odd_ref[m, part]
                halo.append(jnp.where(even, o, e) if side == 0 else jnp.where(even, e, o))
            product.append(u * halo[0] + v * halo[1])
        high, lower = split(jnp.concatenate(product, axis=0))
        got = dot_nn(high, table) + dot_nn(lower, table)
        add(-1 if side == 0 else rows, got)
    for i in range(rows):
        add(i, f_scr[pl.ds(i, pairs, stride=rows), :])
    held = {r: mask_row(value * scale, r, coarse_rows, region, regions) for r, value in out.items()}
    held = smooth(
        held, range(-HALO, coarse_rows + HALO), coarse_rows, region, regions, twice_ref[...], once_ref[...]
    )
    for r in range(coarse_rows):
        own_out[r] = held[r]
    for k in range(HALO):
        before, after = held[k - HALO], held[coarse_rows + k]
        a_out[k] = jnp.where(even, after, before)
        b_out[k] = jnp.where(even, before, after)


def backward(q_terms, kind, value, weight, tables_y, pert, halo_even, halo_odd, hot, scale, coarse_rows, coarse_columns):
    members, _, levels, rows, columns = pert.shape
    pairs = members * levels
    chunk = 4 if levels % 4 == 0 else 1
    outs = [jax.ShapeDtypeStruct((n, pairs, coarse_columns), F32) for n in (coarse_rows, HALO, HALO)]
    return pl.pallas_call(
        functools.partial(backward_kernel, scale, chunk, len(q_terms)),
        out_shape=outs,
        scratch_shapes=[
            pltpu.VMEM((levels * rows + 2 * levels, columns), F32),
            pltpu.VMEM((levels * rows + 2 * levels, columns), F32),
            pltpu.VMEM((pairs * rows, coarse_columns), F32),
        ],
        compiler_params=params(28),
        name="adjoint_to_coarse",
    )(*q_terms, kind, value, weight, *tables_y[1:], pert, halo_even, halo_odd, *hot)


def join_kernel(coarse_rows, own_ref, even_ref, odd_ref, out_ref):
    even = lax.rem(lax.axis_index("reg"), 2) == 0
    pairs = own_ref.shape[1]
    for r in range(coarse_rows):
        total = own_ref[r]
        if r < HALO:
            total = total + jnp.where(even, odd_ref[r], even_ref[r])
        k = r - (coarse_rows - HALO)
        if k >= 0:
            total = total + jnp.where(even, even_ref[k], odd_ref[k])
        out_ref[pl.ds(r, pairs, stride=coarse_rows), :] = total


def join(own, got_even, got_odd):
    coarse_rows, pairs, columns = own.shape
    return pl.pallas_call(
        functools.partial(join_kernel, coarse_rows),
        out_shape=jax.ShapeDtypeStruct((pairs * coarse_rows, columns), F32),
        compiler_params=params(16),
        name="join_rows",
    )(own, got_even, got_odd)


def local(alpha, perturbation, obs_cell, obs_kind, obs_value, obs_weight):
    members, levels, coarse_rows, coarse_columns = alpha.shape
    _, _, _, rows, columns = perturbation.shape
    scale = 1.0 / math.sqrt(members * lax.axis_size("mem"))
    flat = alpha.reshape(-1, coarse_columns)
    cell, kind, value, weight = (x.reshape(1, -1) for x in (obs_cell, obs_kind, obs_value, obs_weight))
    along_y = weights(coarse_columns, columns)
    flat_odd = swap_odd(flat)
    flat_even = swap_even(flat)
    pack_a, pack_b, cell, kind, own = pack(perturbation, cell, kind, flat, coarse_rows)
    halo_odd = swap_odd(pack_b)
    halo_even = swap_even(pack_a)
    hot = tables(cell, kind, levels, rows, columns)
    q, edge_fine = forward(own, flat_even, flat_odd, along_y, perturbation, hot, scale)
    q = edge(q, edge_fine, halo_even, halo_odd, hot, members, levels)
    terms = others(q, "mem")
    own, send_a, send_b = backward(
        terms, kind, value, weight, along_y, perturbation, halo_even, halo_odd, hot, scale,
        coarse_rows, coarse_columns,
    )
    got_odd = swap_odd(send_b)
    got_even = swap_even(send_a)
    return join(own, got_even, got_odd).reshape(alpha.shape)


def solution(mesh):
    return jax.shard_map(
        local,
        mesh=mesh,
        in_specs=(
            P("mem", None, "reg", None),
            P("mem", None, None, "reg", None),
            P("reg"),
            P("reg"),
            P("reg"),
            P("reg"),
        ),
        out_specs=P("mem", None, "reg", None),
        check_vma=False,
    )
```

time: 46.4 us -> 38.2 us (0.82)
  Pallas kernels: 18 us -> 11.6 us
  waiting for transfers between devices: 13.4 us -> 7.94 us
  local copies, waits for them, and re-layouts: 0.01 us -> 2.2 us
  starting transfers between devices: 14.7 us -> 16.1 us
    ppermute x3, waiting for transfers between devices: 11 us -> 5.6 us  [swap_odd(): return lax.ppermute(value, 'reg', swap_pairs(lax.axis_size('reg'), True))]
    unnamed x8, local copies, waits for them, and re-layouts: 0.01 us -> 2.2 us
    pallas_call x1, Pallas kernels: 5.77 us -> 3.67 us  [forward(): pl.pallas_call(functools.partial(forward_kernel, scale, chunk), out_shape...]
    pallas_call x1 -> x3, Pallas kernels: 4.6 us -> 2.51 us  [the longest x1 1.2 us: tables(): pl.pallas_call(functools.partial(tables_kernel, levels, rows, columns), o...]
    pallas_call x1, Pallas kernels: 6.07 us -> 4.24 us  [backward(): pl.pallas_call(functools.partial(backward_kernel, scale, chunk, len(q_ter...]
    ppermute x3, starting transfers between devices: 11.3 us -> 12.7 us  [swap_odd(): return lax.ppermute(value, 'reg', swap_pairs(lax.axis_size('reg'), True))]
    ppermute x3, starting transfers between devices: 0.22 us -> 0.7 us  [swap_even(): return lax.ppermute(value, 'reg', swap_pairs(lax.axis_size('reg'), False))]
  transfers between devices with their start and end apart: 9 -> 9, of which waited for: 5 -> 5; matrix products, arithmetic and copies ran while one was open for 0% -> 0% of each run, Pallas kernels for 12% -> 16%
where the time goes in v3:
time: 38.2 us; the launch traced here: 38 us
  starting transfers between devices  16.1 us (42%)
  Pallas kernels  11.6 us (30%)
  waiting for transfers between devices  7.94 us (21%)
  local copies, waits for them, and re-layouts  2.2 us (6%)
    ppermute x3, starting transfers between devices, swap_odd(): return lax.ppermute(value, 'reg', swap_pairs(lax.axis_size('reg'), True))  12.7 us
    ppermute x3, waiting for transfers between devices, swap_odd(): return lax.ppermute(value, 'reg', swap_pairs(lax.axis_size('reg'), True))  5.6 us
    pallas_call x1, Pallas kernels, backward(): pl.pallas_call(functools.partial(backward_kernel, scale, chunk, len(q_ter...  4.24 us
    pallas_call x1, Pallas kernels, forward(): pl.pallas_call(functools.partial(forward_kernel, scale, chunk), out_shape...  3.67 us
    ppermute x3, starting transfers between devices, others(): got = [lax.ppermute(value, axis, pairs) for pairs in sends]  2.71 us
    ppermute x3, waiting for transfers between devices, others(): got = [lax.ppermute(value, axis, pairs) for pairs in sends]  2.33 us
    unnamed x8, local copies, waits for them, and re-layouts  2.2 us
    pallas_call x1, Pallas kernels, tables(): pl.pallas_call(functools.partial(tables_kernel, levels, rows, columns), o...  1.2 us
  transfers between devices with their start and end apart: 9, of which 5 were waited for; matrix products, arithmetic and copies ran while one was open for 0% of the time, Pallas kernels for 16%

profile of v3, /device:TPU:1, one launch (start us, length us, event | category | flops | bytes accessed | tf_op | source)
XLA Modules:
  0.0 38.0 jit_solution(13381300405491077295)
XLA Ops:
  0.0 4.6 %collective-permute-start.1 = (f32[512,128]{1,0:T(8,128)}, f32[512,128]{1,0:T(8,128)S(1)}, u32[]{:S(2)}, u32[]{:S(2)}) collective-permute-start(f32[512,128]{1,0:T(8,128)} %bitcast.8), channel_id=1, source_target_pairs={{1,2},{2,1},{3,4},{4,3},{5,6},{6,5},{9,10},{10,9},{11,12},{12,11},... | collective-permute-start | bytes 786440 | tf_op jit(solution)/shard_map/ppermute | solution.py:36
  4.6 0.1 collective-permute-start
  4.7 0.0 copy-start
  4.7 2.2 %copy-done = bf16[8,2,16,16,512]{4,3,2,1,0:T(8,128)(2,1)S(1)} copy-done((bf16[8,2,16,16,512]{4,3,2,1,0:T(8,128)(2,1)S(1)}, bf16[8,2,16,16,512]{4,3,2,1,0:T(8,128)(2,1)}, u32[]{:S(2)}) %copy-start) | copy-done | bytes 4194328
  6.8 1.0 %pack_rows.1 = (f32[8,2,16,512]{3,2,1,0:T(8,128)S(1)}, f32[8,2,16,512]{3,2,1,0:T(8,128)S(1)}, s32[1,1024]{1,0:T(1,128)S(1)}, s32[1,1024]{1,0:T(1,128)S(1)}, f32[4,128,128]{2,1,0:T(8,128)S(1)}) custom-call(bf16[8,2,16,16,512]{4,3,2,1,0:T(8,128)(2,1)S(1)} %copy-done, s32[1,1024]{1,0:T(1,128)} %bitcast.11, s32[1,1024]{1,0:T(1,128)} %bitcast.12, f32[512,128]{1,0:T(8,128)} %bitcast.10), custom_call_target="tpu_custom_call" | custom-call | tf_op jit(solution)/shard_map/pack_rows/pallas_call | solution.py:216
  7.9 0.6 %collective-permute-start.2 = (f32[8,2,16,512]{3,2,1,0:T(8,128)S(1)}, f32[8,2,16,512]{3,2,1,0:T(8,128)S(1)}, u32[]{:S(2)}, u32[]{:S(2)}) collective-permute-start(f32[8,2,16,512]{3,2,1,0:T(8,128)S(1)} %get-tuple-element.37), channel_id=1, source_target_pairs={{0,1},{1,0},{2,3},{3,2},{4,5},{5,4},{6,7},{7,6},{8,9},{9,8},{10,11... | collective-permute-start | bytes 1572872 | tf_op jit(solution)/shard_map/ppermute | solution.py:32
  8.5 0.0 copy-start.1
  8.5 3.4 %collective-permute-start.3 = (f32[8,2,16,512]{3,2,1,0:T(8,128)S(1)}, f32[8,2,16,512]{3,2,1,0:T(8,128)S(1)}, u32[]{:S(2)}, u32[]{:S(2)}) collective-permute-start(f32[8,2,16,512]{3,2,1,0:T(8,128)S(1)} %get-tuple-element.38), channel_id=1, source_target_pairs={{1,2},{2,1},{3,4},{4,3},{5,6},{6,5},{9,10},{10,9},{11,12},{12,11},... | collective-permute-start | bytes 1572872 | tf_op jit(solution)/shard_map/ppermute | solution.py:36
  11.8 0.3 weights.1
  12.1 1.2 %one_hots.1 = (bf16[288,1024]{1,0:T(8,128)(2,1)S(1)}, bf16[288,1024]{1,0:T(8,128)(2,1)S(1)}, bf16[288,1024]{1,0:T(8,128)(2,1)S(1)}, bf16[512,1024]{1,0:T(8,128)(2,1)S(1)}, bf16[512,1024]{1,0:T(8,128)(2,1)S(1)}) custom-call(s32[1,1024]{1,0:T(1,128)S(1)} %get-tuple-element.28.cell_ref, s32[1,1024]{1,0:T(1,128)S(1)} %get-tuple-element.29.kind_ref.refs_4_), custom_call_target="tpu_custom_call" | custom-call | tf_op jit(solution)/shard_map/one_hots/pallas_call | solution.py:270
  13.3 0.0 collective-permute-done.1.odd_ref
  13.3 0.0 collective-permute-done.even_ref
  13.3 0.0 copy-done.1
  13.4 0.0 copy-start.2
  13.4 0.0 copy-start.3
  13.4 3.7 %increment_at_obs.1 = (f32[4,1024]{1,0:T(4,128)S(1)}, f32[2,128,512]{2,1,0:T(8,128)S(1)}) custom-call(f32[4,128,128]{2,1,0:T(8,128)S(1)} %get-tuple-element.24.own_ref, f32[512,128]{1,0:T(8,128)S(1)} %collective-permute-done.even_ref, f32[512,128]{1,0:T(8,128)S(1)} %collective-permute-done.1.odd_ref, bf16[256,512]{1,0:T(8,128)(2,1)S(1)} %get-tuple-element.25.up_ref, ...), custom_call_target="tpu_custom_call" | custom-call | tf_op jit(solution)/shard_map/increment_at_obs/pallas_call | solution.py:356
  17.1 0.0 collective-permute-done.2.even_ref.refs_11_
  17.1 2.3 %collective-permute-done.3.odd_ref.refs_12_ = f32[8,2,16,512]{3,2,1,0:T(8,128)S(1)} collective-permute-done((f32[8,2,16,512]{3,2,1,0:T(8,128)S(1)}, f32[8,2,16,512]{3,2,1,0:T(8,128)S(1)}, u32[]{:S(2)}, u32[]{:S(2)}) %collective-permute-start.3) | collective-permute-done | bytes 524320 | tf_op jit(solution)/shard_map/ppermute | solution.py:36
  19.3 0.5 %edge_at_obs.1.refs_0_ = f32[4,1024]{1,0:T(4,128)S(1)} custom-call(f32[4,1024]{1,0:T(4,128)S(1)} %get-tuple-element.35.q_ref, f32[2,128,512]{2,1,0:T(8,128)S(1)} %get-tuple-element.36.fine_ref, f32[8,2,16,512]{3,2,1,0:T(8,128)S(1)} %collective-permute-done.2.even_ref.refs_11_, f32[8,2,16,512]{3,2,1,0:T(8,128)S(1)} %collective-permute-done.3.odd_ref.refs_12_, ...), custom_call_target="tpu_custom_call" | custom-call | tf_op jit(solution)/shard_map/edge_at_obs/pallas_call | solution.py:397
  19.8 2.2 %collective-permute-start.6 = (f32[4,1024]{1,0:T(4,128)S(1)}, f32[4,1024]{1,0:T(4,128)S(1)}, u32[]{:S(2)}, u32[]{:S(2)}) collective-permute-start(f32[4,1024]{1,0:T(4,128)S(1)} %edge_at_obs.1.refs_0_), channel_id=1, source_target_pairs={{0,24},{8,16},{16,8},{24,0},{1,25},{9,17},{17,9},{25,1},{2,26},{10... | collective-permute-start | bytes 49160 | tf_op jit(solution)/shard_map/ppermute | solution.py:57
  22.0 0.2 collective-permute-start.5
  22.3 0.3 collective-permute-start.4
  22.5 0.8 %collective-permute-done.6.refs_3_ = f32[4,1024]{1,0:T(4,128)S(1)} collective-permute-done((f32[4,1024]{1,0:T(4,128)S(1)}, f32[4,1024]{1,0:T(4,128)S(1)}, u32[]{:S(2)}, u32[]{:S(2)}) %collective-permute-start.6) | collective-permute-done | bytes 16416 | tf_op jit(solution)/shard_map/ppermute | solution.py:57
  23.4 1.3 %collective-permute-done.5.refs_2_ = f32[4,1024]{1,0:T(4,128)S(1)} collective-permute-done((f32[4,1024]{1,0:T(4,128)S(1)}, f32[4,1024]{1,0:T(4,128)S(1)}, u32[]{:S(2)}, u32[]{:S(2)}) %collective-permute-start.5) | collective-permute-done | bytes 16416 | tf_op jit(solution)/shard_map/ppermute | solution.py:57
  24.6 0.2 collective-permute-done.4.refs_1_
  24.9 0.0 copy-done.2
  24.9 0.0 copy-done.3
  24.9 4.2 %adjoint_to_coarse.1 = (f32[4,128,128]{2,1,0:T(8,128)S(1)}, f32[3,128,128]{2,1,0:T(8,128)S(1)}, f32[3,128,128]{2,1,0:T(8,128)S(1)}) custom-call(f32[4,1024]{1,0:T(4,128)S(1)} %edge_at_obs.1.refs_0_, f32[4,1024]{1,0:T(4,128)S(1)} %collective-permute-done.4.refs_1_, f32[4,1024]{1,0:T(4,128)S(1)} %collective-permute-done.5.refs_2_, ...), custom_call_target="tpu_custom_call" | custom-call | tf_op jit(solution)/shard_map/adjoint_to_coarse/pallas_call | solution.py:496
  29.1 0.1 collective-permute-start.7
  29.2 4.7 %collective-permute-start.8 = (f32[3,128,128]{2,1,0:T(8,128)S(1)}, f32[3,128,128]{2,1,0:T(8,128)S(1)}, u32[]{:S(2)}, u32[]{:S(2)}) collective-permute-start(f32[3,128,128]{2,1,0:T(8,128)S(1)} %get-tuple-element.42), channel_id=1, source_target_pairs={{1,2},{2,1},{3,4},{4,3},{5,6},{6,5},{9,10},{10,9},{11,12},{12,11},... | collective-permute-start | bytes 589832 | tf_op jit(solution)/shard_map/ppermute | solution.py:36
  33.9 0.0 collective-permute-done.7.even_ref
  33.9 3.3 %collective-permute-done.8.odd_ref = f32[3,128,128]{2,1,0:T(8,128)S(1)} collective-permute-done((f32[3,128,128]{2,1,0:T(8,128)S(1)}, f32[3,128,128]{2,1,0:T(8,128)S(1)}, u32[]{:S(2)}, u32[]{:S(2)}) %collective-permute-start.8) | collective-permute-done | bytes 196640 | tf_op jit(solution)/shard_map/ppermute | solution.py:36
  37.2 0.8 %join_rows.1 = f32[512,128]{1,0:T(8,128)} custom-call(f32[4,128,128]{2,1,0:T(8,128)S(1)} %get-tuple-element.40.own_ref, f32[3,128,128]{2,1,0:T(8,128)S(1)} %collective-permute-done.7.even_ref, f32[3,128,128]{2,1,0:T(8,128)S(1)} %collective-permute-done.8.odd_ref), custom_call_target="tpu_custom_call" | custom-call | tf_op jit(solution)/shard_map/join_rows/pallas_call | solution.py:524
Async XLA Ops:
  0.0 13.3 %collective-permute-start.1 = (f32[512,128]{1,0:T(8,128)}, f32[512,128]{1,0:T(8,128)S(1)}, u32[]{:S(2)}, u32[]{:S(2)}) collective-permute-start(f32[512,128]{1,0:T(8,128)} %bitcast.8), channel_id=1, source_target_pairs={{1,2},{2,1},{3,4},{4,3},{5,6},{6,5},{9,10},{10,9},{11,12},{12,11},... | collective-permute-start | bytes 786440 | tf_op jit(solution)/shard_map/ppermute | solution.py:36
  4.6 8.8 %collective-permute-start = (f32[512,128]{1,0:T(8,128)}, f32[512,128]{1,0:T(8,128)S(1)}, u32[]{:S(2)}, u32[]{:S(2)}) collective-permute-start(f32[512,128]{1,0:T(8,128)} %bitcast.9), channel_id=1, source_target_pairs={{0,1},{1,0},{2,3},{3,2},{4,5},{5,4},{6,7},{7,6},{8,9},{9,8},{10,11... | collective-permute-start | bytes 786440 | tf_op jit(solution)/shard_map/ppermute | solution.py:32
  4.7 2.2 %copy-start = (bf16[8,2,16,16,512]{4,3,2,1,0:T(8,128)(2,1)S(1)}, bf16[8,2,16,16,512]{4,3,2,1,0:T(8,128)(2,1)}, u32[]{:S(2)}) copy-start(bf16[8,2,16,16,512]{4,3,2,1,0:T(8,128)(2,1)} %refs_10_.1) | copy-start | bytes 12582916
  7.9 9.2 %collective-permute-start.2 = (f32[8,2,16,512]{3,2,1,0:T(8,128)S(1)}, f32[8,2,16,512]{3,2,1,0:T(8,128)S(1)}, u32[]{:S(2)}, u32[]{:S(2)}) collective-permute-start(f32[8,2,16,512]{3,2,1,0:T(8,128)S(1)} %get-tuple-element.37), channel_id=1, source_target_pairs={{0,1},{1,0},{2,3},{3,2},{4,5},{5,4},{6,7},{7,6},{8,9},{9,8},{10,11... | collective-permute-start | bytes 1572872 | tf_op jit(solution)/shard_map/ppermute | solution.py:32
  8.5 4.9 %copy-start.1 = (bf16[8,2,16,16,512]{4,3,2,1,0:T(8,128)(2,1)S(1)}, bf16[8,2,16,16,512]{4,3,2,1,0:T(8,128)(2,1)}, u32[]{:S(2)}) copy-start(bf16[8,2,16,16,512]{4,3,2,1,0:T(8,128)(2,1)} %refs_10_.1) | copy-start | bytes 12582916
  8.5 10.9 %collective-permute-start.3 = (f32[8,2,16,512]{3,2,1,0:T(8,128)S(1)}, f32[8,2,16,512]{3,2,1,0:T(8,128)S(1)}, u32[]{:S(2)}, u32[]{:S(2)}) collective-permute-start(f32[8,2,16,512]{3,2,1,0:T(8,128)S(1)} %get-tuple-element.38), channel_id=1, source_target_pairs={{1,2},{2,1},{3,4},{4,3},{5,6},{6,5},{9,10},{10,9},{11,12},{12,11},... | collective-permute-start | bytes 1572872 | tf_op jit(solution)/shard_map/ppermute | solution.py:36
  13.4 11.5 %copy-start.2 = (f32[1024]{0:T(1024)S(1)}, f32[1024]{0:T(1024)}, u32[]{:S(2)}) copy-start(f32[1024]{0:T(1024)} %param.10) | copy-start | bytes 12292
  13.4 11.5 %copy-start.3 = (f32[1024]{0:T(1024)S(1)}, f32[1024]{0:T(1024)}, u32[]{:S(2)}) copy-start(f32[1024]{0:T(1024)} %param.11) | copy-start | bytes 12292
  19.8 3.6 %collective-permute-start.6 = (f32[4,1024]{1,0:T(4,128)S(1)}, f32[4,1024]{1,0:T(4,128)S(1)}, u32[]{:S(2)}, u32[]{:S(2)}) collective-permute-start(f32[4,1024]{1,0:T(4,128)S(1)} %edge_at_obs.1.refs_0_), channel_id=1, source_target_pairs={{0,24},{8,16},{16,8},{24,0},{1,25},{9,17},{17,9},{25,1},{2,26},{10... | collective-permute-start | bytes 49160 | tf_op jit(solution)/shard_map/ppermute | solution.py:57
  22.0 2.6 %collective-permute-start.5 = (f32[4,1024]{1,0:T(4,128)S(1)}, f32[4,1024]{1,0:T(4,128)S(1)}, u32[]{:S(2)}, u32[]{:S(2)}) collective-permute-start(f32[4,1024]{1,0:T(4,128)S(1)} %edge_at_obs.1.refs_0_), channel_id=1, source_target_pairs={{0,16},{8,24},{16,0},{24,8},{1,17},{9,25},{17,1},{25,9},{2,18},{10... | collective-permute-start | bytes 49160 | tf_op jit(solution)/shard_map/ppermute | solution.py:57
  22.3 2.6 %collective-permute-start.4 = (f32[4,1024]{1,0:T(4,128)S(1)}, f32[4,1024]{1,0:T(4,128)S(1)}, u32[]{:S(2)}, u32[]{:S(2)}) collective-permute-start(f32[4,1024]{1,0:T(4,128)S(1)} %edge_at_obs.1.refs_0_), channel_id=1, source_target_pairs={{0,8},{8,0},{16,24},{24,16},{1,9},{9,1},{17,25},{25,17},{2,10},{10... | collective-permute-start | bytes 49160 | tf_op jit(solution)/shard_map/ppermute | solution.py:57
  29.1 4.8 %collective-permute-start.7 = (f32[3,128,128]{2,1,0:T(8,128)S(1)}, f32[3,128,128]{2,1,0:T(8,128)S(1)}, u32[]{:S(2)}, u32[]{:S(2)}) collective-permute-start(f32[3,128,128]{2,1,0:T(8,128)S(1)} %get-tuple-element.41), channel_id=1, source_target_pairs={{0,1},{1,0},{2,3},{3,2},{4,5},{5,4},{6,7},{7,6},{8,9},{9,8},{10,11... | collective-permute-start | bytes 589832 | tf_op jit(solution)/shard_map/ppermute | solution.py:32
  29.2 8.1 %collective-permute-start.8 = (f32[3,128,128]{2,1,0:T(8,128)S(1)}, f32[3,128,128]{2,1,0:T(8,128)S(1)}, u32[]{:S(2)}, u32[]{:S(2)}) collective-permute-start(f32[3,128,128]{2,1,0:T(8,128)S(1)} %get-tuple-element.42), channel_id=1, source_target_pairs={{1,2},{2,1},{3,4},{4,3},{5,6},{6,5},{9,10},{10,9},{11,12},{12,11},... | collective-permute-start | bytes 589832 | tf_op jit(solution)/shard_map/ppermute | solution.py:36

commit v4 on v3

--- a/solution.py
+++ b/solution.py
@@ -54,7 +54,9 @@
         rounds.append(sends)
         stride *= radix
     for number, sends in enumerate(rounds):
-        got = [lax.ppermute(value, axis, pairs) for pairs in sends]
+        got = []
+        for pairs in sends:
+            got.append(lax.ppermute(value, axis, pairs))
         if number == len(rounds) - 1:
             return [value] + got
         for part in got:
@@ -154,37 +156,23 @@
     return level, row, rest - row * columns
 
 
-def weights_kernel(up_ref, down_ref, twice_ref, once_ref):
-    coarse = twice_ref.shape[1]
-    fine = up_ref.shape[1]
-    up = table_y(coarse, fine, 0)
-    up_ref[...] = jnp.concatenate([up, up], axis=0)
+def down_kernel(down_ref):
+    fine, coarse = down_ref.shape
     down_ref[...] = table_y(coarse, fine, 1)
-    twice_ref[...], once_ref[...] = filters(coarse)
-
-
-def weights(coarse, fine):
-    shapes = ((2 * coarse, fine), (fine, coarse), (2 * coarse, coarse), (2 * coarse, coarse))
+
+
+def down_weights(coarse, fine):
     return pl.pallas_call(
-        weights_kernel,
-        out_shape=[jax.ShapeDtypeStruct(shape, BF16) for shape in shapes],
+        down_kernel,
+        out_shape=jax.ShapeDtypeStruct((fine, coarse), BF16),
         compiler_params=params(16),
-        cost_estimate=pl.CostEstimate(flops=1 << 33, bytes_accessed=1 << 24, transcendentals=0),
-        name="weights",
+        cost_estimate=pl.CostEstimate(flops=1160000000, bytes_accessed=1 << 20, transcendentals=0),
+        name="down_weights",
     )()
 
 
-def pack_kernel(
-    pert_ref, cell_hbm, kind_hbm, flat_hbm,
-    a_ref, b_ref, cell_ref, kind_ref, own_ref,
-    flat_ref, sem,
-):
+def pack_kernel(pert_ref, a_ref, b_ref):
     members, parts, levels, rows, columns = pert_ref.shape
-    copies = []
-    for n, (source, to) in enumerate(((cell_hbm, cell_ref), (kind_hbm, kind_ref), (flat_hbm, flat_ref))):
-        copy = pltpu.make_async_copy(source, to, sem.at[n])
-        copy.start()
-        copies.append(copy)
     inner = levels * rows
     even = lax.rem(lax.axis_index("reg"), 2) == 0
     shape = (2 * levels, inner)
@@ -198,33 +186,26 @@
             got = dot_nn(chooser, pert_ref[m, part].reshape(inner, columns))
             a_ref[m, part] = got[:levels]
             b_ref[m, part] = got[levels:]
-    for copy in copies:
-        copy.wait()
-    coarse_rows, pairs, _ = own_ref.shape
-    for r in range(coarse_rows):
-        own_ref[r] = flat_ref[pl.ds(r, pairs, stride=coarse_rows), :]
-
-
-def pack(pert, cell, kind, flat, coarse_rows):
+
+
+def pack(pert):
     members, parts, levels, _, columns = pert.shape
-    shapes = [jax.ShapeDtypeStruct((members, parts, levels, columns), F32)] * 2
-    shapes += [jax.ShapeDtypeStruct(cell.shape, cell.dtype)] * 2
-    shapes.append(jax.ShapeDtypeStruct((coarse_rows, flat.shape[0] // coarse_rows, flat.shape[1]), F32))
-    vmem = pl.BlockSpec(memory_space=pltpu.VMEM)
-    hbm = pl.BlockSpec(memory_space=pltpu.HBM)
-    cell, kind, flat = (pltpu.with_memory_space_constraint(x, pltpu.HBM) for x in (cell, kind, flat))
+    out = jax.ShapeDtypeStruct((members, parts, levels, columns), F32)
     return pl.pallas_call(
         pack_kernel,
-        in_specs=[vmem, hbm, hbm, hbm],
-        out_specs=[vmem] * len(shapes),
-        out_shape=shapes,
-        scratch_shapes=[pltpu.VMEM(flat.shape, flat.dtype), pltpu.SemaphoreType.DMA((3,))],
+        out_shape=[out, out],
         compiler_params=params(16),
         name="pack_rows",
-    )(pert, cell, kind, flat)
-
-
-def tables_kernel(levels, rows, columns, cell_ref, kind_ref, r0_ref, ru_ref, rv_ref, c0_ref, cy_ref):
+    )(pert)
+
+
+def tables_kernel(
+    levels, rows, columns, cell_ref, kind_ref, r0_ref, ru_ref, rv_ref, c0_ref, cy_ref, up_ref, twice_ref, once_ref
+):
+    coarse = twice_ref.shape[1]
+    up = table_y(coarse, columns, 0)
+    up_ref[...] = jnp.concatenate([up, up], axis=0)
+    twice_ref[...], once_ref[...] = filters(coarse)
     cell, kind = cell_ref[...], kind_ref[...]
     level, row, column = decode(cell, rows, columns)
     line = level * rows + row
@@ -264,15 +245,18 @@
     lax.fori_loop(0, columns // step, cells, 0)
 
 
-def tables(cell, kind, levels, rows, columns):
+def tables(cell, kind, levels, rows, columns, coarse):
     count = cell.shape[1]
     lines = levels * rows + 2 * levels
-    return pl.pallas_call(
+    shapes = [(n, count) for n in (lines, lines, lines, columns, columns)]
+    shapes += [(2 * coarse, columns), (2 * coarse, coarse), (2 * coarse, coarse)]
+    made = pl.pallas_call(
         functools.partial(tables_kernel, levels, rows, columns),
-        out_shape=[jax.ShapeDtypeStruct((n, count), BF16) for n in (lines, lines, lines, columns, columns)],
+        out_shape=[jax.ShapeDtypeStruct(shape, BF16) for shape in shapes],
         compiler_params=params(16),
         name="one_hots",
     )(cell, kind)
+    return made[:5], made[5:]
 
 
 def forward_kernel(
@@ -284,13 +268,14 @@
     region = lax.axis_index("reg")
     regions = lax.axis_size("reg")
     members, _, levels, rows, _ = pert_ref.shape
-    coarse_rows, pairs, _ = own_ref.shape
+    pairs = members * levels
+    coarse_rows = own_ref.shape[0] // pairs
     ratio = rows // coarse_rows
     block = chunk * rows
     inner = levels * rows
     even = lax.rem(region, 2) == 0
     table = up_ref[...]
-    rows_in = {r: own_ref[r] for r in range(coarse_rows)}
+    rows_in = {r: own_ref[pl.ds(r, pairs, stride=coarse_rows), :] for r in range(coarse_rows)}
     for k in range(HALO):
         low = coarse_rows - HALO + k
         e = even_ref[pl.ds(low, pairs, stride=coarse_rows), :]
@@ -348,9 +333,9 @@
 
 
 def forward(own, got_even, got_odd, weight, pert, hot, scale):
-    up, _, twice, once = weight
+    up, twice, once = weight
     members, _, levels, rows, columns = pert.shape
-    _, pairs, coarse_columns = own.shape
+    pairs, coarse_columns = members * levels, own.shape[1]
     chunk = 4 if levels % 4 == 0 else 1
     count = hot[0].shape[1]
     return pl.pallas_call(
@@ -491,10 +476,9 @@
 def backward(q_terms, kind, value, weight, tables_y, pert, halo_even, halo_odd, hot, scale, coarse_rows, coarse_columns):
     members, _, levels, rows, columns = pert.shape
     pairs = members * levels
-    chunk = 4 if levels % 4 == 0 else 1
     outs = [jax.ShapeDtypeStruct((n, pairs, coarse_columns), F32) for n in (coarse_rows, HALO, HALO)]
     return pl.pallas_call(
-        functools.partial(backward_kernel, scale, chunk, len(q_terms)),
+        functools.partial(backward_kernel, scale, 4 if levels % 4 == 0 else 1, len(q_terms)),
         out_shape=outs,
         scratch_shapes=[
             pltpu.VMEM((levels * rows + 2 * levels, columns), F32),
@@ -503,7 +487,7 @@
         ],
         compiler_params=params(28),
         name="adjoint_to_coarse",
-    )(*q_terms, kind, value, weight, *tables_y[1:], pert, halo_even, halo_odd, *hot)
+    )(*q_terms, kind, value, weight, *tables_y, pert, halo_even, halo_odd, *hot)
 
 
 def join_kernel(coarse_rows, own_ref, even_ref, odd_ref, out_ref):
@@ -535,18 +519,18 @@
     scale = 1.0 / math.sqrt(members * lax.axis_size("mem"))
     flat = alpha.reshape(-1, coarse_columns)
     cell, kind, value, weight = (x.reshape(1, -1) for x in (obs_cell, obs_kind, obs_value, obs_weight))
-    along_y = weights(coarse_columns, columns)
+    down = down_weights(coarse_columns, columns)
     flat_odd = swap_odd(flat)
     flat_even = swap_even(flat)
-    pack_a, pack_b, cell, kind, own = pack(perturbation, cell, kind, flat, coarse_rows)
+    pack_a, pack_b = pack(perturbation)
     halo_odd = swap_odd(pack_b)
     halo_even = swap_even(pack_a)
-    hot = tables(cell, kind, levels, rows, columns)
-    q, edge_fine = forward(own, flat_even, flat_odd, along_y, perturbation, hot, scale)
+    hot, along_y = tables(cell, kind, levels, rows, columns, coarse_columns)
+    q, edge_fine = forward(flat, flat_even, flat_odd, along_y, perturbation, hot, scale)
     q = edge(q, edge_fine, halo_even, halo_odd, hot, members, levels)
     terms = others(q, "mem")
     own, send_a, send_b = backward(
-        terms, kind, value, weight, along_y, perturbation, halo_even, halo_odd, hot, scale,
+        terms, kind, value, weight, (down, *along_y[1:]), perturbation, halo_even, halo_odd, hot, scale,
         coarse_rows, coarse_columns,
     )
     got_odd = swap_odd(send_b)

time: 38.2 us -> 42.7 us (1.12)
  waiting for transfers between devices: 7.94 us -> 11.3 us
  local copies, waits for them, and re-layouts: 2.2 us -> 3.16 us
    ppermute x3, waiting for transfers between devices: 5.6 us -> 7.93 us  [swap_odd(): return lax.ppermute(value, 'reg', swap_pairs(lax.axis_size('reg'), True))]
    ppermute x3, waiting for transfers between devices: 2.33 us -> 3.37 us  [others(): got.append(lax.ppermute(value, axis, pairs))]
    unnamed x8 -> x14, local copies, waits for them, and re-layouts: 2.2 us -> 3.16 us
    ppermute x3, starting transfers between devices: 12.7 us -> 13.2 us  [swap_odd(): return lax.ppermute(value, 'reg', swap_pairs(lax.axis_size('reg'), True))]
    ppermute x3, starting transfers between devices: 0.7 us -> 0.2 us  [swap_even(): return lax.ppermute(value, 'reg', swap_pairs(lax.axis_size('reg'), False))]
  transfers between devices with their start and end apart: 9 -> 9, of which waited for: 5 -> 4; matrix products, arithmetic and copies ran while one was open for 0% -> 0% of each run, Pallas kernels for 16% -> 12%
where the time goes in v4:
time: 42.7 us; the launch traced here: 42.5 us
  starting transfers between devices  16.4 us (38%)
  Pallas kernels  11.5 us (27%)
  waiting for transfers between devices  11.3 us (26%)
  local copies, waits for them, and re-layouts  3.16 us (7%)
    ppermute x3, starting transfers between devices, swap_odd(): return lax.ppermute(value, 'reg', swap_pairs(lax.axis_size('reg'), True))  13.2 us
    ppermute x3, waiting for transfers between devices, swap_odd(): return lax.ppermute(value, 'reg', swap_pairs(lax.axis_size('reg'), True))  7.93 us
    pallas_call x1, Pallas kernels, backward(): pl.pallas_call(functools.partial(backward_kernel, scale, 4 if levels % 4...  4.33 us
    pallas_call x1, Pallas kernels, forward(): pl.pallas_call(functools.partial(forward_kernel, scale, chunk), out_shape...  3.69 us
    ppermute x3, waiting for transfers between devices, others(): got.append(lax.ppermute(value, axis, pairs))  3.37 us
    unnamed x14, local copies, waits for them, and re-layouts  3.16 us
    ppermute x3, starting transfers between devices, others(): got.append(lax.ppermute(value, axis, pairs))  2.94 us
    pallas_call x1, Pallas kernels, tables(): pl.pallas_call(functools.partial(tables_kernel, levels, rows, columns), o...  1.36 us
  transfers between devices with their start and end apart: 9, of which 4 were waited for; matrix products, arithmetic and copies ran while one was open for 0% of the time, Pallas kernels for 12%

profile of v4, /device:TPU:1, one launch (start us, length us, event | category | flops | bytes accessed | tf_op | source)
XLA Modules:
  0.0 42.5 jit_solution(5991927169178769828)
XLA Ops:
  0.0 0.0 copy-start
  0.0 2.2 %copy-done = bf16[8,2,16,16,512]{4,3,2,1,0:T(8,128)(2,1)S(1)} copy-done((bf16[8,2,16,16,512]{4,3,2,1,0:T(8,128)(2,1)S(1)}, bf16[8,2,16,16,512]{4,3,2,1,0:T(8,128)(2,1)}, u32[]{:S(2)}) %copy-start) | copy-done | bytes 4194328
  2.2 0.0 copy-start.3
  2.2 0.0 copy-start.6
  2.2 0.0 copy-start.1
  2.2 0.8 %pack_rows.1 = (f32[8,2,16,512]{3,2,1,0:T(8,128)S(1)}, f32[8,2,16,512]{3,2,1,0:T(8,128)S(1)}) custom-call(bf16[8,2,16,16,512]{4,3,2,1,0:T(8,128)(2,1)S(1)} %copy-done), custom_call_target="tpu_custom_call" | custom-call | tf_op jit(solution)/shard_map/pack_rows/pallas_call | solution.py:194
  3.0 0.1 collective-permute-start.2
  3.1 4.7 %collective-permute-start.3 = (f32[8,2,16,512]{3,2,1,0:T(8,128)S(1)}, f32[8,2,16,512]{3,2,1,0:T(8,128)S(1)}, u32[]{:S(2)}, u32[]{:S(2)}) collective-permute-start(f32[8,2,16,512]{3,2,1,0:T(8,128)S(1)} %get-tuple-element.31), channel_id=1, source_target_pairs={{1,2},{2,1},{3,4},{4,3},{5,6},{6,5},{9,10},{10,9},{11,12},{12,11},... | collective-permute-start | bytes 1572872 | tf_op jit(solution)/shard_map/ppermute | solution.py:36
  7.8 0.1 collective-permute-start
  7.9 3.6 %collective-permute-start.1 = (f32[512,128]{1,0:T(8,128)}, f32[512,128]{1,0:T(8,128)S(1)}, u32[]{:S(2)}, u32[]{:S(2)}) collective-permute-start(f32[512,128]{1,0:T(8,128)} %bitcast.7), channel_id=1, source_target_pairs={{1,2},{2,1},{3,4},{4,3},{5,6},{6,5},{9,10},{10,9},{11,12},{12,11},... | collective-permute-start | bytes 786440 | tf_op jit(solution)/shard_map/ppermute | solution.py:36
  11.5 0.0 copy-done.3
  11.5 0.0 copy-done.6
  11.5 1.4 %one_hots.1 = (bf16[288,1024]{1,0:T(8,128)(2,1)S(1)}, bf16[288,1024]{1,0:T(8,128)(2,1)S(1)}, bf16[288,1024]{1,0:T(8,128)(2,1)S(1)}, bf16[512,1024]{1,0:T(8,128)(...) custom-call(s32[1,1024]{1,0:T(1,128)S(1)} %bitcast.13, ...), custom_call_target="tpu_custom_call" | custom-call | tf_op jit(solution)/shard_map/one_hots/pallas_call | solution.py:253
  12.8 0.0 collective-permute-done.even_ref
  12.9 4.6 %collective-permute-done.1.odd_ref = f32[512,128]{1,0:T(8,128)S(1)} collective-permute-done((f32[512,128]{1,0:T(8,128)}, f32[512,128]{1,0:T(8,128)S(1)}, u32[]{:S(2)}, u32[]{:S(2)}) %collective-permute-start.1) | collective-permute-done | bytes 262176 | tf_op jit(solution)/shard_map/ppermute | solution.py:36
  17.5 0.0 copy-done.1
  17.5 0.0 copy-start.2
  17.5 0.9 %copy-done.2 = f32[8,16,4,128]{3,2,1,0:T(4,128)S(1)} copy-done((f32[8,16,4,128]{3,2,1,0:T(4,128)S(1)}, f32[8,16,4,128]{3,2,1,0:T(4,128)}, u32[]{:S(2)}) %copy-start.2) | copy-done | bytes 262168
  18.4 3.7 %increment_at_obs.1 = (f32[4,1024]{1,0:T(4,128)S(1)}, f32[2,128,512]{2,1,0:T(8,128)S(1)}) custom-call(f32[512,128]{1,0:T(8,128)S(1)} %bitcast.8, f32[512,128]{1,0:T(8,128)S(1)} %collective-permute-done.even_ref, f32[512,128]{1,0:T(8,128)S(1)} %collective-permute-done.1.odd_ref, bf16[256,512]{1,0:T(8,128)(2,1)S(1)} %get-tuple-element.20.up_ref, ...), custom_call_target="tpu_custom_call" | custom-call | tf_op jit(solution)/shard_map/increment_at_obs/pallas_call | solution.py:341
  22.1 0.0 copy-start.4
  22.1 0.0 copy-start.5
  22.1 0.0 collective-permute-done.2.even_ref.refs_11_
  22.1 0.0 collective-permute-done.3.odd_ref.refs_12_
  22.1 0.5 %edge_at_obs.1.refs_0_ = f32[4,1024]{1,0:T(4,128)S(1)} custom-call(f32[4,1024]{1,0:T(4,128)S(1)} %get-tuple-element.28.q_ref, f32[2,128,512]{2,1,0:T(8,128)S(1)} %get-tuple-element.29.fine_ref, f32[8,2,16,512]{3,2,1,0:T(8,128)S(1)} %collective-permute-done.2.even_ref.refs_11_, f32[8,2,16,512]{3,2,1,0:T(8,128)S(1)} %collective-permute-done.3.odd_ref.refs_12_, ...), custom_call_target="tpu_custom_call" | custom-call | tf_op jit(solution)/shard_map/edge_at_obs/pallas_call | solution.py:382
  22.6 1.7 %collective-permute-start.4 = (f32[4,1024]{1,0:T(4,128)S(1)}, f32[4,1024]{1,0:T(4,128)S(1)}, u32[]{:S(2)}, u32[]{:S(2)}) collective-permute-start(f32[4,1024]{1,0:T(4,128)S(1)} %edge_at_obs.1.refs_0_), channel_id=1, source_target_pairs={{0,8},{8,0},{16,24},{24,16},{1,9},{9,1},{17,25},{25,17},{2,10},{10... | collective-permute-start | bytes 49160 | tf_op jit(solution)/shard_map/ppermute | solution.py:59
  24.3 1.2 %collective-permute-start.5 = (f32[4,1024]{1,0:T(4,128)S(1)}, f32[4,1024]{1,0:T(4,128)S(1)}, u32[]{:S(2)}, u32[]{:S(2)}) collective-permute-start(f32[4,1024]{1,0:T(4,128)S(1)} %edge_at_obs.1.refs_0_), channel_id=1, source_target_pairs={{0,16},{8,24},{16,0},{24,8},{1,17},{9,25},{17,1},{25,9},{2,18},{10... | collective-permute-start | bytes 49160 | tf_op jit(solution)/shard_map/ppermute | solution.py:59
  25.6 0.0 collective-permute-start.6
  25.6 0.1 down_weights.1.refs_7_
  25.7 0.0 collective-permute-done.4.refs_1_
  25.7 1.2 %collective-permute-done.5.refs_2_ = f32[4,1024]{1,0:T(4,128)S(1)} collective-permute-done((f32[4,1024]{1,0:T(4,128)S(1)}, f32[4,1024]{1,0:T(4,128)S(1)}, u32[]{:S(2)}, u32[]{:S(2)}) %collective-permute-start.5) | collective-permute-done | bytes 16416 | tf_op jit(solution)/shard_map/ppermute | solution.py:59
  26.9 2.1 %collective-permute-done.6.refs_3_ = f32[4,1024]{1,0:T(4,128)S(1)} collective-permute-done((f32[4,1024]{1,0:T(4,128)S(1)}, f32[4,1024]{1,0:T(4,128)S(1)}, u32[]{:S(2)}, u32[]{:S(2)}) %collective-permute-start.6) | collective-permute-done | bytes 16416 | tf_op jit(solution)/shard_map/ppermute | solution.py:59
  29.1 0.0 copy-done.4
  29.1 0.0 copy-done.5
  29.1 4.3 %adjoint_to_coarse.1 = (f32[4,128,128]{2,1,0:T(8,128)S(1)}, f32[3,128,128]{2,1,0:T(8,128)S(1)}, f32[3,128,128]{2,1,0:T(8,128)S(1)}) custom-call(f32[4,1024]{1,0:T(4,128)S(1)} %edge_at_obs.1.refs_0_, f32[4,1024]{1,0:T(4,128)S(1)} %collective-permute-done.4.refs_1_, f32[4,1024]{1,0:T(4,128)S(1)} %collective-permute-done.5.refs_2_, ...), custom_call_target="tpu_custom_call" | custom-call | tf_op jit(solution)/shard_map/adjoint_to_coarse/pallas_call | solution.py:480
  33.4 0.1 collective-permute-start.7
  33.5 5.0 %collective-permute-start.8 = (f32[3,128,128]{2,1,0:T(8,128)S(1)}, f32[3,128,128]{2,1,0:T(8,128)S(1)}, u32[]{:S(2)}, u32[]{:S(2)}) collective-permute-start(f32[3,128,128]{2,1,0:T(8,128)S(1)} %get-tuple-element.34), channel_id=1, source_target_pairs={{1,2},{2,1},{3,4},{4,3},{5,6},{6,5},{9,10},{10,9},{11,12},{12,11},... | collective-permute-start | bytes 589832 | tf_op jit(solution)/shard_map/ppermute | solution.py:36
  38.4 0.0 collective-permute-done.7.even_ref
  38.4 3.3 %collective-permute-done.8.odd_ref = f32[3,128,128]{2,1,0:T(8,128)S(1)} collective-permute-done((f32[3,128,128]{2,1,0:T(8,128)S(1)}, f32[3,128,128]{2,1,0:T(8,128)S(1)}, u32[]{:S(2)}, u32[]{:S(2)}) %collective-permute-start.8) | collective-permute-done | bytes 196640 | tf_op jit(solution)/shard_map/ppermute | solution.py:36
  41.8 0.8 %join_rows.1 = f32[512,128]{1,0:T(8,128)} custom-call(f32[4,128,128]{2,1,0:T(8,128)S(1)} %get-tuple-element.32.own_ref, f32[3,128,128]{2,1,0:T(8,128)S(1)} %collective-permute-done.7.even_ref, f32[3,128,128]{2,1,0:T(8,128)S(1)} %collective-permute-done.8.odd_ref), custom_call_target="tpu_custom_call" | custom-call | tf_op jit(solution)/shard_map/join_rows/pallas_call | solution.py:508
Async XLA Ops:
  0.0 2.2 %copy-start = (bf16[8,2,16,16,512]{4,3,2,1,0:T(8,128)(2,1)S(1)}, bf16[8,2,16,16,512]{4,3,2,1,0:T(8,128)(2,1)}, u32[]{:S(2)}) copy-start(bf16[8,2,16,16,512]{4,3,2,1,0:T(8,128)(2,1)} %refs_10_.1) | copy-start | bytes 12582916
  2.2 9.3 %copy-start.3 = (s32[1024]{0:T(1024)S(1)}, s32[1024]{0:T(1024)}, u32[]{:S(2)}) copy-start(s32[1024]{0:T(1024)} %param.9) | copy-start | bytes 12292
  2.2 9.3 %copy-start.6 = (s32[1024]{0:T(1024)S(1)}, s32[1024]{0:T(1024)}, u32[]{:S(2)}) copy-start(s32[1024]{0:T(1024)} %param.8) | copy-start | bytes 12292
  2.2 15.3 %copy-start.1 = (bf16[8,2,16,16,512]{4,3,2,1,0:T(8,128)(2,1)S(1)}, bf16[8,2,16,16,512]{4,3,2,1,0:T(8,128)(2,1)}, u32[]{:S(2)}) copy-start(bf16[8,2,16,16,512]{4,3,2,1,0:T(8,128)(2,1)} %refs_10_.1) | copy-start | bytes 12582916
  3.0 19.1 %collective-permute-start.2 = (f32[8,2,16,512]{3,2,1,0:T(8,128)S(1)}, f32[8,2,16,512]{3,2,1,0:T(8,128)S(1)}, u32[]{:S(2)}, u32[]{:S(2)}) collective-permute-start(f32[8,2,16,512]{3,2,1,0:T(8,128)S(1)} %get-tuple-element.30), channel_id=1, source_target_pairs={{0,1},{1,0},{2,3},{3,2},{4,5},{5,4},{6,7},{7,6},{8,9},{9,8},{10,11... | collective-permute-start | bytes 1572872 | tf_op jit(solution)/shard_map/ppermute | solution.py:32
  3.1 19.1 %collective-permute-start.3 = (f32[8,2,16,512]{3,2,1,0:T(8,128)S(1)}, f32[8,2,16,512]{3,2,1,0:T(8,128)S(1)}, u32[]{:S(2)}, u32[]{:S(2)}) collective-permute-start(f32[8,2,16,512]{3,2,1,0:T(8,128)S(1)} %get-tuple-element.31), channel_id=1, source_target_pairs={{1,2},{2,1},{3,4},{4,3},{5,6},{6,5},{9,10},{10,9},{11,12},{12,11},... | collective-permute-start | bytes 1572872 | tf_op jit(solution)/shard_map/ppermute | solution.py:36
  7.8 5.1 %collective-permute-start = (f32[512,128]{1,0:T(8,128)}, f32[512,128]{1,0:T(8,128)S(1)}, u32[]{:S(2)}, u32[]{:S(2)}) collective-permute-start(f32[512,128]{1,0:T(8,128)} %bitcast.6), channel_id=1, source_target_pairs={{0,1},{1,0},{2,3},{3,2},{4,5},{5,4},{6,7},{7,6},{8,9},{9,8},{10,11... | collective-permute-start | bytes 786440 | tf_op jit(solution)/shard_map/ppermute | solution.py:32
  7.9 9.6 %collective-permute-start.1 = (f32[512,128]{1,0:T(8,128)}, f32[512,128]{1,0:T(8,128)S(1)}, u32[]{:S(2)}, u32[]{:S(2)}) collective-permute-start(f32[512,128]{1,0:T(8,128)} %bitcast.7), channel_id=1, source_target_pairs={{1,2},{2,1},{3,4},{4,3},{5,6},{6,5},{9,10},{10,9},{11,12},{12,11},... | collective-permute-start | bytes 786440 | tf_op jit(solution)/shard_map/ppermute | solution.py:36
  17.5 1.0 %copy-start.2 = (f32[8,16,4,128]{3,2,1,0:T(4,128)S(1)}, f32[8,16,4,128]{3,2,1,0:T(4,128)}, u32[]{:S(2)}) copy-start(f32[8,16,4,128]{3,2,1,0:T(4,128)} %param.6) | copy-start | bytes 786436
  22.1 7.0 %copy-start.4 = (f32[1024]{0:T(1024)S(1)}, f32[1024]{0:T(1024)}, u32[]{:S(2)}) copy-start(f32[1024]{0:T(1024)} %param.10) | copy-start | bytes 12292
  22.1 6.9 %copy-start.5 = (f32[1024]{0:T(1024)S(1)}, f32[1024]{0:T(1024)}, u32[]{:S(2)}) copy-start(f32[1024]{0:T(1024)} %param.11) | copy-start | bytes 12292
  22.6 3.0 %collective-permute-start.4 = (f32[4,1024]{1,0:T(4,128)S(1)}, f32[4,1024]{1,0:T(4,128)S(1)}, u32[]{:S(2)}, u32[]{:S(2)}) collective-permute-start(f32[4,1024]{1,0:T(4,128)S(1)} %edge_at_obs.1.refs_0_), channel_id=1, source_target_pairs={{0,8},{8,0},{16,24},{24,16},{1,9},{9,1},{17,25},{25,17},{2,10},{10... | collective-permute-start | bytes 49160 | tf_op jit(solution)/shard_map/ppermute | solution.py:59
  24.3 2.6 %collective-permute-start.5 = (f32[4,1024]{1,0:T(4,128)S(1)}, f32[4,1024]{1,0:T(4,128)S(1)}, u32[]{:S(2)}, u32[]{:S(2)}) collective-permute-start(f32[4,1024]{1,0:T(4,128)S(1)} %edge_at_obs.1.refs_0_), channel_id=1, source_target_pairs={{0,16},{8,24},{16,0},{24,8},{1,17},{9,25},{17,1},{25,9},{2,18},{10... | collective-permute-start | bytes 49160 | tf_op jit(solution)/shard_map/ppermute | solution.py:59
  25.6 3.5 %collective-permute-start.6 = (f32[4,1024]{1,0:T(4,128)S(1)}, f32[4,1024]{1,0:T(4,128)S(1)}, u32[]{:S(2)}, u32[]{:S(2)}) collective-permute-start(f32[4,1024]{1,0:T(4,128)S(1)} %edge_at_obs.1.refs_0_), channel_id=1, source_target_pairs={{0,24},{8,16},{16,8},{24,0},{1,25},{9,17},{17,9},{25,1},{2,26},{10... | collective-permute-start | bytes 49160 | tf_op jit(solution)/shard_map/ppermute | solution.py:59
  33.4 5.0 %collective-permute-start.7 = (f32[3,128,128]{2,1,0:T(8,128)S(1)}, f32[3,128,128]{2,1,0:T(8,128)S(1)}, u32[]{:S(2)}, u32[]{:S(2)}) collective-permute-start(f32[3,128,128]{2,1,0:T(8,128)S(1)} %get-tuple-element.33), channel_id=1, source_target_pairs={{0,1},{1,0},{2,3},{3,2},{4,5},{5,4},{6,7},{7,6},{8,9},{9,8},{10,11... | collective-permute-start | bytes 589832 | tf_op jit(solution)/shard_map/ppermute | solution.py:32
  33.5 8.3 %collective-permute-start.8 = (f32[3,128,128]{2,1,0:T(8,128)S(1)}, f32[3,128,128]{2,1,0:T(8,128)S(1)}, u32[]{:S(2)}, u32[]{:S(2)}) collective-permute-start(f32[3,128,128]{2,1,0:T(8,128)S(1)} %get-tuple-element.34), channel_id=1, source_target_pairs={{1,2},{2,1},{3,4},{4,3},{5,6},{6,5},{9,10},{10,9},{11,12},{12,11},... | collective-permute-start | bytes 589832 | tf_op jit(solution)/shard_map/ppermute | solution.py:36

commit v5 on v4

--- a/solution.py
+++ b/solution.py
@@ -148,6 +148,11 @@
     return value
 
 
+def sides():
+    odd = lax.rem(lax.axis_index("reg"), 2)
+    return 1 - odd, odd
+
+
 def decode(cell, rows, columns):
     plane = rows * columns
     level = cell // plane
@@ -171,31 +176,26 @@
     )()
 
 
-def pack_kernel(pert_ref, a_ref, b_ref):
+def pack_kernel(last_parity, pert_ref, out_ref):
     members, parts, levels, rows, columns = pert_ref.shape
-    inner = levels * rows
-    even = lax.rem(lax.axis_index("reg"), 2) == 0
-    shape = (2 * levels, inner)
-    pick = iota(shape, 0)
-    to_a = pick < levels
-    edge = jnp.where(to_a == even, rows - 1, 0)
-    wanted = jnp.where(to_a, pick, pick - levels) * rows + edge
+    half = rows // 2
+    last = jnp.where(lax.rem(lax.axis_index("reg"), 2) == last_parity, 1, 0)
+    shape = (levels, levels * half)
+    wanted = iota(shape, 0) * half + last * (half - 1)
     chooser = jnp.where(iota(shape, 1) == wanted, 1.0, 0.0).astype(BF16)
+    inside = pl.ds(pl.multiple_of(last * half, half), half)
     for m in range(members):
         for part in range(parts):
-            got = dot_nn(chooser, pert_ref[m, part].reshape(inner, columns))
-            a_ref[m, part] = got[:levels]
-            b_ref[m, part] = got[levels:]
-
-
-def pack(pert):
+            block = pert_ref[m, part, :, inside, :].reshape(levels * half, columns)
+            out_ref[m, part] = dot_nn(chooser, block)
+
+
+def pack(pert, last_parity):
     members, parts, levels, _, columns = pert.shape
-    out = jax.ShapeDtypeStruct((members, parts, levels, columns), F32)
     return pl.pallas_call(
-        pack_kernel,
-        out_shape=[out, out],
+        functools.partial(pack_kernel, last_parity),
+        out_shape=jax.ShapeDtypeStruct((members, parts, levels, columns), F32),
         compiler_params=params(16),
-        name="pack_rows",
     )(pert)
 
 
@@ -353,27 +353,28 @@
 
 
 def edge_kernel(members, levels, q_ref, fine_ref, even_ref, odd_ref, ru_ref, rv_ref, c0_ref, out_ref):
-    even = lax.rem(lax.axis_index("reg"), 2) == 0
+    side = sides()
+    lines, _ = ru_ref.shape
+    inner = lines - 2 * levels
     table = []
     for part in range(2):
-        for side in range(2):
+        for near, halo_ref in zip(side, (even_ref, odd_ref)):
             total = None
             for m in range(members):
-                e, o = even_ref[m, part], odd_ref[m, part]
-                halo = jnp.where(even, o, e) if side == 0 else jnp.where(even, e, o)
-                term = fine_ref[side, pl.ds(m * levels, levels), :] * halo
+                term = fine_ref[near, pl.ds(m * levels, levels), :] * halo_ref[m, part]
                 total = term if total is None else total + term
             table.append(total)
     high, lower = split(jnp.concatenate(table, axis=0))
     z = dot_nn(jnp.concatenate([high, lower], axis=0), c0_ref[...])
-    tail = 2 * levels
-    z = z[: 2 * tail] + z[2 * tail :]
-    rim = pl.ds(ru_ref.shape[0] - tail, tail)
-    in_u = jnp.sum(ru_ref[rim, :].astype(F32) * z[:tail], axis=0, keepdims=True)
-    in_v = jnp.sum(rv_ref[rim, :].astype(F32) * z[tail:], axis=0, keepdims=True)
+    z = z[: 4 * levels] + z[4 * levels :]
+    for n, ref in ((0, ru_ref), (2, rv_ref)):
+        total = q_ref[pl.ds(2 - n // 2, 1), :]
+        for k in range(2):
+            here = pl.ds(pl.multiple_of(inner + side[k] * levels, levels), levels)
+            part = z[(n + k) * levels : (n + k + 1) * levels]
+            total = total + jnp.sum(ref[here, :].astype(F32) * part, axis=0, keepdims=True)
+        out_ref[pl.ds(2 - n // 2, 1), :] = total
     out_ref[pl.ds(0, 1), :] = q_ref[pl.ds(0, 1), :]
-    out_ref[pl.ds(1, 1), :] = q_ref[pl.ds(1, 1), :] + in_v
-    out_ref[pl.ds(2, 1), :] = q_ref[pl.ds(2, 1), :] + in_u
     out_ref[pl.ds(3, 1), :] = q_ref[pl.ds(3, 1), :]
 
 
@@ -400,7 +401,6 @@
     ratio = rows // coarse_rows
     inner = levels * rows
     even = lax.rem(region, 2) == 0
-    table = down_ref[...]
 
     q = q_refs[0][...]
     for ref in q_refs[1:]:
@@ -417,51 +417,51 @@
     r0, ru, rv = r0_ref[...], ru_ref[...], rv_ref[...]
     lines = r0.shape[0]
     left = [r0 * x + ru * y for x, y in zip(split(a), split(c))] + [rv * x for x in split(g)]
-    both = dot_nt(jnp.concatenate(left, axis=0), c0_ref[...])
-    left = [r0[:inner] * x for x in split(b)]
-    along = dot_nt(jnp.concatenate(left, axis=0), cy_ref[...])
+    left = jnp.concatenate(left, axis=0)
+    left_y = jnp.concatenate([r0[:inner] * x for x in split(b)], axis=0)
+    both = dot_nt(left, c0_ref[...])
+    along = dot_nt(left_y, cy_ref[...])
     total = both[:lines] + both[lines : 2 * lines]
     u_scr[pl.ds(0, inner), :] = total[:inner] + (along[:inner] + along[inner:])
     u_scr[pl.ds(inner, lines - inner), :] = total[inner:]
     v_scr[...] = both[2 * lines : 3 * lines] + both[3 * lines :]
 
+    def project(products):
+        high, lower = split(jnp.concatenate(products, axis=0))
+        return dot_nn(high, down_ref[...]) + dot_nn(lower, down_ref[...])
+
     block = chunk * rows
     for s in range(levels // chunk):
-        product = []
+        products = []
         for m in range(members):
-            for n in range(chunk):
-                k = s * chunk + n
-                u = u_scr[pl.ds(k * rows, rows), :]
-                v = v_scr[pl.ds(k * rows, rows), :]
-                product.append(u * pert_ref[m, 0, k].astype(F32) + v * pert_ref[m, 1, k].astype(F32))
-        high, lower = split(jnp.concatenate(product, axis=0))
-        got = dot_nn(high, table) + dot_nn(lower, table)
+            for k in range(s * chunk, (s + 1) * chunk):
+                here = pl.ds(k * rows, rows)
+                pu, pv = pert_ref[m, 0, k].astype(F32), pert_ref[m, 1, k].astype(F32)
+                products.append(u_scr[here, :] * pu + v_scr[here, :] * pv)
+        got = project(products)
         for m in range(members):
             f_scr[pl.ds(m * inner + s * block, block), :] = got[m * block : (m + 1) * block]
 
-    out = {}
-
-    def add(i, value):
-        low, w0, w1 = weights_x(i, ratio)
-        for at, w in ((low, w0), (low + 1, w1)):
-            out[at] = w * value if at not in out else out[at] + w * value
-
-    for side in range(2):
-        u = u_scr[pl.ds(inner + side * levels, levels), :]
-        v = v_scr[pl.ds(inner + side * levels, levels), :]
-        product = []
+    edges = {}
+    for n in range(2):
+        rim = pl.ds(inner + n * levels, levels)
+        u, v = u_scr[rim, :], v_scr[rim, :]
+        found = []
         for m in range(members):
             halo = []
             for part in range(2):
-                e, o = even_ref[m, part], odd_ref[m, part]
-                halo.append(jnp.where(even, o, e) if side == 0 else jnp.where(even, e, o))
-            product.append(u * halo[0] + v * halo[1])
-        high, lower = split(jnp.concatenate(product, axis=0))
-        got = dot_nn(high, table) + dot_nn(lower, table)
-        add(-1 if side == 0 else rows, got)
-    for i in range(rows):
-        add(i, f_scr[pl.ds(i, pairs, stride=rows), :])
-    held = {r: mask_row(value * scale, r, coarse_rows, region, regions) for r, value in out.items()}
+                x, y = even_ref[m, part], odd_ref[m, part]
+                halo.append(jnp.where(even, y, x) if n == 0 else jnp.where(even, x, y))
+            found.append(u * halo[0] + v * halo[1])
+        edges[-1 if n == 0 else rows] = project(found)
+
+    held = {}
+    for i in range(-1, rows + 1):
+        value = edges[i] if i in edges else f_scr[pl.ds(i, pairs, stride=rows), :]
+        low, w0, w1 = weights_x(i, ratio)
+        for at, w in ((low, w0), (low + 1, w1)):
+            held[at] = w * value if at not in held else held[at] + w * value
+    held = {r: mask_row(value * scale, r, coarse_rows, region, regions) for r, value in held.items()}
     held = smooth(
         held, range(-HALO, coarse_rows + HALO), coarse_rows, region, regions, twice_ref[...], once_ref[...]
     )
@@ -490,24 +490,43 @@
     )(*q_terms, kind, value, weight, *tables_y, pert, halo_even, halo_odd, *hot)
 
 
-def join_kernel(coarse_rows, own_ref, even_ref, odd_ref, out_ref):
+def join_kernel(coarse_rows, own_ref, even_ref, odd_ref, out_hbm, out_scr, sem):
     even = lax.rem(lax.axis_index("reg"), 2) == 0
     pairs = own_ref.shape[1]
-    for r in range(coarse_rows):
-        total = own_ref[r]
-        if r < HALO:
-            total = total + jnp.where(even, odd_ref[r], even_ref[r])
-        k = r - (coarse_rows - HALO)
-        if k >= 0:
-            total = total + jnp.where(even, even_ref[k], odd_ref[k])
-        out_ref[pl.ds(r, pairs, stride=coarse_rows), :] = total
+    chunks = sem.shape[0]
+    some = pairs // chunks
+    copies = []
+    for n in range(chunks):
+        here = pl.ds(n * some, some)
+        for r in range(coarse_rows):
+            total = own_ref[r, here, :]
+            if r < HALO:
+                total = total + jnp.where(even, odd_ref[r, here, :], even_ref[r, here, :])
+            k = r - (coarse_rows - HALO)
+            if k >= 0:
+                total = total + jnp.where(even, even_ref[k, here, :], odd_ref[k, here, :])
+            out_scr[pl.ds(n * some * coarse_rows + r, some, stride=coarse_rows), :] = total
+        block = pl.ds(n * some * coarse_rows, some * coarse_rows)
+        copy = pltpu.make_async_copy(out_scr.at[block], out_hbm.at[block], sem.at[n])
+        copy.start()
+        copies.append(copy)
+    for copy in copies:
+        copy.wait()
 
 
 def join(own, got_even, got_odd):
     coarse_rows, pairs, columns = own.shape
+    chunks = 4 if pairs % 32 == 0 else 1
+    vmem = pl.BlockSpec(memory_space=pltpu.VMEM)
     return pl.pallas_call(
         functools.partial(join_kernel, coarse_rows),
+        in_specs=[vmem, vmem, vmem],
+        out_specs=pl.BlockSpec(memory_space=pltpu.HBM),
         out_shape=jax.ShapeDtypeStruct((pairs * coarse_rows, columns), F32),
+        scratch_shapes=[
+            pltpu.VMEM((pairs * coarse_rows, columns), F32),
+            pltpu.SemaphoreType.DMA((chunks,)),
+        ],
         compiler_params=params(16),
         name="join_rows",
     )(own, got_even, got_odd)
@@ -522,9 +541,10 @@
     down = down_weights(coarse_columns, columns)
     flat_odd = swap_odd(flat)
     flat_even = swap_even(flat)
-    pack_a, pack_b = pack(perturbation)
-    halo_odd = swap_odd(pack_b)
-    halo_even = swap_even(pack_a)
+    packed = pack(perturbation, 1)
+    halo_odd = swap_odd(packed)
+    packed = pack(perturbation, 0)
+    halo_even = swap_even(packed)
     hot, along_y = tables(cell, kind, levels, rows, columns, coarse_columns)
     q, edge_fine = forward(flat, flat_even, flat_odd, along_y, perturbation, hot, scale)
     q = edge(q, edge_fine, halo_even, halo_odd, hot, members, levels)

time: 42.7 us -> 41.7 us (0.977)
  local copies, waits for them, and re-layouts: 3.16 us -> 2.21 us
    unnamed x14, local copies, waits for them, and re-layouts: 3.16 us -> 2.21 us
    pallas_call x2 -> x3, Pallas kernels: 1.58 us -> 1.53 us  [the longest x2 0.78 us: pack(): pl.pallas_call(functools.partial(pack_kernel, last_parity), out_shape=jax...]
  transfers between devices with their start and end apart: 9 -> 9, of which waited for: 4 -> 4; matrix products, arithmetic and copies ran while one was open for 0% -> 0% of each run, Pallas kernels for 12% -> 13%
where the time goes in v5:
time: 41.7 us; the launch traced here: 41.5 us
  starting transfers between devices  16.4 us (39%)
  Pallas kernels  11.4 us (27%)
  waiting for transfers between devices  11.3 us (27%)
  local copies, waits for them, and re-layouts  2.21 us (5%)
    ppermute x3, starting transfers between devices, swap_odd(): return lax.ppermute(value, 'reg', swap_pairs(lax.axis_size('reg'), True))  13 us
    ppermute x3, waiting for transfers between devices, swap_odd(): return lax.ppermute(value, 'reg', swap_pairs(lax.axis_size('reg'), True))  7.92 us
    pallas_call x1, Pallas kernels, backward(): pl.pallas_call(functools.partial(backward_kernel, scale, 4 if levels % 4...  4.32 us
    pallas_call x1, Pallas kernels, forward(): pl.pallas_call(functools.partial(forward_kernel, scale, chunk), out_shape...  3.69 us
    ppermute x3, waiting for transfers between devices, others(): got.append(lax.ppermute(value, axis, pairs))  3.37 us
    ppermute x3, starting transfers between devices, others(): got.append(lax.ppermute(value, axis, pairs))  3.17 us
    unnamed x14, local copies, waits for them, and re-layouts  2.21 us
    pallas_call x1, Pallas kernels, tables(): pl.pallas_call(functools.partial(tables_kernel, levels, rows, columns), o...  1.36 us
  transfers between devices with their start and end apart: 9, of which 4 were waited for; matrix products, arithmetic and copies ran while one was open for 0% of the time, Pallas kernels for 13%

profile of v5, /device:TPU:1, one launch (start us, length us, event | category | flops | bytes accessed | tf_op | source)
XLA Modules:
  0.0 41.5 jit_solution(6743597852413711759)
XLA Ops:
  0.0 0.0 copy-start
  0.0 2.2 %copy-done = bf16[8,2,16,16,512]{4,3,2,1,0:T(8,128)(2,1)S(1)} copy-done((bf16[8,2,16,16,512]{4,3,2,1,0:T(8,128)(2,1)S(1)}, bf16[8,2,16,16,512]{4,3,2,1,0:T(8,128)(2,1)}, u32[]{:S(2)}) %copy-start) | copy-done | bytes 4194328
  2.2 0.0 copy-start.2
  2.2 0.0 copy-start.3
  2.2 0.0 copy-start.6
  2.2 0.0 copy-start.1
  2.2 0.4 shard_map.64
  2.6 0.1 collective-permute-start.2
  2.6 0.4 shard_map.65
  3.0 4.7 %collective-permute-start.3 = (f32[8,2,16,512]{3,2,1,0:T(8,128)S(1)}, f32[8,2,16,512]{3,2,1,0:T(8,128)S(1)}, u32[]{:S(2)}, u32[]{:S(2)}) collective-permute-start(f32[8,2,16,512]{3,2,1,0:T(8,128)S(1)} %shard_map.65), channel_id=1, source_target_pairs={{1,2},{2,1},{3,4},{4,3},{5,6},{6,5},{9,10},{10,9},{11,12},{12,11},... | collective-permute-start | bytes 1572872 | tf_op jit(solution)/shard_map/ppermute | solution.py:36
  7.8 0.0 copy-done.2
  7.8 0.1 collective-permute-start
  7.8 3.6 %collective-permute-start.1 = (f32[512,128]{1,0:T(8,128)S(1)}, f32[512,128]{1,0:T(8,128)S(1)}, u32[]{:S(2)}, u32[]{:S(2)}) collective-permute-start(f32[512,128]{1,0:T(8,128)S(1)} %bitcast.7), channel_id=1, source_target_pairs={{1,2},{2,1},{3,4},{4,3},{5,6},{6,5},{9,10},{10,9},{11,12},{12,11},... | collective-permute-start | bytes 786440 | tf_op jit(solution)/shard_map/ppermute | solution.py:36
  11.4 0.0 copy-done.3
  11.4 0.0 copy-done.6
  11.4 1.4 %one_hots.1 = (bf16[288,1024]{1,0:T(8,128)(2,1)S(1)}, bf16[288,1024]{1,0:T(8,128)(2,1)S(1)}, bf16[288,1024]{1,0:T(8,128)(2,1)S(1)}, bf16[512,1024]{1,0:T(8,128)(...) custom-call(s32[1,1024]{1,0:T(1,128)S(1)} %bitcast.13, ...), custom_call_target="tpu_custom_call" | custom-call | tf_op jit(solution)/shard_map/one_hots/pallas_call | solution.py:253
  12.8 0.0 collective-permute-done.even_ref
  12.8 4.6 %collective-permute-done.1.odd_ref = f32[512,128]{1,0:T(8,128)S(1)} collective-permute-done((f32[512,128]{1,0:T(8,128)S(1)}, f32[512,128]{1,0:T(8,128)S(1)}, u32[]{:S(2)}, u32[]{:S(2)}) %collective-permute-start.1) | collective-permute-done | bytes 262176 | tf_op jit(solution)/shard_map/ppermute | solution.py:36
  17.4 0.0 copy-done.1
  17.4 3.7 %increment_at_obs.1 = (f32[4,1024]{1,0:T(4,128)S(1)}, f32[2,128,512]{2,1,0:T(8,128)S(1)}) custom-call(f32[512,128]{1,0:T(8,128)S(1)} %bitcast.8, f32[512,128]{1,0:T(8,128)S(1)} %collective-permute-done.even_ref, f32[512,128]{1,0:T(8,128)S(1)} %collective-permute-done.1.odd_ref, bf16[256,512]{1,0:T(8,128)(2,1)S(1)} %get-tuple-element.18.up_ref, ...), custom_call_target="tpu_custom_call" | custom-call | tf_op jit(solution)/shard_map/increment_at_obs/pallas_call | solution.py:341
  21.1 0.0 copy-start.4
  21.1 0.0 copy-start.5
  21.1 0.0 collective-permute-done.2.even_ref.refs_11_
  21.2 0.0 collective-permute-done.3.odd_ref.refs_12_
  21.2 0.5 %edge_at_obs.1.refs_0_ = f32[4,1024]{1,0:T(4,128)S(1)} custom-call(f32[4,1024]{1,0:T(4,128)S(1)} %get-tuple-element.26.q_ref, f32[2,128,512]{2,1,0:T(8,128)S(1)} %get-tuple-element.27.fine_ref, f32[8,2,16,512]{3,2,1,0:T(8,128)S(1)} %collective-permute-done.2.even_ref.refs_11_, f32[8,2,16,512]{3,2,1,0:T(8,128)S(1)} %collective-permute-done.3.odd_ref.refs_12_, ...), custom_call_target="tpu_custom_call" | custom-call | tf_op jit(solution)/shard_map/edge_at_obs/pallas_call | solution.py:383
  21.6 1.9 %collective-permute-start.4 = (f32[4,1024]{1,0:T(4,128)S(1)}, f32[4,1024]{1,0:T(4,128)S(1)}, u32[]{:S(2)}, u32[]{:S(2)}) collective-permute-start(f32[4,1024]{1,0:T(4,128)S(1)} %edge_at_obs.1.refs_0_), channel_id=1, source_target_pairs={{0,8},{8,0},{16,24},{24,16},{1,9},{9,1},{17,25},{25,17},{2,10},{10... | collective-permute-start | bytes 49160 | tf_op jit(solution)/shard_map/ppermute | solution.py:59
  23.5 1.2 %collective-permute-start.5 = (f32[4,1024]{1,0:T(4,128)S(1)}, f32[4,1024]{1,0:T(4,128)S(1)}, u32[]{:S(2)}, u32[]{:S(2)}) collective-permute-start(f32[4,1024]{1,0:T(4,128)S(1)} %edge_at_obs.1.refs_0_), channel_id=1, source_target_pairs={{0,16},{8,24},{16,0},{24,8},{1,17},{9,25},{17,1},{25,9},{2,18},{10... | collective-permute-start | bytes 49160 | tf_op jit(solution)/shard_map/ppermute | solution.py:59
  24.8 0.0 collective-permute-start.6
  24.8 0.1 down_weights.1.refs_7_
  24.9 0.0 collective-permute-done.4.refs_1_
  24.9 1.2 %collective-permute-done.5.refs_2_ = f32[4,1024]{1,0:T(4,128)S(1)} collective-permute-done((f32[4,1024]{1,0:T(4,128)S(1)}, f32[4,1024]{1,0:T(4,128)S(1)}, u32[]{:S(2)}, u32[]{:S(2)}) %collective-permute-start.5) | collective-permute-done | bytes 16416 | tf_op jit(solution)/shard_map/ppermute | solution.py:59
  26.1 2.1 %collective-permute-done.6.refs_3_ = f32[4,1024]{1,0:T(4,128)S(1)} collective-permute-done((f32[4,1024]{1,0:T(4,128)S(1)}, f32[4,1024]{1,0:T(4,128)S(1)}, u32[]{:S(2)}, u32[]{:S(2)}) %collective-permute-start.6) | collective-permute-done | bytes 16416 | tf_op jit(solution)/shard_map/ppermute | solution.py:59
  28.3 0.0 copy-done.4
  28.3 0.0 copy-done.5
  28.3 4.3 %adjoint_to_coarse.1 = (f32[4,128,128]{2,1,0:T(8,128)S(1)}, f32[3,128,128]{2,1,0:T(8,128)S(1)}, f32[3,128,128]{2,1,0:T(8,128)S(1)}) custom-call(f32[4,1024]{1,0:T(4,128)S(1)} %edge_at_obs.1.refs_0_, f32[4,1024]{1,0:T(4,128)S(1)} %collective-permute-done.4.refs_1_, f32[4,1024]{1,0:T(4,128)S(1)} %collective-permute-done.5.refs_2_, ...), custom_call_target="tpu_custom_call" | custom-call | tf_op jit(solution)/shard_map/adjoint_to_coarse/pallas_call | solution.py:480
  32.6 0.1 collective-permute-start.7
  32.7 4.7 %collective-permute-start.8 = (f32[3,128,128]{2,1,0:T(8,128)S(1)}, f32[3,128,128]{2,1,0:T(8,128)S(1)}, u32[]{:S(2)}, u32[]{:S(2)}) collective-permute-start(f32[3,128,128]{2,1,0:T(8,128)S(1)} %get-tuple-element.30), channel_id=1, source_target_pairs={{1,2},{2,1},{3,4},{4,3},{5,6},{6,5},{9,10},{10,9},{11,12},{12,11},... | collective-permute-start | bytes 589832 | tf_op jit(solution)/shard_map/ppermute | solution.py:36
  37.4 0.0 collective-permute-done.7.even_ref
  37.4 3.3 %collective-permute-done.8.odd_ref = f32[3,128,128]{2,1,0:T(8,128)S(1)} collective-permute-done((f32[3,128,128]{2,1,0:T(8,128)S(1)}, f32[3,128,128]{2,1,0:T(8,128)S(1)}, u32[]{:S(2)}, u32[]{:S(2)}) %collective-permute-start.8) | collective-permute-done | bytes 196640 | tf_op jit(solution)/shard_map/ppermute | solution.py:36
  40.7 0.7 %join_rows.1 = f32[512,128]{1,0:T(8,128)} custom-call(f32[4,128,128]{2,1,0:T(8,128)S(1)} %get-tuple-element.28.own_ref, f32[3,128,128]{2,1,0:T(8,128)S(1)} %collective-permute-done.7.even_ref, f32[3,128,128]{2,1,0:T(8,128)S(1)} %collective-permute-done.8.odd_ref), custom_call_target="tpu_custom_call" | custom-call | tf_op jit(solution)/shard_map/join_rows/pallas_call | solution.py:521
Async XLA Ops:
  0.0 2.2 %copy-start = (bf16[8,2,16,16,512]{4,3,2,1,0:T(8,128)(2,1)S(1)}, bf16[8,2,16,16,512]{4,3,2,1,0:T(8,128)(2,1)}, u32[]{:S(2)}) copy-start(bf16[8,2,16,16,512]{4,3,2,1,0:T(8,128)(2,1)} %refs_10_.1) | copy-start | bytes 12582916
  2.2 5.6 %copy-start.2 = (f32[8,16,4,128]{3,2,1,0:T(4,128)S(1)}, f32[8,16,4,128]{3,2,1,0:T(4,128)}, u32[]{:S(2)}) copy-start(f32[8,16,4,128]{3,2,1,0:T(4,128)} %param.6) | copy-start | bytes 786436
  2.2 9.2 %copy-start.3 = (s32[1024]{0:T(1024)S(1)}, s32[1024]{0:T(1024)}, u32[]{:S(2)}) copy-start(s32[1024]{0:T(1024)} %param.9) | copy-start | bytes 12292
  2.2 9.2 %copy-start.6 = (s32[1024]{0:T(1024)S(1)}, s32[1024]{0:T(1024)}, u32[]{:S(2)}) copy-start(s32[1024]{0:T(1024)} %param.8) | copy-start | bytes 12292
  2.2 15.2 %copy-start.1 = (bf16[8,2,16,16,512]{4,3,2,1,0:T(8,128)(2,1)S(1)}, bf16[8,2,16,16,512]{4,3,2,1,0:T(8,128)(2,1)}, u32[]{:S(2)}) copy-start(bf16[8,2,16,16,512]{4,3,2,1,0:T(8,128)(2,1)} %refs_10_.1) | copy-start | bytes 12582916
  2.6 18.6 %collective-permute-start.2 = (f32[8,2,16,512]{3,2,1,0:T(8,128)S(1)}, f32[8,2,16,512]{3,2,1,0:T(8,128)S(1)}, u32[]{:S(2)}, u32[]{:S(2)}) collective-permute-start(f32[8,2,16,512]{3,2,1,0:T(8,128)S(1)} %shard_map.64), channel_id=1, source_target_pairs={{0,1},{1,0},{2,3},{3,2},{4,5},{5,4},{6,7},{7,6},{8,9},{9,8},{10,11... | collective-permute-start | bytes 1572872 | tf_op jit(solution)/shard_map/ppermute | solution.py:32
  3.0 18.1 %collective-permute-start.3 = (f32[8,2,16,512]{3,2,1,0:T(8,128)S(1)}, f32[8,2,16,512]{3,2,1,0:T(8,128)S(1)}, u32[]{:S(2)}, u32[]{:S(2)}) collective-permute-start(f32[8,2,16,512]{3,2,1,0:T(8,128)S(1)} %shard_map.65), channel_id=1, source_target_pairs={{1,2},{2,1},{3,4},{4,3},{5,6},{6,5},{9,10},{10,9},{11,12},{12,11},... | collective-permute-start | bytes 1572872 | tf_op jit(solution)/shard_map/ppermute | solution.py:36
  7.8 5.1 %collective-permute-start = (f32[512,128]{1,0:T(8,128)S(1)}, f32[512,128]{1,0:T(8,128)S(1)}, u32[]{:S(2)}, u32[]{:S(2)}) collective-permute-start(f32[512,128]{1,0:T(8,128)S(1)} %bitcast.6), channel_id=1, source_target_pairs={{0,1},{1,0},{2,3},{3,2},{4,5},{5,4},{6,7},{7,6},{8,9},{9,8},{10,11... | collective-permute-start | bytes 786440 | tf_op jit(solution)/shard_map/ppermute | solution.py:32
  7.8 9.6 %collective-permute-start.1 = (f32[512,128]{1,0:T(8,128)S(1)}, f32[512,128]{1,0:T(8,128)S(1)}, u32[]{:S(2)}, u32[]{:S(2)}) collective-permute-start(f32[512,128]{1,0:T(8,128)S(1)} %bitcast.7), channel_id=1, source_target_pairs={{1,2},{2,1},{3,4},{4,3},{5,6},{6,5},{9,10},{10,9},{11,12},{12,11},... | collective-permute-start | bytes 786440 | tf_op jit(solution)/shard_map/ppermute | solution.py:36
  21.1 7.2 %copy-start.4 = (f32[1024]{0:T(1024)S(1)}, f32[1024]{0:T(1024)}, u32[]{:S(2)}) copy-start(f32[1024]{0:T(1024)} %param.10) | copy-start | bytes 12292
  21.1 7.1 %copy-start.5 = (f32[1024]{0:T(1024)S(1)}, f32[1024]{0:T(1024)}, u32[]{:S(2)}) copy-start(f32[1024]{0:T(1024)} %param.11) | copy-start | bytes 12292
  21.6 3.3 %collective-permute-start.4 = (f32[4,1024]{1,0:T(4,128)S(1)}, f32[4,1024]{1,0:T(4,128)S(1)}, u32[]{:S(2)}, u32[]{:S(2)}) collective-permute-start(f32[4,1024]{1,0:T(4,128)S(1)} %edge_at_obs.1.refs_0_), channel_id=1, source_target_pairs={{0,8},{8,0},{16,24},{24,16},{1,9},{9,1},{17,25},{25,17},{2,10},{10... | collective-permute-start | bytes 49160 | tf_op jit(solution)/shard_map/ppermute | solution.py:59
  23.5 2.6 %collective-permute-start.5 = (f32[4,1024]{1,0:T(4,128)S(1)}, f32[4,1024]{1,0:T(4,128)S(1)}, u32[]{:S(2)}, u32[]{:S(2)}) collective-permute-start(f32[4,1024]{1,0:T(4,128)S(1)} %edge_at_obs.1.refs_0_), channel_id=1, source_target_pairs={{0,16},{8,24},{16,0},{24,8},{1,17},{9,25},{17,1},{25,9},{2,18},{10... | collective-permute-start | bytes 49160 | tf_op jit(solution)/shard_map/ppermute | solution.py:59
  24.8 3.5 %collective-permute-start.6 = (f32[4,1024]{1,0:T(4,128)S(1)}, f32[4,1024]{1,0:T(4,128)S(1)}, u32[]{:S(2)}, u32[]{:S(2)}) collective-permute-start(f32[4,1024]{1,0:T(4,128)S(1)} %edge_at_obs.1.refs_0_), channel_id=1, source_target_pairs={{0,24},{8,16},{16,8},{24,0},{1,25},{9,17},{17,9},{25,1},{2,26},{10... | collective-permute-start | bytes 49160 | tf_op jit(solution)/shard_map/ppermute | solution.py:59
  32.6 4.8 %collective-permute-start.7 = (f32[3,128,128]{2,1,0:T(8,128)S(1)}, f32[3,128,128]{2,1,0:T(8,128)S(1)}, u32[]{:S(2)}, u32[]{:S(2)}) collective-permute-start(f32[3,128,128]{2,1,0:T(8,128)S(1)} %get-tuple-element.29), channel_id=1, source_target_pairs={{0,1},{1,0},{2,3},{3,2},{4,5},{5,4},{6,7},{7,6},{8,9},{9,8},{10,11... | collective-permute-start | bytes 589832 | tf_op jit(solution)/shard_map/ppermute | solution.py:32
  32.7 8.1 %collective-permute-start.8 = (f32[3,128,128]{2,1,0:T(8,128)S(1)}, f32[3,128,128]{2,1,0:T(8,128)S(1)}, u32[]{:S(2)}, u32[]{:S(2)}) collective-permute-start(f32[3,128,128]{2,1,0:T(8,128)S(1)} %get-tuple-element.30), channel_id=1, source_target_pairs={{1,2},{2,1},{3,4},{4,3},{5,6},{6,5},{9,10},{10,9},{11,12},{12,11},... | collective-permute-start | bytes 589832 | tf_op jit(solution)/shard_map/ppermute | solution.py:36

commit v6 on v5

--- a/solution.py
+++ b/solution.py
@@ -388,16 +388,23 @@
     )(q, fine, halo_even, halo_odd, ru, rv, c0)
 
 
+def smooth_outside(held, before, twice_ref, once_ref):
+    last = max(held) - 1
+    rows = {r: jnp.where(before, held[r], held[last - r]) for r in range(-1, PASSES)}
+    return smooth(rows, range(-HALO, 0), last + 1, 0, 1, twice_ref[...], once_ref[...])
+
+
 def backward_kernel(scale, chunk, terms, *refs):
     q_refs = refs[:terms]
     (kind_ref, value_ref, weight_ref, down_ref, twice_ref, once_ref, pert_ref, even_ref, odd_ref,
      r0_ref, ru_ref, rv_ref, c0_ref, cy_ref,
-     own_out, a_out, b_out,
+     held_out, b_out,
      u_scr, v_scr, f_scr) = refs[terms:]
     region = lax.axis_index("reg")
     regions = lax.axis_size("reg")
     members, _, levels, rows, _ = pert_ref.shape
-    coarse_rows, pairs, _ = own_out.shape
+    height, pairs, _ = held_out.shape
+    coarse_rows = height - 2
     ratio = rows // coarse_rows
     inner = levels * rows
     even = lax.rem(region, 2) == 0
@@ -462,21 +469,17 @@
         for at, w in ((low, w0), (low + 1, w1)):
             held[at] = w * value if at not in held else held[at] + w * value
     held = {r: mask_row(value * scale, r, coarse_rows, region, regions) for r, value in held.items()}
-    held = smooth(
-        held, range(-HALO, coarse_rows + HALO), coarse_rows, region, regions, twice_ref[...], once_ref[...]
-    )
-    for r in range(coarse_rows):
-        own_out[r] = held[r]
+    for r, value in held.items():
+        held_out[r + 1] = value
+    near = smooth_outside(held, even, twice_ref, once_ref)
     for k in range(HALO):
-        before, after = held[k - HALO], held[coarse_rows + k]
-        a_out[k] = jnp.where(even, after, before)
-        b_out[k] = jnp.where(even, before, after)
+        b_out[k] = jnp.where(even, near[k - HALO], near[-1 - k])
 
 
 def backward(q_terms, kind, value, weight, tables_y, pert, halo_even, halo_odd, hot, scale, coarse_rows, coarse_columns):
     members, _, levels, rows, columns = pert.shape
     pairs = members * levels
-    outs = [jax.ShapeDtypeStruct((n, pairs, coarse_columns), F32) for n in (coarse_rows, HALO, HALO)]
+    outs = [jax.ShapeDtypeStruct((n, pairs, coarse_columns), F32) for n in (coarse_rows + 2, HALO)]
     return pl.pallas_call(
         functools.partial(backward_kernel, scale, 4 if levels % 4 == 0 else 1, len(q_terms)),
         out_shape=outs,
@@ -488,6 +491,30 @@
         compiler_params=params(28),
         name="adjoint_to_coarse",
     )(*q_terms, kind, value, weight, *tables_y, pert, halo_even, halo_odd, *hot)
+
+
+def finish_kernel(held_ref, twice_ref, once_ref, own_out, a_out):
+    region = lax.axis_index("reg")
+    regions = lax.axis_size("reg")
+    even = lax.rem(region, 2) == 0
+    coarse_rows = own_out.shape[0]
+    held = {r: held_ref[r + 1] for r in range(-1, coarse_rows + 1)}
+    near = smooth_outside(held, jnp.logical_not(even), twice_ref, once_ref)
+    for k in range(HALO):
+        a_out[k] = jnp.where(even, near[-1 - k], near[k - HALO])
+    own = smooth(held, range(coarse_rows), coarse_rows, region, regions, twice_ref[...], once_ref[...])
+    for r in range(coarse_rows):
+        own_out[r] = own[r]
+
+
+def finish(held, tables_y):
+    height, pairs, columns = held.shape
+    return pl.pallas_call(
+        finish_kernel,
+        out_shape=[jax.ShapeDtypeStruct((n, pairs, columns), F32) for n in (height - 2, HALO)],
+        compiler_params=params(16),
+        name="finish_rows",
+    )(held, *tables_y)
 
 
 def join_kernel(coarse_rows, own_ref, even_ref, odd_ref, out_hbm, out_scr, sem):
@@ -549,11 +576,12 @@
     q, edge_fine = forward(flat, flat_even, flat_odd, along_y, perturbation, hot, scale)
     q = edge(q, edge_fine, halo_even, halo_odd, hot, members, levels)
     terms = others(q, "mem")
-    own, send_a, send_b = backward(
+    held, send_b = backward(
         terms, kind, value, weight, (down, *along_y[1:]), perturbation, halo_even, halo_odd, hot, scale,
         coarse_rows, coarse_columns,
     )
     got_odd = swap_odd(send_b)
+    own, send_a = finish(held, along_y[1:])
     got_even = swap_even(send_a)
     return join(own, got_even, got_odd).reshape(alpha.shape)
 

time: 41.7 us -> 41.7 us (level)
  no operation moved by 1% of the time
where the time goes in v6:
time: 41.7 us; the launch traced here: 41.6 us
  starting transfers between devices  16.4 us (39%)
  Pallas kernels  11.5 us (28%)
  waiting for transfers between devices  11.3 us (27%)
  local copies, waits for them, and re-layouts  2.21 us (5%)
    ppermute x3, starting transfers between devices, swap_odd(): return lax.ppermute(value, 'reg', swap_pairs(lax.axis_size('reg'), True))  13 us
    ppermute x3, waiting for transfers between devices, swap_odd(): return lax.ppermute(value, 'reg', swap_pairs(lax.axis_size('reg'), True))  7.92 us
    pallas_call x1, Pallas kernels, backward(): pl.pallas_call(functools.partial(backward_kernel, scale, 4 if levels % 4...  4.03 us
    pallas_call x1, Pallas kernels, forward(): pl.pallas_call(functools.partial(forward_kernel, scale, chunk), out_shape...  3.69 us
    ppermute x3, waiting for transfers between devices, others(): got.append(lax.ppermute(value, axis, pairs))  3.37 us
    ppermute x3, starting transfers between devices, others(): got.append(lax.ppermute(value, axis, pairs))  3.17 us
    unnamed x14, local copies, waits for them, and re-layouts  2.21 us
    pallas_call x1, Pallas kernels, tables(): pl.pallas_call(functools.partial(tables_kernel, levels, rows, columns), o...  1.36 us
  transfers between devices with their start and end apart: 9, of which 4 were waited for; matrix products, arithmetic and copies ran while one was open for 0% of the time, Pallas kernels for 13%

profile of v6, /device:TPU:1, one launch (start us, length us, event | category | flops | bytes accessed | tf_op | source)
XLA Modules:
  0.0 41.6 jit_solution(12341367633446966678)
XLA Ops:
  0.0 0.0 copy-start
  0.0 2.2 %copy-done = bf16[8,2,16,16,512]{4,3,2,1,0:T(8,128)(2,1)S(1)} copy-done((bf16[8,2,16,16,512]{4,3,2,1,0:T(8,128)(2,1)S(1)}, bf16[8,2,16,16,512]{4,3,2,1,0:T(8,128)(2,1)}, u32[]{:S(2)}) %copy-start) | copy-done | bytes 4194328
  2.2 0.0 copy-start.2
  2.2 0.0 copy-start.3
  2.2 0.0 copy-start.6
  2.2 0.0 copy-start.1
  2.2 0.4 shard_map.64
  2.6 0.1 collective-permute-start.2
  2.6 0.4 shard_map.65
  3.0 4.7 %collective-permute-start.3 = (f32[8,2,16,512]{3,2,1,0:T(8,128)S(1)}, f32[8,2,16,512]{3,2,1,0:T(8,128)S(1)}, u32[]{:S(2)}, u32[]{:S(2)}) collective-permute-start(f32[8,2,16,512]{3,2,1,0:T(8,128)S(1)} %shard_map.65), channel_id=1, source_target_pairs={{1,2},{2,1},{3,4},{4,3},{5,6},{6,5},{9,10},{10,9},{11,12},{12,11},... | collective-permute-start | bytes 1572872 | tf_op jit(solution)/shard_map/ppermute | solution.py:36
  7.8 0.0 copy-done.2
  7.8 0.1 collective-permute-start
  7.8 3.6 %collective-permute-start.1 = (f32[512,128]{1,0:T(8,128)S(1)}, f32[512,128]{1,0:T(8,128)S(1)}, u32[]{:S(2)}, u32[]{:S(2)}) collective-permute-start(f32[512,128]{1,0:T(8,128)S(1)} %bitcast.7), channel_id=1, source_target_pairs={{1,2},{2,1},{3,4},{4,3},{5,6},{6,5},{9,10},{10,9},{11,12},{12,11},... | collective-permute-start | bytes 786440 | tf_op jit(solution)/shard_map/ppermute | solution.py:36
  11.4 0.0 copy-done.3
  11.4 0.0 copy-done.6
  11.4 1.4 %one_hots.1 = (bf16[288,1024]{1,0:T(8,128)(2,1)S(1)}, bf16[288,1024]{1,0:T(8,128)(2,1)S(1)}, bf16[288,1024]{1,0:T(8,128)(2,1)S(1)}, bf16[512,1024]{1,0:T(8,128)(...) custom-call(s32[1,1024]{1,0:T(1,128)S(1)} %bitcast.13, ...), custom_call_target="tpu_custom_call" | custom-call | tf_op jit(solution)/shard_map/one_hots/pallas_call | solution.py:253
  12.8 0.0 collective-permute-done.even_ref
  12.8 4.6 %collective-permute-done.1.odd_ref = f32[512,128]{1,0:T(8,128)S(1)} collective-permute-done((f32[512,128]{1,0:T(8,128)S(1)}, f32[512,128]{1,0:T(8,128)S(1)}, u32[]{:S(2)}, u32[]{:S(2)}) %collective-permute-start.1) | collective-permute-done | bytes 262176 | tf_op jit(solution)/shard_map/ppermute | solution.py:36
  17.4 0.0 copy-done.1
  17.4 3.7 %increment_at_obs.1 = (f32[4,1024]{1,0:T(4,128)S(1)}, f32[2,128,512]{2,1,0:T(8,128)S(1)}) custom-call(f32[512,128]{1,0:T(8,128)S(1)} %bitcast.8, f32[512,128]{1,0:T(8,128)S(1)} %collective-permute-done.even_ref, f32[512,128]{1,0:T(8,128)S(1)} %collective-permute-done.1.odd_ref, bf16[256,512]{1,0:T(8,128)(2,1)S(1)} %get-tuple-element.19.up_ref, ...), custom_call_target="tpu_custom_call" | custom-call | tf_op jit(solution)/shard_map/increment_at_obs/pallas_call | solution.py:341
  21.1 0.0 copy-start.4
  21.1 0.0 copy-start.5
  21.1 0.0 collective-permute-done.2.even_ref.refs_11_
  21.2 0.0 collective-permute-done.3.odd_ref.refs_12_
  21.2 0.5 %edge_at_obs.1.refs_0_ = f32[4,1024]{1,0:T(4,128)S(1)} custom-call(f32[4,1024]{1,0:T(4,128)S(1)} %get-tuple-element.27.q_ref, f32[2,128,512]{2,1,0:T(8,128)S(1)} %get-tuple-element.28.fine_ref, f32[8,2,16,512]{3,2,1,0:T(8,128)S(1)} %collective-permute-done.2.even_ref.refs_11_, f32[8,2,16,512]{3,2,1,0:T(8,128)S(1)} %collective-permute-done.3.odd_ref.refs_12_, ...), custom_call_target="tpu_custom_call" | custom-call | tf_op jit(solution)/shard_map/edge_at_obs/pallas_call | solution.py:383
  21.6 1.9 %collective-permute-start.4 = (f32[4,1024]{1,0:T(4,128)S(1)}, f32[4,1024]{1,0:T(4,128)S(1)}, u32[]{:S(2)}, u32[]{:S(2)}) collective-permute-start(f32[4,1024]{1,0:T(4,128)S(1)} %edge_at_obs.1.refs_0_), channel_id=1, source_target_pairs={{0,8},{8,0},{16,24},{24,16},{1,9},{9,1},{17,25},{25,17},{2,10},{10... | collective-permute-start | bytes 49160 | tf_op jit(solution)/shard_map/ppermute | solution.py:59
  23.5 1.2 %collective-permute-start.5 = (f32[4,1024]{1,0:T(4,128)S(1)}, f32[4,1024]{1,0:T(4,128)S(1)}, u32[]{:S(2)}, u32[]{:S(2)}) collective-permute-start(f32[4,1024]{1,0:T(4,128)S(1)} %edge_at_obs.1.refs_0_), channel_id=1, source_target_pairs={{0,16},{8,24},{16,0},{24,8},{1,17},{9,25},{17,1},{25,9},{2,18},{10... | collective-permute-start | bytes 49160 | tf_op jit(solution)/shard_map/ppermute | solution.py:59
  24.8 0.0 collective-permute-start.6
  24.8 0.1 down_weights.1.refs_7_
  24.9 0.0 collective-permute-done.4.refs_1_
  24.9 1.2 %collective-permute-done.5.refs_2_ = f32[4,1024]{1,0:T(4,128)S(1)} collective-permute-done((f32[4,1024]{1,0:T(4,128)S(1)}, f32[4,1024]{1,0:T(4,128)S(1)}, u32[]{:S(2)}, u32[]{:S(2)}) %collective-permute-start.5) | collective-permute-done | bytes 16416 | tf_op jit(solution)/shard_map/ppermute | solution.py:59
  26.1 2.1 %collective-permute-done.6.refs_3_ = f32[4,1024]{1,0:T(4,128)S(1)} collective-permute-done((f32[4,1024]{1,0:T(4,128)S(1)}, f32[4,1024]{1,0:T(4,128)S(1)}, u32[]{:S(2)}, u32[]{:S(2)}) %collective-permute-start.6) | collective-permute-done | bytes 16416 | tf_op jit(solution)/shard_map/ppermute | solution.py:59
  28.3 0.0 copy-done.4
  28.3 0.0 copy-done.5
  28.3 4.0 %adjoint_to_coarse.1 = (f32[6,128,128]{2,1,0:T(8,128)S(1)}, f32[3,128,128]{2,1,0:T(8,128)S(1)}) custom-call(f32[4,1024]{1,0:T(4,128)S(1)} %edge_at_obs.1.refs_0_, f32[4,1024]{1,0:T(4,128)S(1)} %collective-permute-done.4.refs_1_, f32[4,1024]{1,0:T(4,128)S(1)} %collective-permute-done.5.refs_2_, f32[4,1024]{1,0:T(4,128)S(1)} %collective-permute-done.6.refs_3_, ...), custom_call_target="tpu_custom_call" | custom-call | tf_op jit(solution)/shard_map/adjoint_to_coarse/pallas_call | solution.py:483
  32.3 0.4 finish_rows.1
  32.7 0.1 collective-permute-start.7
  32.8 4.7 %collective-permute-start.8 = (f32[3,128,128]{2,1,0:T(8,128)S(1)}, f32[3,128,128]{2,1,0:T(8,128)S(1)}, u32[]{:S(2)}, u32[]{:S(2)}) collective-permute-start(f32[3,128,128]{2,1,0:T(8,128)S(1)} %get-tuple-element.32), channel_id=1, source_target_pairs={{1,2},{2,1},{3,4},{4,3},{5,6},{6,5},{9,10},{10,9},{11,12},{12,11},... | collective-permute-start | bytes 589832 | tf_op jit(solution)/shard_map/ppermute | solution.py:36
  37.5 0.0 collective-permute-done.7.even_ref
  37.5 3.3 %collective-permute-done.8.odd_ref = f32[3,128,128]{2,1,0:T(8,128)S(1)} collective-permute-done((f32[3,128,128]{2,1,0:T(8,128)S(1)}, f32[3,128,128]{2,1,0:T(8,128)S(1)}, u32[]{:S(2)}, u32[]{:S(2)}) %collective-permute-start.8) | collective-permute-done | bytes 196640 | tf_op jit(solution)/shard_map/ppermute | solution.py:36
  40.8 0.7 %join_rows.1 = f32[512,128]{1,0:T(8,128)} custom-call(f32[4,128,128]{2,1,0:T(8,128)S(1)} %get-tuple-element.30.own_ref, f32[3,128,128]{2,1,0:T(8,128)S(1)} %collective-permute-done.7.even_ref, f32[3,128,128]{2,1,0:T(8,128)S(1)} %collective-permute-done.8.odd_ref), custom_call_target="tpu_custom_call" | custom-call | tf_op jit(solution)/shard_map/join_rows/pallas_call | solution.py:548
Async XLA Ops:
  0.0 2.2 %copy-start = (bf16[8,2,16,16,512]{4,3,2,1,0:T(8,128)(2,1)S(1)}, bf16[8,2,16,16,512]{4,3,2,1,0:T(8,128)(2,1)}, u32[]{:S(2)}) copy-start(bf16[8,2,16,16,512]{4,3,2,1,0:T(8,128)(2,1)} %refs_10_.1) | copy-start | bytes 12582916
  2.2 5.6 %copy-start.2 = (f32[8,16,4,128]{3,2,1,0:T(4,128)S(1)}, f32[8,16,4,128]{3,2,1,0:T(4,128)}, u32[]{:S(2)}) copy-start(f32[8,16,4,128]{3,2,1,0:T(4,128)} %param.6) | copy-start | bytes 786436
  2.2 9.2 %copy-start.3 = (s32[1024]{0:T(1024)S(1)}, s32[1024]{0:T(1024)}, u32[]{:S(2)}) copy-start(s32[1024]{0:T(1024)} %param.9) | copy-start | bytes 12292
  2.2 9.2 %copy-start.6 = (s32[1024]{0:T(1024)S(1)}, s32[1024]{0:T(1024)}, u32[]{:S(2)}) copy-start(s32[1024]{0:T(1024)} %param.8) | copy-start | bytes 12292
  2.2 15.2 %copy-start.1 = (bf16[8,2,16,16,512]{4,3,2,1,0:T(8,128)(2,1)S(1)}, bf16[8,2,16,16,512]{4,3,2,1,0:T(8,128)(2,1)}, u32[]{:S(2)}) copy-start(bf16[8,2,16,16,512]{4,3,2,1,0:T(8,128)(2,1)} %refs_10_.1) | copy-start | bytes 12582916
  2.6 18.6 %collective-permute-start.2 = (f32[8,2,16,512]{3,2,1,0:T(8,128)S(1)}, f32[8,2,16,512]{3,2,1,0:T(8,128)S(1)}, u32[]{:S(2)}, u32[]{:S(2)}) collective-permute-start(f32[8,2,16,512]{3,2,1,0:T(8,128)S(1)} %shard_map.64), channel_id=1, source_target_pairs={{0,1},{1,0},{2,3},{3,2},{4,5},{5,4},{6,7},{7,6},{8,9},{9,8},{10,11... | collective-permute-start | bytes 1572872 | tf_op jit(solution)/shard_map/ppermute | solution.py:32
  3.0 18.1 %collective-permute-start.3 = (f32[8,2,16,512]{3,2,1,0:T(8,128)S(1)}, f32[8,2,16,512]{3,2,1,0:T(8,128)S(1)}, u32[]{:S(2)}, u32[]{:S(2)}) collective-permute-start(f32[8,2,16,512]{3,2,1,0:T(8,128)S(1)} %shard_map.65), channel_id=1, source_target_pairs={{1,2},{2,1},{3,4},{4,3},{5,6},{6,5},{9,10},{10,9},{11,12},{12,11},... | collective-permute-start | bytes 1572872 | tf_op jit(solution)/shard_map/ppermute | solution.py:36
  7.8 5.1 %collective-permute-start = (f32[512,128]{1,0:T(8,128)S(1)}, f32[512,128]{1,0:T(8,128)S(1)}, u32[]{:S(2)}, u32[]{:S(2)}) collective-permute-start(f32[512,128]{1,0:T(8,128)S(1)} %bitcast.6), channel_id=1, source_target_pairs={{0,1},{1,0},{2,3},{3,2},{4,5},{5,4},{6,7},{7,6},{8,9},{9,8},{10,11... | collective-permute-start | bytes 786440 | tf_op jit(solution)/shard_map/ppermute | solution.py:32
  7.8 9.6 %collective-permute-start.1 = (f32[512,128]{1,0:T(8,128)S(1)}, f32[512,128]{1,0:T(8,128)S(1)}, u32[]{:S(2)}, u32[]{:S(2)}) collective-permute-start(f32[512,128]{1,0:T(8,128)S(1)} %bitcast.7), channel_id=1, source_target_pairs={{1,2},{2,1},{3,4},{4,3},{5,6},{6,5},{9,10},{10,9},{11,12},{12,11},... | collective-permute-start | bytes 786440 | tf_op jit(solution)/shard_map/ppermute | solution.py:36
  21.1 7.2 %copy-start.4 = (f32[1024]{0:T(1024)S(1)}, f32[1024]{0:T(1024)}, u32[]{:S(2)}) copy-start(f32[1024]{0:T(1024)} %param.10) | copy-start | bytes 12292
  21.1 7.1 %copy-start.5 = (f32[1024]{0:T(1024)S(1)}, f32[1024]{0:T(1024)}, u32[]{:S(2)}) copy-start(f32[1024]{0:T(1024)} %param.11) | copy-start | bytes 12292
  21.6 3.3 %collective-permute-start.4 = (f32[4,1024]{1,0:T(4,128)S(1)}, f32[4,1024]{1,0:T(4,128)S(1)}, u32[]{:S(2)}, u32[]{:S(2)}) collective-permute-start(f32[4,1024]{1,0:T(4,128)S(1)} %edge_at_obs.1.refs_0_), channel_id=1, source_target_pairs={{0,8},{8,0},{16,24},{24,16},{1,9},{9,1},{17,25},{25,17},{2,10},{10... | collective-permute-start | bytes 49160 | tf_op jit(solution)/shard_map/ppermute | solution.py:59
  23.5 2.6 %collective-permute-start.5 = (f32[4,1024]{1,0:T(4,128)S(1)}, f32[4,1024]{1,0:T(4,128)S(1)}, u32[]{:S(2)}, u32[]{:S(2)}) collective-permute-start(f32[4,1024]{1,0:T(4,128)S(1)} %edge_at_obs.1.refs_0_), channel_id=1, source_target_pairs={{0,16},{8,24},{16,0},{24,8},{1,17},{9,25},{17,1},{25,9},{2,18},{10... | collective-permute-start | bytes 49160 | tf_op jit(solution)/shard_map/ppermute | solution.py:59
  24.8 3.5 %collective-permute-start.6 = (f32[4,1024]{1,0:T(4,128)S(1)}, f32[4,1024]{1,0:T(4,128)S(1)}, u32[]{:S(2)}, u32[]{:S(2)}) collective-permute-start(f32[4,1024]{1,0:T(4,128)S(1)} %edge_at_obs.1.refs_0_), channel_id=1, source_target_pairs={{0,24},{8,16},{16,8},{24,0},{1,25},{9,17},{17,9},{25,1},{2,26},{10... | collective-permute-start | bytes 49160 | tf_op jit(solution)/shard_map/ppermute | solution.py:59
  32.7 4.8 %collective-permute-start.7 = (f32[3,128,128]{2,1,0:T(8,128)S(1)}, f32[3,128,128]{2,1,0:T(8,128)S(1)}, u32[]{:S(2)}, u32[]{:S(2)}) collective-permute-start(f32[3,128,128]{2,1,0:T(8,128)S(1)} %get-tuple-element.31), channel_id=1, source_target_pairs={{0,1},{1,0},{2,3},{3,2},{4,5},{5,4},{6,7},{7,6},{8,9},{9,8},{10,11... | collective-permute-start | bytes 589832 | tf_op jit(solution)/shard_map/ppermute | solution.py:32
  32.8 8.1 %collective-permute-start.8 = (f32[3,128,128]{2,1,0:T(8,128)S(1)}, f32[3,128,128]{2,1,0:T(8,128)S(1)}, u32[]{:S(2)}, u32[]{:S(2)}) collective-permute-start(f32[3,128,128]{2,1,0:T(8,128)S(1)} %get-tuple-element.32), channel_id=1, source_target_pairs={{1,2},{2,1},{3,4},{4,3},{5,6},{6,5},{9,10},{10,9},{11,12},{12,11},... | collective-permute-start | bytes 589832 | tf_op jit(solution)/shard_map/ppermute | solution.py:36

commit v7 on v6

--- a/solution.py
+++ b/solution.py
@@ -352,40 +352,36 @@
     )(own, got_even, got_odd, up, twice, once, pert, *hot)
 
 
-def edge_kernel(members, levels, q_ref, fine_ref, even_ref, odd_ref, ru_ref, rv_ref, c0_ref, out_ref):
-    side = sides()
-    lines, _ = ru_ref.shape
+def edge_kernel(odd, members, levels, q_ref, fine_ref, halo_ref, ru_ref, rv_ref, c0_ref, out_ref):
+    near = sides()[odd]
+    lines = ru_ref.shape[0]
     inner = lines - 2 * levels
     table = []
     for part in range(2):
-        for near, halo_ref in zip(side, (even_ref, odd_ref)):
-            total = None
-            for m in range(members):
-                term = fine_ref[near, pl.ds(m * levels, levels), :] * halo_ref[m, part]
-                total = term if total is None else total + term
-            table.append(total)
+        total = None
+        for m in range(members):
+            term = fine_ref[near, pl.ds(m * levels, levels), :] * halo_ref[m, part]
+            total = term if total is None else total + term
+        table.append(total)
     high, lower = split(jnp.concatenate(table, axis=0))
     z = dot_nn(jnp.concatenate([high, lower], axis=0), c0_ref[...])
-    z = z[: 4 * levels] + z[4 * levels :]
-    for n, ref in ((0, ru_ref), (2, rv_ref)):
-        total = q_ref[pl.ds(2 - n // 2, 1), :]
-        for k in range(2):
-            here = pl.ds(pl.multiple_of(inner + side[k] * levels, levels), levels)
-            part = z[(n + k) * levels : (n + k + 1) * levels]
-            total = total + jnp.sum(ref[here, :].astype(F32) * part, axis=0, keepdims=True)
-        out_ref[pl.ds(2 - n // 2, 1), :] = total
+    z = z[: 2 * levels] + z[2 * levels :]
+    here = pl.ds(pl.multiple_of(inner + near * levels, levels), levels)
+    in_u = jnp.sum(ru_ref[here, :].astype(F32) * z[:levels], axis=0, keepdims=True)
+    in_v = jnp.sum(rv_ref[here, :].astype(F32) * z[levels:], axis=0, keepdims=True)
     out_ref[pl.ds(0, 1), :] = q_ref[pl.ds(0, 1), :]
+    out_ref[pl.ds(1, 1), :] = q_ref[pl.ds(1, 1), :] + in_v
+    out_ref[pl.ds(2, 1), :] = q_ref[pl.ds(2, 1), :] + in_u
     out_ref[pl.ds(3, 1), :] = q_ref[pl.ds(3, 1), :]
 
 
-def edge(q, fine, halo_even, halo_odd, hot, members, levels):
+def edge(q, fine, halo, odd, hot, members, levels):
     _, ru, rv, c0, _ = hot
     return pl.pallas_call(
-        functools.partial(edge_kernel, members, levels),
+        functools.partial(edge_kernel, odd, members, levels),
         out_shape=jax.ShapeDtypeStruct(q.shape, F32),
-        compiler_params=params(16),
-        name="edge_at_obs",
-    )(q, fine, halo_even, halo_odd, ru, rv, c0)
+        compiler_params=pltpu.CompilerParams(vmem_limit_bytes=16 << 20),
+    )(q, fine, halo, ru, rv, c0)
 
 
 def smooth_outside(held, before, twice_ref, once_ref):
@@ -488,7 +484,7 @@
             pltpu.VMEM((levels * rows + 2 * levels, columns), F32),
             pltpu.VMEM((pairs * rows, coarse_columns), F32),
         ],
-        compiler_params=params(28),
+        compiler_params=pltpu.CompilerParams(vmem_limit_bytes=28 << 20),
         name="adjoint_to_coarse",
     )(*q_terms, kind, value, weight, *tables_y, pert, halo_even, halo_odd, *hot)
 
@@ -574,7 +570,8 @@
     halo_even = swap_even(packed)
     hot, along_y = tables(cell, kind, levels, rows, columns, coarse_columns)
     q, edge_fine = forward(flat, flat_even, flat_odd, along_y, perturbation, hot, scale)
-    q = edge(q, edge_fine, halo_even, halo_odd, hot, members, levels)
+    q = edge(q, edge_fine, halo_even, 0, hot, members, levels)
+    q = edge(q, edge_fine, halo_odd, 1, hot, members, levels)
     terms = others(q, "mem")
     held, send_b = backward(
         terms, kind, value, weight, (down, *along_y[1:]), perturbation, halo_even, halo_odd, hot, scale,

time: 41.7 us -> 42 us (level)
  transfers between devices with their start and end apart: 9 -> 9, of which waited for: 4 -> 4; matrix products, arithmetic and copies ran while one was open for 0% -> 0% of each run, Pallas kernels for 13% -> 14%
where the time goes in v7:
time: 42 us; the launch traced here: 41.8 us
  starting transfers between devices  16.4 us (39%)
  Pallas kernels  11.8 us (28%)
  waiting for transfers between devices  11.3 us (27%)
  local copies, waits for them, and re-layouts  2.21 us (5%)
    ppermute x3, starting transfers between devices, swap_odd(): return lax.ppermute(value, 'reg', swap_pairs(lax.axis_size('reg'), True))  13.2 us
    ppermute x3, waiting for transfers between devices, swap_odd(): return lax.ppermute(value, 'reg', swap_pairs(lax.axis_size('reg'), True))  7.92 us
    pallas_call x1, Pallas kernels, backward(): pl.pallas_call(functools.partial(backward_kernel, scale, 4 if levels % 4...  4.03 us
    pallas_call x1, Pallas kernels, forward(): pl.pallas_call(functools.partial(forward_kernel, scale, chunk), out_shape...  3.69 us
    ppermute x3, waiting for transfers between devices, others(): got.append(lax.ppermute(value, axis, pairs))  3.38 us
    ppermute x3, starting transfers between devices, others(): got.append(lax.ppermute(value, axis, pairs))  2.93 us
    unnamed x14, local copies, waits for them, and re-layouts  2.21 us
    pallas_call x1, Pallas kernels, tables(): pl.pallas_call(functools.partial(tables_kernel, levels, rows, columns), o...  1.36 us
  transfers between devices with their start and end apart: 9, of which 4 were waited for; matrix products, arithmetic and copies ran while one was open for 0% of the time, Pallas kernels for 14%

profile of v7, /device:TPU:1, one launch (start us, length us, event | category | flops | bytes accessed | tf_op | source)
XLA Modules:
  0.0 41.8 jit_solution(16202990315452815098)
XLA Ops:
  0.0 0.0 copy-start
  0.0 2.2 %copy-done = bf16[8,2,16,16,512]{4,3,2,1,0:T(8,128)(2,1)S(1)} copy-done((bf16[8,2,16,16,512]{4,3,2,1,0:T(8,128)(2,1)S(1)}, bf16[8,2,16,16,512]{4,3,2,1,0:T(8,128)(2,1)}, u32[]{:S(2)}) %copy-start) | copy-done | bytes 4194328
  2.2 0.0 copy-start.2
  2.2 0.0 copy-start.3
  2.2 0.0 copy-start.6
  2.2 0.0 copy-start.1
  2.2 0.4 shard_map.64
  2.6 0.1 collective-permute-start.2
  2.6 0.4 shard_map.66
  3.0 4.7 %collective-permute-start.3 = (f32[8,2,16,512]{3,2,1,0:T(8,128)S(1)}, f32[8,2,16,512]{3,2,1,0:T(8,128)S(1)}, u32[]{:S(2)}, u32[]{:S(2)}) collective-permute-start(f32[8,2,16,512]{3,2,1,0:T(8,128)S(1)} %shard_map.66), channel_id=1, source_target_pairs={{1,2},{2,1},{3,4},{4,3},{5,6},{6,5},{9,10},{10,9},{11,12},{12,11},... | collective-permute-start | bytes 1572872 | tf_op jit(solution)/shard_map/ppermute | solution.py:36
  7.8 0.0 copy-done.2
  7.8 0.1 collective-permute-start
  7.8 3.6 %collective-permute-start.1 = (f32[512,128]{1,0:T(8,128)S(1)}, f32[512,128]{1,0:T(8,128)S(1)}, u32[]{:S(2)}, u32[]{:S(2)}) collective-permute-start(f32[512,128]{1,0:T(8,128)S(1)} %bitcast.7), channel_id=1, source_target_pairs={{1,2},{2,1},{3,4},{4,3},{5,6},{6,5},{9,10},{10,9},{11,12},{12,11},... | collective-permute-start | bytes 786440 | tf_op jit(solution)/shard_map/ppermute | solution.py:36
  11.4 0.0 copy-done.3
  11.4 0.0 copy-done.6
  11.4 1.4 %one_hots.1 = (bf16[288,1024]{1,0:T(8,128)(2,1)S(1)}, bf16[288,1024]{1,0:T(8,128)(2,1)S(1)}, bf16[288,1024]{1,0:T(8,128)(2,1)S(1)}, bf16[512,1024]{1,0:T(8,128)(...) custom-call(s32[1,1024]{1,0:T(1,128)S(1)} %bitcast.13, ...), custom_call_target="tpu_custom_call" | custom-call | tf_op jit(solution)/shard_map/one_hots/pallas_call | solution.py:253
  12.8 0.0 collective-permute-done.even_ref
  12.8 4.6 %collective-permute-done.1.odd_ref = f32[512,128]{1,0:T(8,128)S(1)} collective-permute-done((f32[512,128]{1,0:T(8,128)S(1)}, f32[512,128]{1,0:T(8,128)S(1)}, u32[]{:S(2)}, u32[]{:S(2)}) %collective-permute-start.1) | collective-permute-done | bytes 262176 | tf_op jit(solution)/shard_map/ppermute | solution.py:36
  17.4 0.0 copy-done.1
  17.4 3.7 %increment_at_obs.1 = (f32[4,1024]{1,0:T(4,128)S(1)}, f32[2,128,512]{2,1,0:T(8,128)S(1)}) custom-call(f32[512,128]{1,0:T(8,128)S(1)} %bitcast.8, f32[512,128]{1,0:T(8,128)S(1)} %collective-permute-done.even_ref, f32[512,128]{1,0:T(8,128)S(1)} %collective-permute-done.1.odd_ref, bf16[256,512]{1,0:T(8,128)(2,1)S(1)} %get-tuple-element.19.up_ref, ...), custom_call_target="tpu_custom_call" | custom-call | tf_op jit(solution)/shard_map/increment_at_obs/pallas_call | solution.py:341
  21.1 0.0 collective-permute-done.2.halo_ref.refs_11_
  21.1 0.4 shard_map.65.q_ref
  21.5 0.0 copy-start.4
  21.5 0.0 copy-start.5
  21.5 0.0 collective-permute-done.3.halo_ref.refs_12_
  21.5 0.4 shard_map.67.refs_0_
  21.9 1.7 %collective-permute-start.4 = (f32[4,1024]{1,0:T(4,128)S(1)}, f32[4,1024]{1,0:T(4,128)S(1)}, u32[]{:S(2)}, u32[]{:S(2)}) collective-permute-start(f32[4,1024]{1,0:T(4,128)S(1)} %shard_map.67.refs_0_), channel_id=1, source_target_pairs={{0,8},{8,0},{16,24},{24,16},{1,9},{9,1},{17,25},{25,17},{2,10},{10... | collective-permute-start | bytes 49160 | tf_op jit(solution)/shard_map/ppermute | solution.py:59
  23.6 1.2 %collective-permute-start.5 = (f32[4,1024]{1,0:T(4,128)S(1)}, f32[4,1024]{1,0:T(4,128)S(1)}, u32[]{:S(2)}, u32[]{:S(2)}) collective-permute-start(f32[4,1024]{1,0:T(4,128)S(1)} %shard_map.67.refs_0_), channel_id=1, source_target_pairs={{0,16},{8,24},{16,0},{24,8},{1,17},{9,25},{17,1},{25,9},{2,18},{10... | collective-permute-start | bytes 49160 | tf_op jit(solution)/shard_map/ppermute | solution.py:59
  24.8 0.0 collective-permute-start.6
  24.8 0.1 down_weights.1.refs_7_
  24.9 0.0 collective-permute-done.4.refs_1_
  24.9 1.2 %collective-permute-done.5.refs_2_ = f32[4,1024]{1,0:T(4,128)S(1)} collective-permute-done((f32[4,1024]{1,0:T(4,128)S(1)}, f32[4,1024]{1,0:T(4,128)S(1)}, u32[]{:S(2)}, u32[]{:S(2)}) %collective-permute-start.5) | collective-permute-done | bytes 16416 | tf_op jit(solution)/shard_map/ppermute | solution.py:59
  26.1 2.1 %collective-permute-done.6.refs_3_ = f32[4,1024]{1,0:T(4,128)S(1)} collective-permute-done((f32[4,1024]{1,0:T(4,128)S(1)}, f32[4,1024]{1,0:T(4,128)S(1)}, u32[]{:S(2)}, u32[]{:S(2)}) %collective-permute-start.6) | collective-permute-done | bytes 16416 | tf_op jit(solution)/shard_map/ppermute | solution.py:59
  28.3 0.0 copy-done.4
  28.3 0.0 copy-done.5
  28.3 4.0 %adjoint_to_coarse.1 = (f32[6,128,128]{2,1,0:T(8,128)S(1)}, f32[3,128,128]{2,1,0:T(8,128)S(1)}) custom-call(f32[4,1024]{1,0:T(4,128)S(1)} %shard_map.67.refs_0_, f32[4,1024]{1,0:T(4,128)S(1)} %collective-permute-done.4.refs_1_, f32[4,1024]{1,0:T(4,128)S(1)} %collective-permute-done.5.refs_2_, f32[4,1024]{1,0:T(4,128)S(1)} %collective-permute-done.6.refs_3_, ...), custom_call_target="tpu_custom_call" | custom-call | tf_op jit(solution)/shard_map/adjoint_to_coarse/pallas_call | solution.py:479
  32.3 0.4 finish_rows.1
  32.7 0.1 collective-permute-start.7
  32.8 4.9 %collective-permute-start.8 = (f32[3,128,128]{2,1,0:T(8,128)S(1)}, f32[3,128,128]{2,1,0:T(8,128)S(1)}, u32[]{:S(2)}, u32[]{:S(2)}) collective-permute-start(f32[3,128,128]{2,1,0:T(8,128)S(1)} %get-tuple-element.32), channel_id=1, source_target_pairs={{1,2},{2,1},{3,4},{4,3},{5,6},{6,5},{9,10},{10,9},{11,12},{12,11},... | collective-permute-start | bytes 589832 | tf_op jit(solution)/shard_map/ppermute | solution.py:36
  37.7 0.0 collective-permute-done.7.even_ref
  37.7 3.3 %collective-permute-done.8.odd_ref = f32[3,128,128]{2,1,0:T(8,128)S(1)} collective-permute-done((f32[3,128,128]{2,1,0:T(8,128)S(1)}, f32[3,128,128]{2,1,0:T(8,128)S(1)}, u32[]{:S(2)}, u32[]{:S(2)}) %collective-permute-start.8) | collective-permute-done | bytes 196640 | tf_op jit(solution)/shard_map/ppermute | solution.py:36
  41.1 0.7 %join_rows.1 = f32[512,128]{1,0:T(8,128)} custom-call(f32[4,128,128]{2,1,0:T(8,128)S(1)} %get-tuple-element.30.own_ref, f32[3,128,128]{2,1,0:T(8,128)S(1)} %collective-permute-done.7.even_ref, f32[3,128,128]{2,1,0:T(8,128)S(1)} %collective-permute-done.8.odd_ref), custom_call_target="tpu_custom_call" | custom-call | tf_op jit(solution)/shard_map/join_rows/pallas_call | solution.py:544
Async XLA Ops:
  0.0 2.2 %copy-start = (bf16[8,2,16,16,512]{4,3,2,1,0:T(8,128)(2,1)S(1)}, bf16[8,2,16,16,512]{4,3,2,1,0:T(8,128)(2,1)}, u32[]{:S(2)}) copy-start(bf16[8,2,16,16,512]{4,3,2,1,0:T(8,128)(2,1)} %refs_10_.1) | copy-start | bytes 12582916
  2.2 5.6 %copy-start.2 = (f32[8,16,4,128]{3,2,1,0:T(4,128)S(1)}, f32[8,16,4,128]{3,2,1,0:T(4,128)}, u32[]{:S(2)}) copy-start(f32[8,16,4,128]{3,2,1,0:T(4,128)} %param.6) | copy-start | bytes 786436
  2.2 9.2 %copy-start.3 = (s32[1024]{0:T(1024)S(1)}, s32[1024]{0:T(1024)}, u32[]{:S(2)}) copy-start(s32[1024]{0:T(1024)} %param.9) | copy-start | bytes 12292
  2.2 9.2 %copy-start.6 = (s32[1024]{0:T(1024)S(1)}, s32[1024]{0:T(1024)}, u32[]{:S(2)}) copy-start(s32[1024]{0:T(1024)} %param.8) | copy-start | bytes 12292
  2.2 15.2 %copy-start.1 = (bf16[8,2,16,16,512]{4,3,2,1,0:T(8,128)(2,1)S(1)}, bf16[8,2,16,16,512]{4,3,2,1,0:T(8,128)(2,1)}, u32[]{:S(2)}) copy-start(bf16[8,2,16,16,512]{4,3,2,1,0:T(8,128)(2,1)} %refs_10_.1) | copy-start | bytes 12582916
  2.6 18.5 %collective-permute-start.2 = (f32[8,2,16,512]{3,2,1,0:T(8,128)S(1)}, f32[8,2,16,512]{3,2,1,0:T(8,128)S(1)}, u32[]{:S(2)}, u32[]{:S(2)}) collective-permute-start(f32[8,2,16,512]{3,2,1,0:T(8,128)S(1)} %shard_map.64), channel_id=1, source_target_pairs={{0,1},{1,0},{2,3},{3,2},{4,5},{5,4},{6,7},{7,6},{8,9},{9,8},{10,11... | collective-permute-start | bytes 1572872 | tf_op jit(solution)/shard_map/ppermute | solution.py:32
  3.0 18.5 %collective-permute-start.3 = (f32[8,2,16,512]{3,2,1,0:T(8,128)S(1)}, f32[8,2,16,512]{3,2,1,0:T(8,128)S(1)}, u32[]{:S(2)}, u32[]{:S(2)}) collective-permute-start(f32[8,2,16,512]{3,2,1,0:T(8,128)S(1)} %shard_map.66), channel_id=1, source_target_pairs={{1,2},{2,1},{3,4},{4,3},{5,6},{6,5},{9,10},{10,9},{11,12},{12,11},... | collective-permute-start | bytes 1572872 | tf_op jit(solution)/shard_map/ppermute | solution.py:36
  7.8 5.1 %collective-permute-start = (f32[512,128]{1,0:T(8,128)S(1)}, f32[512,128]{1,0:T(8,128)S(1)}, u32[]{:S(2)}, u32[]{:S(2)}) collective-permute-start(f32[512,128]{1,0:T(8,128)S(1)} %bitcast.6), channel_id=1, source_target_pairs={{0,1},{1,0},{2,3},{3,2},{4,5},{5,4},{6,7},{7,6},{8,9},{9,8},{10,11... | collective-permute-start | bytes 786440 | tf_op jit(solution)/shard_map/ppermute | solution.py:32
  7.8 9.6 %collective-permute-start.1 = (f32[512,128]{1,0:T(8,128)S(1)}, f32[512,128]{1,0:T(8,128)S(1)}, u32[]{:S(2)}, u32[]{:S(2)}) collective-permute-start(f32[512,128]{1,0:T(8,128)S(1)} %bitcast.7), channel_id=1, source_target_pairs={{1,2},{2,1},{3,4},{4,3},{5,6},{6,5},{9,10},{10,9},{11,12},{12,11},... | collective-permute-start | bytes 786440 | tf_op jit(solution)/shard_map/ppermute | solution.py:36
  21.5 6.8 %copy-start.4 = (f32[1024]{0:T(1024)S(1)}, f32[1024]{0:T(1024)}, u32[]{:S(2)}) copy-start(f32[1024]{0:T(1024)} %param.10) | copy-start | bytes 12292
  21.5 6.8 %copy-start.5 = (f32[1024]{0:T(1024)S(1)}, f32[1024]{0:T(1024)}, u32[]{:S(2)}) copy-start(f32[1024]{0:T(1024)} %param.11) | copy-start | bytes 12292
  21.9 3.0 %collective-permute-start.4 = (f32[4,1024]{1,0:T(4,128)S(1)}, f32[4,1024]{1,0:T(4,128)S(1)}, u32[]{:S(2)}, u32[]{:S(2)}) collective-permute-start(f32[4,1024]{1,0:T(4,128)S(1)} %shard_map.67.refs_0_), channel_id=1, source_target_pairs={{0,8},{8,0},{16,24},{24,16},{1,9},{9,1},{17,25},{25,17},{2,10},{10... | collective-permute-start | bytes 49160 | tf_op jit(solution)/shard_map/ppermute | solution.py:59
  23.6 2.6 %collective-permute-start.5 = (f32[4,1024]{1,0:T(4,128)S(1)}, f32[4,1024]{1,0:T(4,128)S(1)}, u32[]{:S(2)}, u32[]{:S(2)}) collective-permute-start(f32[4,1024]{1,0:T(4,128)S(1)} %shard_map.67.refs_0_), channel_id=1, source_target_pairs={{0,16},{8,24},{16,0},{24,8},{1,17},{9,25},{17,1},{25,9},{2,18},{10... | collective-permute-start | bytes 49160 | tf_op jit(solution)/shard_map/ppermute | solution.py:59
  24.8 3.5 %collective-permute-start.6 = (f32[4,1024]{1,0:T(4,128)S(1)}, f32[4,1024]{1,0:T(4,128)S(1)}, u32[]{:S(2)}, u32[]{:S(2)}) collective-permute-start(f32[4,1024]{1,0:T(4,128)S(1)} %shard_map.67.refs_0_), channel_id=1, source_target_pairs={{0,24},{8,16},{16,8},{24,0},{1,25},{9,17},{17,9},{25,1},{2,26},{10... | collective-permute-start | bytes 49160 | tf_op jit(solution)/shard_map/ppermute | solution.py:59
  32.7 5.0 %collective-permute-start.7 = (f32[3,128,128]{2,1,0:T(8,128)S(1)}, f32[3,128,128]{2,1,0:T(8,128)S(1)}, u32[]{:S(2)}, u32[]{:S(2)}) collective-permute-start(f32[3,128,128]{2,1,0:T(8,128)S(1)} %get-tuple-element.31), channel_id=1, source_target_pairs={{0,1},{1,0},{2,3},{3,2},{4,5},{5,4},{6,7},{7,6},{8,9},{9,8},{10,11... | collective-permute-start | bytes 589832 | tf_op jit(solution)/shard_map/ppermute | solution.py:32
  32.8 8.3 %collective-permute-start.8 = (f32[3,128,128]{2,1,0:T(8,128)S(1)}, f32[3,128,128]{2,1,0:T(8,128)S(1)}, u32[]{:S(2)}, u32[]{:S(2)}) collective-permute-start(f32[3,128,128]{2,1,0:T(8,128)S(1)} %get-tuple-element.32), channel_id=1, source_target_pairs={{1,2},{2,1},{3,4},{4,3},{5,6},{6,5},{9,10},{10,9},{11,12},{12,11},... | collective-permute-start | bytes 589832 | tf_op jit(solution)/shard_map/ppermute | solution.py:36
